TPU v7x, 32 devices: a whole 2x2x4 slice. The times are simulated.
32 devices in a mesh: gx: 8 (over z, x), gy: 4 (over y, core).
Axes of the slice: x: 2, y: 2, z: 4, core: 2. Of those that a mesh axis runs over, the one named last changes fastest.
Arguments:
- probes: bfloat16 [48, 4, 128, 1024], P(None, None, 'gx', 'gy'), may hold values from -6 to 6
- classes: int32 [4, 128, 1024], P(None, 'gx', 'gy'), may hold values from 0 to 7
- class_table: float32 [8], replicated, may hold values from 0.3 to 3
- weights: float32 [4, 128, 1024], P(None, 'gx', 'gy'), may hold values from 5 to 500
- prior_block: float32 [1024, 256], P('gy'), may hold values from -0.1875 to 0.1875
- prior_left: float32 [8, 16, 1024], P(None, None, 'gy'), may hold values from -1.5 to 1.5
- prior_right: float32 [8, 16, 1024], P(None, None, 'gy'), may hold values from -6 to 6
- block_ranks: int32 [8], replicated, may hold values from 4 to 16
Outputs:
- basis: float32 [48, 4, 128, 1024], P(None, None, 'gx', 'gy')
- projected: float32 [48, 48], replicated
All inputs are finite; a program needn't handle non-finite values.
Results may differ from a plain program's by a relative error of at most 0.0018.
Values may be sent and summed in bfloat16 or wider, within the bound.
No kernel may reach another device: no remote copies, remote signals or barrier semaphores. Data moves between devices by JAX's collectives and lax.ppermute only.
A program may use at most 64 MiB of HBM per device.

v0:
```python
import functools
import jax
import jax.numpy as jnp
from jax import lax
from jax.experimental import pallas as pl
from jax.experimental.pallas import tpu as pltpu
from jax.sharding import PartitionSpec as P

HIGH = lax.Precision.HIGHEST
F32 = jnp.float32
BF16 = jnp.bfloat16
LANES = 128
SUB = 8
GROUP = 32
REACH = 3
AUX = 16
VMEM = pl.BlockSpec(memory_space=pltpu.VMEM)
ANY = pl.BlockSpec(memory_space=pl.ANY)


def lanes_of(shape):
    return lax.broadcasted_iota(jnp.int32, shape, len(shape) - 1)


def halves(v):
    hi = v.astype(BF16)
    return hi, (v - hi.astype(F32)).astype(BF16)


def nt(a, b, precision=None):
    return lax.dot_general(a, b, (((1,), (1,)), ((), ())), precision=precision, preferred_element_type=F32)


def pack_kernel(K, NZ, X, p_ref, cls_ref, w_ref, pt_ref, ylo_ref, yhi_ref, xlo_ref, xhi_ref, edge, aux):
    rows, ext = NZ * X, X + 4
    for k in range(K):
        v = p_ref[k * rows : (k + 1) * rows, :].astype(F32)
        for z in range(NZ):
            for h in range(2):
                pt_ref[h, pl.ds((z * ext + 2) * K + k, X, stride=K), :] = v[z * X : (z + 1) * X, h * LANES : (h + 1) * LANES]
    lane = lanes_of((SUB, LANES))
    for kt in range(K // SUB):
        out = [jnp.zeros((SUB, LANES), F32) for _ in range(4)]
        for z in range(NZ):
            for x in range(X):
                row = (z * ext + 2 + x) * K + kt * SUB
                to = z * GROUP + x + REACH
                here = lane == to
                left, right = pt_ref[0, row : row + SUB, :], pt_ref[1, row : row + SUB, :]
                for i, (tile, col) in enumerate(((left, 0), (left, 1), (right, LANES - 1), (right, LANES - 2))):
                    out[i] = jnp.where(here, pltpu.roll(tile, (to - col) % LANES, 1), out[i])
        edge[0, kt * SUB : (kt + 1) * SUB, :] = out[0]
        edge[1, kt * SUB : (kt + 1) * SUB, :] = out[1]
        edge[2, kt * SUB : (kt + 1) * SUB, :] = out[2]
        edge[3, kt * SUB : (kt + 1) * SUB, :] = out[3]
    for side, ref in enumerate((ylo_ref, yhi_ref)):
        for d in range(2):
            ref[d * K : (d + 1) * K, :] = edge[2 * side + d, :K, :].astype(BF16)
    wide = lanes_of((LANES, LANES))
    turned = []
    for source in (cls_ref, w_ref):
        edge[0] = jnp.zeros((LANES, LANES), F32)
        for z in range(NZ):
            v = source[z * X : (z + 1) * X, :].astype(F32)
            if source is cls_ref:
                v = v + 1.0
            edge[0, z * GROUP + REACH : z * GROUP + REACH + X, :] = jnp.where(lanes_of((X, LANES)) < 64, v[:, :LANES], v[:, LANES:])
        turned.append(edge[0].T)
    for side, ref in enumerate((ylo_ref, yhi_ref)):
        at = (0, 1, 2) if side == 0 else (LANES - 1, LANES - 2, LANES - 3)
        aux[...] = jnp.zeros_like(aux)
        for d in range(3):
            aux[d : d + 1, :LANES] = turned[0][at[d] : at[d] + 1, :]
        w_hi, w_lo = halves(turned[1][at[0] : at[0] + 1, :])
        aux[3:4, :LANES] = w_hi.astype(F32)
        aux[4:5, :LANES] = w_lo.astype(F32)
        ref[2 * K : 2 * K + AUX, :] = aux[:AUX, :LANES].astype(BF16)
    for side, ref in enumerate((xlo_ref, xhi_ref)):
        first = 0 if side == 0 else X - 2
        for z in range(NZ):
            for i in range(2):
                row = (z * ext + 2 + first + i) * K
                for h in range(2):
                    ref[(z * 2 + i) * K : (z * 2 + i + 1) * K, h * LANES : (h + 1) * LANES] = pt_ref[h, row : row + K, :].astype(BF16)
        aux[...] = jnp.zeros_like(aux)
        for z in range(NZ):
            c0 = z * X + (0 if side == 0 else X - 3)
            aux[z * SUB : z * SUB + 3, :] = cls_ref[c0 : c0 + 3, :].astype(F32) + 1.0
            w0 = z * X + (0 if side == 0 else X - 1)
            w_hi, w_lo = halves(w_ref[w0 : w0 + 1, :])
            aux[z * SUB + 3 : z * SUB + 4, :] = w_hi.astype(F32)
            aux[z * SUB + 4 : z * SUB + 5, :] = w_lo.astype(F32)
        ref[2 * NZ * K : 2 * NZ * K + NZ * SUB, :] = aux[...].astype(BF16)


def merged(own, from_left, from_right):
    X = GROUP // 2
    m = lanes_of(own.shape) % GROUP
    left = pltpu.roll(from_left, LANES - X, 1)
    right = pltpu.roll(from_right, X, 1)
    out = jnp.where(m < X + REACH, own, jnp.where(m < X + 2 * REACH, right, 0.0))
    return jnp.where(m < REACH, left, out)


def main_kernel(
    K, NZ, X, levels, R,
    table_ref, pt_in, xl_ref, xr_ref, yl_ref, yr_ref, rl_ref, rr_ref, ylo_ref, yhi_ref, cls_ref, w_ref, block_ref, factor_ref,
    s_ref, v_ref, u_ref, gx_ref, pt_ref, t_ref, cg, wg, rg, cf, hp, ht,
):
    ext, wide = X + 4, X + 2
    KT = K // SUB
    sq = (LANES, LANES)
    lane_sq = lanes_of(sq)
    for z in range(NZ):
        for i in range(2):
            for h in range(2):
                cut = (slice((z * 2 + i) * K, (z * 2 + i + 1) * K), slice(h * LANES, (h + 1) * LANES))
                pt_ref[h, (z * ext + i) * K : (z * ext + i + 1) * K, :] = xl_ref[cut].astype(F32)
                at = z * ext + X + 2 + i
                pt_ref[h, at * K : (at + 1) * K, :] = xr_ref[cut].astype(F32)
    y_aux = [ref[2 * K : 2 * K + AUX, :].astype(F32) for ref in (yl_ref, yr_ref)]
    x_aux = [ref[2 * NZ * K : 2 * NZ * K + NZ * SUB, :].astype(F32) for ref in (xl_ref, xr_ref)]
    sides = []
    for side in range(2):
        own = y_aux[side]
        a = rl_ref[side, 2 * K : 2 * K + AUX, :].astype(F32)
        b = rr_ref[side, 2 * K : 2 * K + AUX, :].astype(F32)
        sides.append(merged(own, a, b))
    spread = jnp.zeros(sq, F32)
    row_sq = lax.broadcasted_iota(jnp.int32, sq, 0)
    spread_w = jnp.zeros(sq, F32)
    for side in range(2):
        at = (LANES - 1, LANES - 2, LANES - 3) if side == 0 else (0, 1, 2)
        for d in range(3):
            spread = jnp.where(row_sq == at[d], sides[side][d : d + 1, :], spread)
        spread_w = jnp.where(row_sq == at[0], sides[side][3:4, :] + sides[side][4:5, :], spread_w)
    y_class, y_weight = spread.T, spread_w.T
    keep = (lane_sq >= LANES // 2, lane_sq < LANES // 2)
    cg[0] = jnp.where(keep[0], y_class, 0.0)
    cg[3] = jnp.where(keep[1], y_class, 0.0)
    wg[0] = jnp.where(keep[0], y_weight, 0.0)
    wg[3] = jnp.where(keep[1], y_weight, 0.0)
    for h in range(2):
        lo = slice(h * LANES, (h + 1) * LANES)
        cg[1 + h] = jnp.zeros(sq, F32)
        wg[1 + h] = jnp.zeros(sq, F32)
        for z in range(NZ):
            g = z * GROUP
            cg[1 + h, g + REACH : g + REACH + X, :] = cls_ref[z * X : (z + 1) * X, lo].astype(F32) + 1.0
            cg[1 + h, g : g + REACH, :] = x_aux[0][z * SUB : z * SUB + 3, lo]
            cg[1 + h, g + REACH + X : g + 2 * REACH + X, :] = x_aux[1][z * SUB : z * SUB + 3, lo]
            wg[1 + h, g + REACH : g + REACH + X, :] = w_ref[z * X : (z + 1) * X, lo]
            wg[1 + h, g + REACH - 1 : g + REACH, :] = x_aux[0][z * SUB + 3 : z * SUB + 4, lo] + x_aux[0][z * SUB + 4 : z * SUB + 5, lo]
            wg[1 + h, g + REACH + X : g + REACH + X + 1, :] = x_aux[1][z * SUB + 3 : z * SUB + 4, lo] + x_aux[1][z * SUB + 4 : z * SUB + 5, lo]
    for t in range(4):
        ids = cg[t]
        cond = jnp.zeros(sq, F32)
        for j in range(table_ref.shape[0]):
            cond = jnp.where(ids == float(j + 1), table_ref[j], cond)
        cg[t] = cond

    zeros_g = jnp.zeros((GROUP, LANES), F32)

    def ahead(ref, t):
        nxt = ref[t + 1] if t < 3 else jnp.zeros(sq, F32)
        return jnp.where(lane_sq == LANES - 1, pltpu.roll(nxt, LANES - 1, 1), pltpu.roll(ref[t], LANES - 1, 1))

    def behind(ref, t):
        prv = ref[t - 1] if t > 0 else jnp.zeros(sq, F32)
        return jnp.where(lane_sq == 0, pltpu.roll(prv, 1, 1), pltpu.roll(ref[t], 1, 1))

    def around(ref, t):
        v = ref[t]
        return [
            pltpu.roll(v, LANES - 1, 0),
            pltpu.roll(v, 1, 0),
            ahead(ref, t),
            behind(ref, t),
            jnp.concatenate([v[GROUP:], zeros_g], 0),
            jnp.concatenate([zeros_g, v[:-GROUP]], 0),
        ]

    for t in range(4):
        c = cg[t]
        total = jnp.ones(sq, F32)
        for other in around(cg, t):
            total = total + 0.5 * (c + other)
        rg[t] = 1.0 / total
    picked = jnp.zeros(sq, F32)
    for t in range(4):
        c, r, w = cg[t], rg[t], wg[t]
        pairs = zip(around(cg, t), around(rg, t))
        terms = [r] + [0.5 * (c + c_n) * (r * r_n) for c_n, r_n in pairs]
        for j, term in enumerate(terms):
            if t in (1, 2):
                cf[j, t - 1] = w * term
                cf[7 + j, t - 1] = term
            else:
                to = j if t == 0 else 8 + j
                start = LANES - 1 if t == 0 else 0
                picked = jnp.where(lane_sq == to, pltpu.roll(w * term, (to - start) % LANES, 1), picked)
    edge_cf = picked.T
    for side, (recv, mine) in enumerate(((yl_ref, ylo_ref), (yr_ref, yhi_ref))):
        p1 = merged(recv[:K, :].astype(F32), rl_ref[side, :K, :].astype(F32), rr_ref[side, :K, :].astype(F32))
        p2 = recv[K : 2 * K, :].astype(F32)
        p0 = mine[:K, :].astype(F32)
        y_next, y_prev = (p0, p2) if side == 0 else (p2, p0)
        parts = [
            p1,
            pltpu.roll(p1, LANES - 1, 1),
            pltpu.roll(p1, 1, 1),
            y_next,
            y_prev,
            pltpu.roll(p1, LANES - GROUP, 1),
            pltpu.roll(p1, GROUP, 1),
        ]
        total = edge_cf[8 * side : 8 * side + 1, :] * parts[0]
        for j in range(1, 7):
            total = total + edge_cf[8 * side + j : 8 * side + j + 1, :] * parts[j]
        hp[side] = p1
        ht[side] = total

    lane = lanes_of((SUB, LANES))
    is_first, is_last = lane == 0, lane == LANES - 1

    def stencil(z, coef_row, first_cf, src, centre_row, x_step, z_step, halo, kt):
        row = pl.multiple_of(centre_row + kt * SUB, SUB)
        c = [src[h, pl.ds(row, SUB), :] for h in range(2)]
        up = [src[h, pl.ds(row + x_step, SUB), :] for h in range(2)]
        down = [src[h, pl.ds(row - x_step, SUB), :] for h in range(2)]
        hl = pltpu.roll(halo[0, kt * SUB : (kt + 1) * SUB, :], LANES - coef_row, 1)
        hr = pltpu.roll(halo[1, kt * SUB : (kt + 1) * SUB, :], LANES - 1 - coef_row, 1)
        fwd = [pltpu.roll(v, LANES - 1, 1) for v in c]
        bwd = [pltpu.roll(v, 1, 1) for v in c]
        nxt = [jnp.where(is_last, fwd[1], fwd[0]), jnp.where(is_last, hr, fwd[1])]
        prv = [jnp.where(is_first, hl, bwd[0]), jnp.where(is_first, bwd[0], bwd[1])]
        out = []
        for h in range(2):
            co = [cf[first_cf + j, h, pl.ds(coef_row, 1), :] for j in range(7)]
            acc = co[0] * c[h] + co[1] * up[h] + co[2] * down[h] + co[3] * nxt[h] + co[4] * prv[h]
            if z < NZ - 1:
                acc = acc + co[5] * src[h, pl.ds(row + z_step, SUB), :]
            if z > 0:
                acc = acc + co[6] * src[h, pl.ds(row - z_step, SUB), :]
            out.append(acc)
        return row, out

    def stage_one(i, carry):
        for z in range(NZ):
            for kt in range(KT):
                _, out = stencil(z, z * GROUP + i + 2, 0, pt_ref, (z * ext + i + 1) * K, K, ext * K, hp, kt)
                to = pl.multiple_of((z * wide + i) * K + kt * SUB, SUB)
                for h in range(2):
                    t_ref[h, pl.ds(to, SUB), :] = out[h]
        return carry

    lax.fori_loop(0, wide, stage_one, 0)

    lane_k = lanes_of((K, LANES))

    def stage_two(i, carry):
        gram, mixed = carry
        places = [[jnp.zeros((K, LANES), F32) for _ in range(levels)] for _ in range(2)]
        for half in range(2):
            x = 2 * i + half
            his = []
            for z in range(NZ):
                lines = []
                for kt in range(KT):
                    _, out = stencil(z, z * GROUP + x + REACH, 7, t_ref, (z * wide + x + 1) * K, K, wide * K, ht, kt)
                    row = pl.multiple_of((z * ext + x + 2) * K + kt * SUB, SUB)
                    to = pl.multiple_of((z * X + x) * K + kt * SUB, SUB)
                    both = []
                    for h in range(2):
                        s = out[h] + pt_ref[h, pl.ds(row, SUB), :]
                        s_ref[h, pl.ds(to, SUB), :] = s
                        both.append(s)
                    lines.append(jnp.concatenate(both, 1))
                line = jnp.concatenate(lines, 0)
                hi, lo = halves(line)
                gram = gram + nt(hi, jnp.concatenate([hi, lo], 0))
                his.append(hi)
            stack = jnp.concatenate(his, 0)
            leaf = nt(stack, block_ref[...]).astype(BF16)
            coef = nt(stack, factor_ref[...])
            for z in range(NZ):
                mixed = mixed + nt(his[z], leaf[z * K : (z + 1) * K])
                part = coef[z * K : (z + 1) * K]
                at = half * NZ * R + z * R
                here = (lane_k >= at) & (lane_k < at + R)
                for q in range(2):
                    for l in range(levels):
                        moved = pltpu.roll(part, (at - (q * levels + l) * R) % LANES, 1)
                        places[q][l] = jnp.where(here, moved, places[q][l])
        for l in range(levels):
            v_ref[l, i] = places[0][l].astype(BF16)
            u_ref[l, i] = places[1][l].astype(BF16)
        return gram, mixed

    gram, mixed = lax.fori_loop(0, X // 2, stage_two, (jnp.zeros((K, 2 * K), F32), jnp.zeros((K, K), F32)))
    low = gram[:, K:]
    gx_ref[...] = jnp.zeros_like(gx_ref)
    gx_ref[:, :K] = gram[:, :K] + low + low.T
    gx_ref[:, LANES // 2 : LANES // 2 + K] = mixed


def couple_kernel(K, level_of, gx_ref, u_ref, *refs):
    sib_refs, out_ref = refs[:-1], refs[-1]
    total = jnp.zeros((K, K), F32)
    sums = {}
    for l, ref in zip(level_of, sib_refs):
        sums.setdefault(l, []).append(ref)
    for l, group in sums.items():
        for i in range(u_ref.shape[1]):
            v = group[0][i].astype(F32)
            for ref in group[1:]:
                v = v + ref[i].astype(F32)
            total = total + nt(u_ref[l, i], v.astype(BF16))
    out_ref[...] = gx_ref[...]
    at = LANES // 2
    out_ref[:, at : at + K] = gx_ref[:, at : at + K] + total


def finish_kernel(K, NZ, X, cells, gx_ref, s_ref, basis_ref, proj_ref, out, sem):
    lane = lanes_of((K, LANES))
    row = lax.broadcasted_iota(jnp.int32, (K, LANES), 0)
    half = LANES // 2
    gx = gx_ref[...] * (1.0 / cells)
    gram = gx[:, :K]
    mixed = gram + gx[:, half : half + K]
    aug = jnp.where(lane < K, gx, jnp.where(lane - half == row, 1.0, 0.0))
    for j in range(K - 1):
        pivot_row = aug[j : j + 1, :]
        factor = aug[:, j : j + 1] * (1.0 / aug[j : j + 1, j : j + 1])
        aug = aug - jnp.where(row > j, factor, 0.0) * pivot_row
    pivots = jnp.sum(jnp.where(lane == row, aug, 0.0), axis=1, keepdims=True)
    inverse = aug[:, half : half + K] * lax.rsqrt(pivots)
    left = jnp.dot(inverse, mixed, precision=HIGH, preferred_element_type=F32)
    proj_ref[...] = nt(left, inverse, precision=HIGH)
    i_hi, i_lo = halves(inverse)
    lhs = jnp.concatenate([i_hi, i_lo, i_hi], 1)
    W = 2 * LANES
    copies = []
    for z in range(NZ):

        def line(x, carry, z=z):
            at = pl.multiple_of((z * X + x) * K, SUB)
            s = jnp.concatenate([s_ref[h, pl.ds(at, K), :] for h in range(2)], 1)
            hi, lo = halves(s)
            b = jnp.dot(lhs, jnp.concatenate([hi, hi, lo], 0), preferred_element_type=F32)
            for h in range(2):
                out[h, z, pl.ds(x, K, stride=X), :] = b[:, h * LANES : (h + 1) * LANES]
            return carry

        lax.fori_loop(0, X, line, 0)
        for h in range(2):
            for part in range(1):
                copies.append(
                    pltpu.make_async_copy(
                        out.at[h, z].reshape(K, X, LANES), basis_ref.at[:, z, :, pl.ds(h * LANES, LANES)], sem.at[z, h]
                    )
                )
                copies[-1].start()
    for c in copies:
        c.wait()


def exchanged(v, axis, bits):
    return lax.ppermute(v, axis, [(i, i ^ bits) for i in range(lax.axis_size(axis))])


def shifted(v, axis, by):
    n = lax.axis_size(axis)
    return lax.ppermute(v, axis, [(i, i + by) for i in range(n) if 0 <= i + by < n])


def summed(v):
    for axis in ("gx", "gy"):
        bit = 1
        while bit < lax.axis_size(axis):
            v = v + exchanged(v, axis, bit)
            bit *= 2
    return v


def shards(probes, classes, class_table, weights, prior_block, prior_left, prior_right, block_ranks):
    K, NZ, X, W = probes.shape
    R = prior_left.shape[1]
    levels = lax.axis_size("gy").bit_length() - 1
    cells = float(NZ * X * W * lax.axis_size("gx") * lax.axis_size("gy"))
    rows, ext, wide = NZ * X, X + 4, X + 2
    shape = jax.ShapeDtypeStruct
    cls2, w2 = classes.reshape(rows, W), weights.reshape(rows, W)
    params = functools.partial(pltpu.CompilerParams, vmem_limit_bytes=32 << 20)
    y_rows, x_rows = 2 * K + AUX, 2 * NZ * K + NZ * SUB
    pt, ylo, yhi, xlo, xhi = pl.pallas_call(
        functools.partial(pack_kernel, K, NZ, X),
        out_shape=(
            shape((2, NZ * ext * K, LANES), F32),
            shape((y_rows, LANES), BF16),
            shape((y_rows, LANES), BF16),
            shape((x_rows, W), BF16),
            shape((x_rows, W), BF16),
        ),
        in_specs=[VMEM] * 3,
        out_specs=(VMEM,) * 5,
        scratch_shapes=[pltpu.VMEM((4, LANES, LANES), F32), pltpu.VMEM((NZ * SUB, W), F32)],
        compiler_params=params(),
        name="pack",
    )(probes.reshape(K * rows, W), cls2, w2)
    xl, xr = shifted(xhi, "gx", 1), shifted(xlo, "gx", -1)
    yl, yr = shifted(yhi, "gy", 1), shifted(ylo, "gy", -1)
    both = jnp.stack([yl, yr])
    rl, rr = shifted(both, "gx", 1), shifted(both, "gx", -1)
    scale = jnp.array([float(W * 2**l) ** -0.5 for l in range(levels)], F32)
    mask = (jnp.arange(R, dtype=jnp.int32)[None, :] < block_ranks[:levels, None]).astype(F32) * scale[:, None]
    right = prior_right[:levels] * mask[:, :, None]
    factor = jnp.concatenate([right, prior_left[:levels]], 0).reshape(2 * levels * R, W)
    if 2 * levels * R < LANES:
        factor = jnp.pad(factor, ((0, LANES - 2 * levels * R), (0, 0)))
    slab = (2, rows * K, LANES)
    side = (levels, X // 2, K, LANES)
    s, v, u, gx, _ = pl.pallas_call(
        functools.partial(main_kernel, K, NZ, X, levels, R),
        out_shape=(
            shape(slab, F32),
            shape(side, BF16),
            shape(side, BF16),
            shape((K, LANES), F32),
            shape(pt.shape, F32),
        ),
        in_specs=[pl.BlockSpec(memory_space=pltpu.SMEM)] + [VMEM] * 13,
        out_specs=(VMEM,) * 5,
        scratch_shapes=[
            pltpu.VMEM((2, NZ * wide * K, LANES), F32),
            pltpu.VMEM((4, LANES, LANES), F32),
            pltpu.VMEM((4, LANES, LANES), F32),
            pltpu.VMEM((4, LANES, LANES), F32),
            pltpu.VMEM((14, 2, LANES, LANES), F32),
            pltpu.VMEM((2, K, LANES), F32),
            pltpu.VMEM((2, K, LANES), F32),
        ],
        input_output_aliases={1: 4},
        compiler_params=params(),
        name="sketch",
    )(class_table, pt, xl, xr, yl, yr, rl, rr, ylo, yhi, cls2, w2, prior_block.astype(BF16), factor.astype(BF16))
    level_of, sibs = [], []
    if levels <= 2:
        for l in range(levels):
            for d in range(2**l):
                level_of.append(l)
                sibs.append(exchanged(v[l], "gy", 2**l + d))
    else:
        pending = v.astype(F32)
        for l in range(levels):
            got = exchanged(pending.astype(BF16), "gy", 2**l)
            level_of.append(l)
            sibs.append(got[0])
            pending = pending[1:] + got[1:].astype(F32)
    gx = pl.pallas_call(
        functools.partial(couple_kernel, K, tuple(level_of)),
        out_shape=shape((K, LANES), F32),
        in_specs=[VMEM] * (2 + len(sibs)),
        out_specs=VMEM,
        compiler_params=params(),
        name="couple",
    )(gx, u, *sibs)
    gx = summed(gx)
    basis, projected = pl.pallas_call(
        functools.partial(finish_kernel, K, NZ, X, cells),
        out_shape=(shape((K, NZ, X, W), F32), shape((K, K), F32)),
        in_specs=[VMEM] * 2,
        out_specs=(ANY, VMEM),
        scratch_shapes=[pltpu.VMEM((2, NZ, K * X, LANES), F32), pltpu.SemaphoreType.DMA((NZ, 2))],
        compiler_params=params(),
        name="finish",
    )(gx, s)
    return basis, projected


def solution(mesh):
    return jax.shard_map(
        shards,
        mesh=mesh,
        in_specs=(
            P(None, None, "gx", "gy"),
            P(None, "gx", "gy"),
            P(),
            P(None, "gx", "gy"),
            P("gy", None),
            P(None, None, "gy"),
            P(None, None, "gy"),
            P(),
        ),
        out_specs=(P(None, None, "gx", "gy"), P()),
        check_vma=False,
    )
```

profile of v0, /device:TPU:0, one launch (start us, length us, event | category | flops | bytes accessed | tf_op | source)
XLA Modules:
  0.0 86.7 jit_solution(7114814339290906557)
XLA Ops:
  0.6 1.4 %copy-done = bf16[48,4,16,256]{3,2,1,0:T(8,128)(2,1)S(1)} copy-done((bf16[48,4,16,256]{3,2,1,0:T(8,128)(2,1)S(1)}, bf16[48,4,16,256]{3,2,1,0:T(8,128)(2,1)}, u32[]{:S(2)}) %copy-start) | copy-done | bytes 1572888
  3.7 1.7 %pack.1 = (f32[2,3840,128]{2,1,0:T(8,128)S(1)}, bf16[112,128]{1,0:T(8,128)(2,1)S(1)}, bf16[112,128]{1,0:T(8,128)(2,1)S(1)}, bf16[416,256]{1,0:T(8,128)(2,1)S(1)}, bf16[416,256]{1,0:T(8,128)(2,1)S(1)}) custom-call(bf16[3072,256]{1,0:T(8,128)(2,1)S(1)} %bitcast.11, s32[64,256]{1,0:T(8,128)S(1)} %bitcast.12, f32[64,256]{1,0:T(8,128)S(1)} %bitcast.14), custom_call_target="tpu_custom_call" | custom-call | tf_op jit(solution)/shard_map/pack/pallas_call | solution.py:396
  5.5 2.4 %collective-permute-start.2 = (bf16[112,128]{1,0:T(8,128)(2,1)S(1)}, bf16[112,128]{1,0:T(8,128)(2,1)S(1)}, u32[]{:S(2)}, u32[]{:S(2)}) collective-permute-start(bf16[112,128]{1,0:T(8,128)(2,1)S(1)} %get-tuple-element.14.yhi_ref), channel_id=1, source_target_pairs={{0,1},{1,2},{2,3},{4,5},{5,6},{6,7},{8,9},{9,10},{10,11},{12,13},{... | collective-permute-start | bytes 86024 | tf_op jit(solution)/shard_map/ppermute | solution.py:374
  7.9 1.3 %collective-permute-start.3 = (bf16[112,128]{1,0:T(8,128)(2,1)S(1)}, bf16[112,128]{1,0:T(8,128)(2,1)S(1)}, u32[]{:S(2)}, u32[]{:S(2)}) collective-permute-start(bf16[112,128]{1,0:T(8,128)(2,1)S(1)} %get-tuple-element.15.ylo_ref), channel_id=1, source_target_pairs={{1,0},{2,1},{3,2},{5,4},{6,5},{7,6},{9,8},{10,9},{11,10},{13,12},{... | collective-permute-start | bytes 86024 | tf_op jit(solution)/shard_map/ppermute | solution.py:374
  9.2 4.2 %collective-permute-start = (bf16[416,256]{1,0:T(8,128)(2,1)S(1)}, bf16[416,256]{1,0:T(8,128)(2,1)S(1)}, u32[]{:S(2)}, u32[]{:S(2)}) collective-permute-start(bf16[416,256]{1,0:T(8,128)(2,1)S(1)} %get-tuple-element.12), channel_id=1, source_target_pairs={{0,4},{4,8},{8,12},{12,16},{16,20},{20,24},{24,28},{1,5},{5,9},{9,... | collective-permute-start | bytes 638984 | tf_op jit(solution)/shard_map/ppermute | solution.py:374
  13.4 1.3 %collective-permute-start.1 = (bf16[416,256]{1,0:T(8,128)(2,1)S(1)}, bf16[416,256]{1,0:T(8,128)(2,1)S(1)}, u32[]{:S(2)}, u32[]{:S(2)}) collective-permute-start(bf16[416,256]{1,0:T(8,128)(2,1)S(1)} %get-tuple-element.13), channel_id=1, source_target_pairs={{4,0},{8,4},{12,8},{16,12},{20,16},{24,20},{28,24},{5,1},{9,5},{13... | collective-permute-start | bytes 638984 | tf_op jit(solution)/shard_map/ppermute | solution.py:374
  17.0 1.0 %convert_element_type.4.block_ref = bf16[256,256]{1,0:T(8,128)(2,1)S(1)} convert(f32[256,256]{1,0:T(8,128)} %param.13) | non-fusion elementwise | flops 65536 | bytes 393216 | tf_op jit(solution)/shard_map/convert_element_type | solution.py:446
  18.0 1.3 %collective-permute-start.5 = (bf16[2,112,128]{2,1,0:T(8,128)(2,1)S(1)}, bf16[2,112,128]{2,1,0:T(8,128)(2,1)S(1)}, u32[]{:S(2)}, u32[]{:S(2)}) collective-permute-start(bf16[2,112,128]{2,1,0:T(8,128)(2,1)S(1)} %pad_maximum_fusion), channel_id=1, source_target_pairs={{4,0},{8,4},{12,8},{16,12},{20,16},{24,20},{28,24},{5,1},{9,5},{13... | collective-permute-start | bytes 172040 | tf_op jit(solution)/shard_map/ppermute | solution.py:374
  19.3 5.2 %collective-permute-start.4 = (bf16[2,112,128]{2,1,0:T(8,128)(2,1)S(1)}, bf16[2,112,128]{2,1,0:T(8,128)(2,1)S(1)}, u32[]{:S(2)}, u32[]{:S(2)}) collective-permute-start(bf16[2,112,128]{2,1,0:T(8,128)(2,1)S(1)} %pad_maximum_fusion), channel_id=1, source_target_pairs={{0,4},{4,8},{8,12},{12,16},{16,20},{20,24},{24,28},{1,5},{5,9},{9,... | collective-permute-start | bytes 172040 | tf_op jit(solution)/shard_map/ppermute | solution.py:374
  24.7 2.0 %collective-permute-done.4.rl_ref = bf16[2,112,128]{2,1,0:T(8,128)(2,1)S(1)} collective-permute-done((bf16[2,112,128]{2,1,0:T(8,128)(2,1)S(1)}, bf16[2,112,128]{2,1,0:T(8,128)(2,1)S(1)}, u32[]{:S(2)}, u32[]{:S(2)}) %collective-permute-start.4) | collective-permute-done | bytes 57376 | tf_op jit(solution)/shard_map/ppermute | solution.py:374
  28.3 12.6 %sketch.1 = (f32[2,3072,128]{2,1,0:T(8,128)S(1)}, bf16[2,8,48,128]{3,2,1,0:T(8,128)(2,1)S(1)}, bf16[2,8,48,128]{3,2,1,0:T(8,128)(2,1)S(1)}, f32[48,128]{1,0:T(8,128)S(1)}, f32[2,3840,128]{2,1,0:T(8,128)S(1)}) custom-call(f32[8]{0:T(128)S(1)} %copy-done.4, f32[2,3840,128]{2,1,0:T(8,128)S(1)} %get-tuple-element.11.pt_in, ...), custom_call_target="tpu_custom_call", output_to_operand_aliasing={{4}: (1, {})} | custom-call | tf_op jit(solution)/shard_map/sketch/pallas_call | solution.py:423
  41.6 3.1 %collective-permute-start.8 = (bf16[8,48,128]{2,1,0:T(8,128)(2,1)S(1)}, bf16[8,48,128]{2,1,0:T(8,128)(2,1)S(1)}, u32[]{:S(2)}, u32[]{:S(2)}) collective-permute-start(bf16[8,48,128]{2,1,0:T(8,128)(2,1)S(1)} %get-tuple-element.20), channel_id=1, source_target_pairs={{0,3},{1,2},{2,1},{3,0},{4,7},{5,6},{6,5},{7,4},{8,11},{9,10},{10,... | collective-permute-start | bytes 294920 | tf_op jit(solution)/shard_map/ppermute | solution.py:369
  44.7 3.1 %collective-permute-done.8.refs_2_ = bf16[8,48,128]{2,1,0:T(8,128)(2,1)S(1)} collective-permute-done((bf16[8,48,128]{2,1,0:T(8,128)(2,1)S(1)}, bf16[8,48,128]{2,1,0:T(8,128)(2,1)S(1)}, u32[]{:S(2)}, u32[]{:S(2)}) %collective-permute-start.8) | collective-permute-done | bytes 98336 | tf_op jit(solution)/shard_map/ppermute | solution.py:369
  47.8 2.3 %collective-permute-done.7.refs_1_ = bf16[8,48,128]{2,1,0:T(8,128)(2,1)S(1)} collective-permute-done((bf16[8,48,128]{2,1,0:T(8,128)(2,1)S(1)}, bf16[8,48,128]{2,1,0:T(8,128)(2,1)S(1)}, u32[]{:S(2)}, u32[]{:S(2)}) %collective-permute-start.7) | collective-permute-done | bytes 98336 | tf_op jit(solution)/shard_map/ppermute | solution.py:369
  50.4 3.0 %collective-permute-start.9 = (f32[48,128]{1,0:T(8,128)S(1)}, f32[48,128]{1,0:T(8,128)S(1)}, u32[]{:S(2)}, u32[]{:S(2)}) collective-permute-start(f32[48,128]{1,0:T(8,128)S(1)} %couple.1), channel_id=1, source_target_pairs={{0,4},{4,0},{8,12},{12,8},{16,20},{20,16},{24,28},{28,24},{1,5},{5... | collective-permute-start | bytes 73736 | tf_op jit(solution)/shard_map/ppermute | solution.py:369
  53.4 1.8 %collective-permute-done.9 = f32[48,128]{1,0:T(8,128)S(1)} collective-permute-done((f32[48,128]{1,0:T(8,128)S(1)}, f32[48,128]{1,0:T(8,128)S(1)}, u32[]{:S(2)}, u32[]{:S(2)}) %collective-permute-start.9) | collective-permute-done | bytes 24608 | tf_op jit(solution)/shard_map/ppermute | solution.py:369
  55.2 3.8 %collective-permute-start.10 = (f32[48,128]{1,0:T(8,128)S(1)}, f32[48,128]{1,0:T(8,128)S(1)}, u32[]{:S(2)}, u32[]{:S(2)}) collective-permute-start(f32[48,128]{1,0:T(8,128)S(1)} %add.17), channel_id=1, source_target_pairs={{0,8},{4,12},{8,0},{12,4},{16,24},{20,28},{24,16},{28,20},{1,9},{5... | collective-permute-start | bytes 73736 | tf_op jit(solution)/shard_map/ppermute | solution.py:369
  59.0 1.8 %collective-permute-done.10 = f32[48,128]{1,0:T(8,128)S(1)} collective-permute-done((f32[48,128]{1,0:T(8,128)S(1)}, f32[48,128]{1,0:T(8,128)S(1)}, u32[]{:S(2)}, u32[]{:S(2)}) %collective-permute-start.10) | collective-permute-done | bytes 24608 | tf_op jit(solution)/shard_map/ppermute | solution.py:369
  60.8 3.0 %collective-permute-start.11 = (f32[48,128]{1,0:T(8,128)S(1)}, f32[48,128]{1,0:T(8,128)S(1)}, u32[]{:S(2)}, u32[]{:S(2)}) collective-permute-start(f32[48,128]{1,0:T(8,128)S(1)} %add.18), channel_id=1, source_target_pairs={{0,16},{4,20},{8,24},{12,28},{16,0},{20,4},{24,8},{28,12},{1,17},{... | collective-permute-start | bytes 73736 | tf_op jit(solution)/shard_map/ppermute | solution.py:369
  63.9 1.8 %collective-permute-done.11 = f32[48,128]{1,0:T(8,128)S(1)} collective-permute-done((f32[48,128]{1,0:T(8,128)S(1)}, f32[48,128]{1,0:T(8,128)S(1)}, u32[]{:S(2)}, u32[]{:S(2)}) %collective-permute-start.11) | collective-permute-done | bytes 24608 | tf_op jit(solution)/shard_map/ppermute | solution.py:369
  65.7 1.2 %collective-permute-done.12 = f32[48,128]{1,0:T(8,128)S(1)} collective-permute-done((f32[48,128]{1,0:T(8,128)S(1)}, f32[48,128]{1,0:T(8,128)S(1)}, u32[]{:S(2)}, u32[]{:S(2)}) %collective-permute-start.12) | collective-permute-done | bytes 24608 | tf_op jit(solution)/shard_map/ppermute | solution.py:369
  66.9 1.9 %collective-permute-start.13 = (f32[48,128]{1,0:T(8,128)S(1)}, f32[48,128]{1,0:T(8,128)S(1)}, u32[]{:S(2)}, u32[]{:S(2)}) collective-permute-start(f32[48,128]{1,0:T(8,128)S(1)} %add.20), channel_id=1, source_target_pairs={{0,2},{1,3},{2,0},{3,1},{4,6},{5,7},{6,4},{7,5},{8,10},{9,11},{10,... | collective-permute-start | bytes 73736 | tf_op jit(solution)/shard_map/ppermute | solution.py:369
  68.8 1.9 %collective-permute-done.13 = f32[48,128]{1,0:T(8,128)S(1)} collective-permute-done((f32[48,128]{1,0:T(8,128)S(1)}, f32[48,128]{1,0:T(8,128)S(1)}, u32[]{:S(2)}, u32[]{:S(2)}) %collective-permute-start.13) | collective-permute-done | bytes 24608 | tf_op jit(solution)/shard_map/ppermute | solution.py:369
  70.7 16.0 %finish.1 = (f32[48,4,16,256]{3,2,1,0:T(8,128)}, f32[48,48]{1,0:T(8,128)}) custom-call(f32[48,128]{1,0:T(8,128)S(1)} %add.21.gx_ref, f32[2,3072,128]{2,1,0:T(8,128)S(1)} %get-tuple-element.19.s_ref), custom_call_target="tpu_custom_call" | custom-call | tf_op jit(solution)/shard_map/finish/pallas_call | solution.py:469
  (31 shorter events, 6.9 us)
Async XLA Ops:
  0.6 1.4 %copy-start = (bf16[48,4,16,256]{3,2,1,0:T(8,128)(2,1)S(1)}, bf16[48,4,16,256]{3,2,1,0:T(8,128)(2,1)}, u32[]{:S(2)}) copy-start(bf16[48,4,16,256]{3,2,1,0:T(8,128)(2,1)} %param.9) | copy-start | bytes 4718596
  2.0 0.8 copy-start.1
  2.9 0.8 copy-start.2
  5.5 12.6 %collective-permute-start.2 = (bf16[112,128]{1,0:T(8,128)(2,1)S(1)}, bf16[112,128]{1,0:T(8,128)(2,1)S(1)}, u32[]{:S(2)}, u32[]{:S(2)}) collective-permute-start(bf16[112,128]{1,0:T(8,128)(2,1)S(1)} %get-tuple-element.14.yhi_ref), channel_id=1, source_target_pairs={{0,1},{1,2},{2,3},{4,5},{5,6},{6,7},{8,9},{9,10},{10,11},{12,13},{... | collective-permute-start | bytes 86024 | tf_op jit(solution)/shard_map/ppermute | solution.py:374
  7.9 10.2 %collective-permute-start.3 = (bf16[112,128]{1,0:T(8,128)(2,1)S(1)}, bf16[112,128]{1,0:T(8,128)(2,1)S(1)}, u32[]{:S(2)}, u32[]{:S(2)}) collective-permute-start(bf16[112,128]{1,0:T(8,128)(2,1)S(1)} %get-tuple-element.15.ylo_ref), channel_id=1, source_target_pairs={{1,0},{2,1},{3,2},{5,4},{6,5},{7,6},{9,8},{10,9},{11,10},{13,12},{... | collective-permute-start | bytes 86024 | tf_op jit(solution)/shard_map/ppermute | solution.py:374
  9.2 17.6 %collective-permute-start = (bf16[416,256]{1,0:T(8,128)(2,1)S(1)}, bf16[416,256]{1,0:T(8,128)(2,1)S(1)}, u32[]{:S(2)}, u32[]{:S(2)}) collective-permute-start(bf16[416,256]{1,0:T(8,128)(2,1)S(1)} %get-tuple-element.12), channel_id=1, source_target_pairs={{0,4},{4,8},{8,12},{12,16},{16,20},{20,24},{24,28},{1,5},{5,9},{9,... | collective-permute-start | bytes 638984 | tf_op jit(solution)/shard_map/ppermute | solution.py:374
  13.4 13.4 %collective-permute-start.1 = (bf16[416,256]{1,0:T(8,128)(2,1)S(1)}, bf16[416,256]{1,0:T(8,128)(2,1)S(1)}, u32[]{:S(2)}, u32[]{:S(2)}) collective-permute-start(bf16[416,256]{1,0:T(8,128)(2,1)S(1)} %get-tuple-element.13), channel_id=1, source_target_pairs={{4,0},{8,4},{12,8},{16,12},{20,16},{24,20},{28,24},{5,1},{9,5},{13... | collective-permute-start | bytes 638984 | tf_op jit(solution)/shard_map/ppermute | solution.py:374
  18.0 6.7 %collective-permute-start.5 = (bf16[2,112,128]{2,1,0:T(8,128)(2,1)S(1)}, bf16[2,112,128]{2,1,0:T(8,128)(2,1)S(1)}, u32[]{:S(2)}, u32[]{:S(2)}) collective-permute-start(bf16[2,112,128]{2,1,0:T(8,128)(2,1)S(1)} %pad_maximum_fusion), channel_id=1, source_target_pairs={{4,0},{8,4},{12,8},{16,12},{20,16},{24,20},{28,24},{5,1},{9,5},{13... | collective-permute-start | bytes 172040 | tf_op jit(solution)/shard_map/ppermute | solution.py:374
  19.3 7.4 %collective-permute-start.4 = (bf16[2,112,128]{2,1,0:T(8,128)(2,1)S(1)}, bf16[2,112,128]{2,1,0:T(8,128)(2,1)S(1)}, u32[]{:S(2)}, u32[]{:S(2)}) collective-permute-start(bf16[2,112,128]{2,1,0:T(8,128)(2,1)S(1)} %pad_maximum_fusion), channel_id=1, source_target_pairs={{0,4},{4,8},{8,12},{12,16},{16,20},{20,24},{24,28},{1,5},{5,9},{9,... | collective-permute-start | bytes 172040 | tf_op jit(solution)/shard_map/ppermute | solution.py:374
  26.8 0.8 copy-start.3
  27.6 0.7 copy-start.4
  40.8 3.9 %collective-permute-start.6 = (bf16[8,48,128]{2,1,0:T(8,128)(2,1)S(1)}, bf16[8,48,128]{2,1,0:T(8,128)(2,1)S(1)}, u32[]{:S(2)}, u32[]{:S(2)}) collective-permute-start(bf16[8,48,128]{2,1,0:T(8,128)(2,1)S(1)} %get-tuple-element.21), channel_id=1, source_target_pairs={{0,1},{1,0},{2,3},{3,2},{4,5},{5,4},{6,7},{7,6},{8,9},{9,8},{10,11... | collective-permute-start | bytes 294920 | tf_op jit(solution)/shard_map/ppermute | solution.py:369
  41.6 6.3 %collective-permute-start.8 = (bf16[8,48,128]{2,1,0:T(8,128)(2,1)S(1)}, bf16[8,48,128]{2,1,0:T(8,128)(2,1)S(1)}, u32[]{:S(2)}, u32[]{:S(2)}) collective-permute-start(bf16[8,48,128]{2,1,0:T(8,128)(2,1)S(1)} %get-tuple-element.20), channel_id=1, source_target_pairs={{0,3},{1,2},{2,1},{3,0},{4,7},{5,6},{6,5},{7,4},{8,11},{9,10},{10,... | collective-permute-start | bytes 294920 | tf_op jit(solution)/shard_map/ppermute | solution.py:369
  44.7 5.5 %collective-permute-start.7 = (bf16[8,48,128]{2,1,0:T(8,128)(2,1)S(1)}, bf16[8,48,128]{2,1,0:T(8,128)(2,1)S(1)}, u32[]{:S(2)}, u32[]{:S(2)}) collective-permute-start(bf16[8,48,128]{2,1,0:T(8,128)(2,1)S(1)} %get-tuple-element.20), channel_id=1, source_target_pairs={{0,2},{1,3},{2,0},{3,1},{4,6},{5,7},{6,4},{7,5},{8,10},{9,11},{10,... | collective-permute-start | bytes 294920 | tf_op jit(solution)/shard_map/ppermute | solution.py:369
  50.4 4.8 %collective-permute-start.9 = (f32[48,128]{1,0:T(8,128)S(1)}, f32[48,128]{1,0:T(8,128)S(1)}, u32[]{:S(2)}, u32[]{:S(2)}) collective-permute-start(f32[48,128]{1,0:T(8,128)S(1)} %couple.1), channel_id=1, source_target_pairs={{0,4},{4,0},{8,12},{12,8},{16,20},{20,16},{24,28},{28,24},{1,5},{5... | collective-permute-start | bytes 73736 | tf_op jit(solution)/shard_map/ppermute | solution.py:369
  55.2 5.6 %collective-permute-start.10 = (f32[48,128]{1,0:T(8,128)S(1)}, f32[48,128]{1,0:T(8,128)S(1)}, u32[]{:S(2)}, u32[]{:S(2)}) collective-permute-start(f32[48,128]{1,0:T(8,128)S(1)} %add.17), channel_id=1, source_target_pairs={{0,8},{4,12},{8,0},{12,4},{16,24},{20,28},{24,16},{28,20},{1,9},{5... | collective-permute-start | bytes 73736 | tf_op jit(solution)/shard_map/ppermute | solution.py:369
  60.8 4.8 %collective-permute-start.11 = (f32[48,128]{1,0:T(8,128)S(1)}, f32[48,128]{1,0:T(8,128)S(1)}, u32[]{:S(2)}, u32[]{:S(2)}) collective-permute-start(f32[48,128]{1,0:T(8,128)S(1)} %add.18), channel_id=1, source_target_pairs={{0,16},{4,20},{8,24},{12,28},{16,0},{20,4},{24,8},{28,12},{1,17},{... | collective-permute-start | bytes 73736 | tf_op jit(solution)/shard_map/ppermute | solution.py:369
  65.7 1.2 %collective-permute-start.12 = (f32[48,128]{1,0:T(8,128)S(1)}, f32[48,128]{1,0:T(8,128)S(1)}, u32[]{:S(2)}, u32[]{:S(2)}) collective-permute-start(f32[48,128]{1,0:T(8,128)S(1)} %add.19), channel_id=1, source_target_pairs={{0,1},{1,0},{2,3},{3,2},{4,5},{5,4},{6,7},{7,6},{8,9},{9,8},{10,11... | collective-permute-start | bytes 73736 | tf_op jit(solution)/shard_map/ppermute | solution.py:369
  66.9 3.8 %collective-permute-start.13 = (f32[48,128]{1,0:T(8,128)S(1)}, f32[48,128]{1,0:T(8,128)S(1)}, u32[]{:S(2)}, u32[]{:S(2)}) collective-permute-start(f32[48,128]{1,0:T(8,128)S(1)} %add.20), channel_id=1, source_target_pairs={{0,2},{1,3},{2,0},{3,1},{4,6},{5,7},{6,4},{7,5},{8,10},{9,11},{10,... | collective-permute-start | bytes 73736 | tf_op jit(solution)/shard_map/ppermute | solution.py:369
where the time goes:
time: 87.3 us; the launch traced here: 86.7 us
  starting transfers between devices  31.3 us (36%)
  Pallas kernels  30.6 us (35%)
  waiting for transfers between devices  16.1 us (18%)
  local copies, waits for them, and re-layouts  5.36 us (6%)
  other arithmetic  2.58 us (3%)
    pallas_call x1, Pallas kernels, shards(): pl.pallas_call(functools.partial(finish_kernel, K, NZ, X, cells), out_sha...  16 us
    ppermute x6, starting transfers between devices, shifted(): lax.ppermute(v, axis, [(i, i + by) for i in range(n) if 0 <= i + by < n])  15.7 us
    ppermute x8, starting transfers between devices, exchanged(): lax.ppermute(v, axis, [(i, i ^ bits) for i in range(lax.axis_size(axis))])  15.6 us
    ppermute x8, waiting for transfers between devices, exchanged(): lax.ppermute(v, axis, [(i, i ^ bits) for i in range(lax.axis_size(axis))])  13.9 us
    pallas_call x1, Pallas kernels, shards(): pl.pallas_call(functools.partial(main_kernel, K, NZ, X, levels, R), out_s...  12.6 us
    unnamed x10, local copies, waits for them, and re-layouts  4.57 us
    ppermute x6, waiting for transfers between devices, shifted(): lax.ppermute(v, axis, [(i, i + by) for i in range(n) if 0 <= i + by < n])  2.2 us
  transfers between devices with their start and end apart: 14, of which 9 were waited for; matrix products, arithmetic and copies ran while one was open for 4% of the time, Pallas kernels for 0%

commit v1 on v0

v1 whole, which is shorter than its diff:
```python
import functools
import jax
import jax.numpy as jnp
from jax import lax
from jax.experimental import pallas as pl
from jax.experimental.pallas import tpu as pltpu
from jax.sharding import PartitionSpec as P

HIGH = lax.Precision.HIGHEST
F32 = jnp.float32
BF16 = jnp.bfloat16
LANES = 128
SUB = 8
GROUP = 32
REACH = 3
AXES = ("gy", "gx")
UNROLL_ONE = 3
UNROLL_TWO = 2
UNROLL_GRAM = 8
NLINES = 4
GRAM_PARTS = 2
AUX = 16
VMEM = pl.BlockSpec(memory_space=pltpu.VMEM)
HBM = pl.BlockSpec(memory_space=pltpu.HBM)


def lanes_of(shape):
    return lax.broadcasted_iota(jnp.int32, shape, len(shape) - 1)


def halves(v):
    hi = v.astype(BF16)
    return hi, (v - hi.astype(F32)).astype(BF16)


def nt(a, b, precision=None):
    return lax.dot_general(a, b, (((1,), (1,)), ((), ())), precision=precision, preferred_element_type=F32)


def pack_kernel(K, NZ, X, p_hbm, cls_hbm, w_hbm, pt_ref, cg_ref, wg_ref, own_ref, y0_ref, y1_ref, x0_ref, x1_ref, p_ref, cls_ref, w_ref, edge, aux, yaux, sem):
    rows, ext = NZ * X, X + 4
    parts = 4
    step = K * rows // parts
    loads = [pltpu.make_async_copy(cls_hbm, cls_ref, sem.at[parts]), pltpu.make_async_copy(w_hbm, w_ref, sem.at[parts + 1])]
    for i in range(parts):
        loads.append(pltpu.make_async_copy(p_hbm.at[pl.ds(i * step, step)], p_ref.at[pl.ds(i * step, step)], sem.at[i]))
    for load in loads:
        load.start()
    loads[0].wait()
    loads[1].wait()
    odd = [lax.rem(lax.axis_index(axis), 2) for axis in ("gx", "gy")]
    turned = []
    for source, grid in ((cls_ref, cg_ref), (w_ref, wg_ref)):
        for h in range(2):
            grid[h] = jnp.zeros((LANES, LANES), F32)
        for z in range(NZ):
            v = source[z * X : (z + 1) * X, :].astype(F32)
            if source is cls_ref:
                v = v + 1.0
            at = z * GROUP + REACH
            for h in range(2):
                grid[h, at : at + X, :] = v[:, h * LANES : (h + 1) * LANES]
        turned.append(jnp.where(lanes_of((LANES, LANES)) < LANES // 2, grid[0], grid[1]).T)
    yaux[...] = jnp.zeros_like(yaux)
    for side in range(2):
        at = (0, 1, 2) if side == 0 else (LANES - 1, LANES - 2, LANES - 3)
        for d in range(3):
            yaux[side, d : d + 1, :] = turned[0][at[d] : at[d] + 1, :]
        w_hi, w_lo = halves(turned[1][at[0] : at[0] + 1, :])
        yaux[side, 3:4, :] = w_hi.astype(F32)
        yaux[side, 4:5, :] = w_lo.astype(F32)
    for i in range(parts):
        loads[2 + i].wait()
        for k in range(i * K // parts, (i + 1) * K // parts):
            v = p_ref[k * rows : (k + 1) * rows, :].astype(F32)
            for z in range(NZ):
                for h in range(2):
                    pt_ref[h, pl.ds((z * ext + 2) * K + k, X, stride=K), :] = v[z * X : (z + 1) * X, h * LANES : (h + 1) * LANES]
    lane = lanes_of((SUB, LANES))
    for kt in range(K // SUB):
        out = [jnp.zeros((SUB, LANES), F32) for _ in range(4)]
        for z in range(NZ):
            for x in range(X):
                row = (z * ext + 2 + x) * K + kt * SUB
                to = z * GROUP + x + REACH
                here = lane == to
                left, right = pt_ref[0, row : row + SUB, :], pt_ref[1, row : row + SUB, :]
                for i, (tile, col) in enumerate(((left, 0), (left, 1), (right, LANES - 1), (right, LANES - 2))):
                    out[i] = jnp.where(here, pltpu.roll(tile, (to - col) % LANES, 1), out[i])
        for i in range(4):
            edge[i, kt * SUB : (kt + 1) * SUB, :] = out[i]
        own_ref[0, kt * SUB : (kt + 1) * SUB, :] = out[0]
        own_ref[1, kt * SUB : (kt + 1) * SUB, :] = out[2]
    for m, ref in enumerate((y0_ref, y1_ref)):
        side = 1 - odd[1] if m == 0 else odd[1]
        for d in range(2):
            ref[d * K : (d + 1) * K, :] = edge[2 * side + d].astype(BF16)
        ref[2 * K : 2 * K + AUX, :] = yaux[side].astype(BF16)
    for m, ref in enumerate((x0_ref, x1_ref)):
        side = 1 - odd[0] if m == 0 else odd[0]
        for z in range(NZ):
            for i in range(2):
                row = pl.multiple_of((z * ext + 2 + side * (X - 2) + i) * K, SUB)
                for h in range(2):
                    ref[(z * 2 + i) * K : (z * 2 + i + 1) * K, h * LANES : (h + 1) * LANES] = pt_ref[h, pl.ds(row, K), :].astype(BF16)
        aux[...] = jnp.zeros_like(aux)
        for z in range(NZ):
            for d in range(3):
                aux[z * SUB + d : z * SUB + d + 1, :] = cls_ref[pl.ds(z * X + side * (X - 3) + d, 1), :].astype(F32) + 1.0
            w_hi, w_lo = halves(w_ref[pl.ds(z * X + side * (X - 1), 1), :])
            aux[z * SUB + 3 : z * SUB + 4, :] = w_hi.astype(F32)
            aux[z * SUB + 4 : z * SUB + 5, :] = w_lo.astype(F32)
        ref[2 * NZ * K : 2 * NZ * K + NZ * SUB, :] = aux[...].astype(BF16)


def merged(own, from_left, from_right):
    X = GROUP // 2
    m = lanes_of(own.shape) % GROUP
    left = pltpu.roll(from_left, LANES - X, 1)
    right = pltpu.roll(from_right, X, 1)
    out = jnp.where(m < X + REACH, own, jnp.where(m < X + 2 * REACH, right, 0.0))
    return jnp.where(m < REACH, left, out)


def main_kernel(
    K, NZ, X, levels, R,
    table_hbm, ranks_hbm, pt_in, x0_ref, x1_ref, y0_ref, y1_ref, q0_ref, q1_ref, own_ref, cin_ref, win_ref, left_hbm, right_hbm,
    s_ref, v_ref, u_ref, pt_ref, t_ref, cg, wg, rg, cf, hp, ht, ys, fac, table_ref, ranks_ref, sem,
):
    ext, wide = X + 4, X + 2
    KT = K // SUB
    sq = (LANES, LANES)
    lane_sq = lanes_of(sq)
    loads = [pltpu.make_async_copy(ref.at[pl.ds(0, levels)], fac.at[i], sem.at[i]) for i, ref in enumerate((right_hbm, left_hbm))]
    loads.append(pltpu.make_async_copy(table_hbm, table_ref, sem.at[2]))
    loads.append(pltpu.make_async_copy(ranks_hbm, ranks_ref, sem.at[3]))
    for load in loads:
        load.start()
    odd = [lax.rem(lax.axis_index(axis), 2) for axis in ("gx", "gy")]
    for m, ref in enumerate((x0_ref, x1_ref)):
        side = 1 - odd[0] if m == 0 else odd[0]
        for z in range(NZ):
            for i in range(2):
                at = pl.multiple_of((z * ext + i + side * (X + 2)) * K, SUB)
                for h in range(2):
                    cut = (slice((z * 2 + i) * K, (z * 2 + i + 1) * K), slice(h * LANES, (h + 1) * LANES))
                    pt_ref[h, pl.ds(at, K), :] = ref[cut].astype(F32)
    for m, ref in enumerate((y0_ref, y1_ref)):
        ys[0, 1 - odd[1] if m == 0 else odd[1]] = ref[...].astype(F32)
        for n, relay in enumerate((q0_ref, q1_ref)):
            ys[1 + (1 - odd[0] if n == 0 else odd[0]), 1 - odd[1] if m == 0 else odd[1]] = relay[m].astype(F32)
    for h in range(2):
        cg[1 + h] = cin_ref[h]
        wg[1 + h] = win_ref[h]
    for m, ref in enumerate((x0_ref, x1_ref)):
        side = 1 - odd[0] if m == 0 else odd[0]
        x_aux = ref[2 * NZ * K : 2 * NZ * K + NZ * SUB, :].astype(F32)
        for z in range(NZ):
            a = z * SUB
            for h in range(2):
                lo = slice(h * LANES, (h + 1) * LANES)
                for d in range(3):
                    cg[1 + h, pl.ds(z * GROUP + side * (X + REACH) + d, 1), :] = x_aux[a + d : a + d + 1, lo]
                beside = z * GROUP + REACH - 1 + side * (X + 1)
                wg[1 + h, pl.ds(beside, 1), :] = x_aux[a + 3 : a + 4, lo] + x_aux[a + 4 : a + 5, lo]
    spread = jnp.zeros(sq, F32)
    row_sq = lax.broadcasted_iota(jnp.int32, sq, 0)
    spread_w = jnp.zeros(sq, F32)
    for side in range(2):
        rows = merged(*(ys[n, side, 2 * K : 2 * K + AUX, :] for n in range(3)))
        at = (LANES - 1, LANES - 2, LANES - 3) if side == 0 else (0, 1, 2)
        for d in range(3):
            spread = jnp.where(row_sq == at[d], rows[d : d + 1, :], spread)
        spread_w = jnp.where(row_sq == at[0], rows[3:4, :] + rows[4:5, :], spread_w)
    y_class, y_weight = spread.T, spread_w.T
    keep = (lane_sq >= LANES // 2, lane_sq < LANES // 2)
    for side in range(2):
        cg[3 * side] = jnp.where(keep[side], y_class, 0.0)
        wg[3 * side] = jnp.where(keep[side], y_weight, 0.0)
    loads[2].wait()
    loads[3].wait()
    for t in range(4):
        ids = cg[t]
        cond = jnp.zeros(sq, F32)
        for j in range(table_ref.shape[0]):
            cond = jnp.where(ids == float(j + 1), table_ref[j], cond)
        cg[t] = cond

    zeros_g = jnp.zeros((GROUP, LANES), F32)

    def ahead(ref, t):
        nxt = ref[t + 1] if t < 3 else jnp.zeros(sq, F32)
        return jnp.where(lane_sq == LANES - 1, pltpu.roll(nxt, LANES - 1, 1), pltpu.roll(ref[t], LANES - 1, 1))

    def behind(ref, t):
        prv = ref[t - 1] if t > 0 else jnp.zeros(sq, F32)
        return jnp.where(lane_sq == 0, pltpu.roll(prv, 1, 1), pltpu.roll(ref[t], 1, 1))

    def around(ref, t):
        v = ref[t]
        return [
            pltpu.roll(v, LANES - 1, 0),
            pltpu.roll(v, 1, 0),
            ahead(ref, t),
            behind(ref, t),
            jnp.concatenate([v[GROUP:], zeros_g], 0),
            jnp.concatenate([zeros_g, v[:-GROUP]], 0),
        ]

    for t in range(4):
        c = cg[t]
        total = jnp.ones(sq, F32)
        for other in around(cg, t):
            total = total + 0.5 * (c + other)
        rg[t] = 1.0 / total
    picked = jnp.zeros(sq, F32)
    for t in range(4):
        c, r, w = cg[t], rg[t], wg[t]
        pairs = zip(around(cg, t), around(rg, t))
        terms = [r] + [0.5 * (c + c_n) * (r * r_n) for c_n, r_n in pairs]
        for j, term in enumerate(terms):
            if t in (1, 2):
                cf[j, t - 1] = w * term
                cf[7 + j, t - 1] = term
            else:
                to = j if t == 0 else 8 + j
                start = LANES - 1 if t == 0 else 0
                picked = jnp.where(lane_sq == to, pltpu.roll(w * term, (to - start) % LANES, 1), picked)
    edge_cf = picked.T
    for side in range(2):
        p1 = merged(*(ys[n, side, :K, :] for n in range(3)))
        p2 = ys[0, side, K : 2 * K, :]
        p0 = own_ref[side]
        y_next, y_prev = (p0, p2) if side == 0 else (p2, p0)
        parts = [
            p1,
            pltpu.roll(p1, LANES - 1, 1),
            pltpu.roll(p1, 1, 1),
            y_next,
            y_prev,
            pltpu.roll(p1, LANES - GROUP, 1),
            pltpu.roll(p1, GROUP, 1),
        ]
        total = edge_cf[8 * side : 8 * side + 1, :] * parts[0]
        for j in range(1, 7):
            total = total + edge_cf[8 * side + j : 8 * side + j + 1, :] * parts[j]
        hp[side] = p1
        ht[side] = total

    lane = lanes_of((SUB, LANES))
    is_first, is_last = lane == 0, lane == LANES - 1

    def stencil(z, coef_row, first_cf, src, centre_row, x_step, z_step, halo, kt):
        row = pl.multiple_of(centre_row + kt * SUB, SUB)
        c = [src[h, pl.ds(row, SUB), :] for h in range(2)]
        up = [src[h, pl.ds(row + x_step, SUB), :] for h in range(2)]
        down = [src[h, pl.ds(row - x_step, SUB), :] for h in range(2)]
        hl = pltpu.roll(halo[0, kt * SUB : (kt + 1) * SUB, :], LANES - coef_row, 1)
        hr = pltpu.roll(halo[1, kt * SUB : (kt + 1) * SUB, :], LANES - 1 - coef_row, 1)
        fwd = [pltpu.roll(v, LANES - 1, 1) for v in c]
        bwd = [pltpu.roll(v, 1, 1) for v in c]
        nxt = [jnp.where(is_last, fwd[1], fwd[0]), jnp.where(is_last, hr, fwd[1])]
        prv = [jnp.where(is_first, hl, bwd[0]), jnp.where(is_first, bwd[0], bwd[1])]
        out = []
        for h in range(2):
            co = [cf[first_cf + j, h, pl.ds(coef_row, 1), :] for j in range(7)]
            acc = co[0] * c[h] + co[1] * up[h] + co[2] * down[h] + co[3] * nxt[h] + co[4] * prv[h]
            if z < NZ - 1:
                acc = acc + co[5] * src[h, pl.ds(row + z_step, SUB), :]
            if z > 0:
                acc = acc + co[6] * src[h, pl.ds(row - z_step, SUB), :]
            out.append(acc)
        return row, out

    def stage_one(i, carry):
        for z in range(NZ):
            for kt in range(KT):
                _, out = stencil(z, z * GROUP + i + 2, 0, pt_ref, (z * ext + i + 1) * K, K, ext * K, hp, kt)
                to = pl.multiple_of((z * wide + i) * K + kt * SUB, SUB)
                for h in range(2):
                    t_ref[h, pl.ds(to, SUB), :] = out[h]
        return carry

    lax.fori_loop(0, wide, stage_one, 0, unroll=UNROLL_ONE)

    lane_k = lanes_of((K, LANES))
    loads[0].wait()
    loads[1].wait()
    rank = lax.broadcasted_iota(jnp.int32, (R, 1), 0)
    terms = []
    for l in range(levels):
        scale = float(2 * LANES * 2**l) ** -0.5
        terms.append(jnp.where(rank < ranks_ref[l], fac[0, l] * scale, 0.0))
    terms += [fac[1, l] for l in range(levels)]
    factor = jnp.concatenate(terms, 0).astype(BF16)

    def stage_two(i, carry):
        places = [[jnp.zeros((K, LANES), F32) for _ in range(levels)] for _ in range(2)]
        for half in range(2):
            x = 2 * i + half
            his = []
            for z in range(NZ):
                lines = []
                for kt in range(KT):
                    _, out = stencil(z, z * GROUP + x + REACH, 7, t_ref, (z * wide + x + 1) * K, K, wide * K, ht, kt)
                    row = pl.multiple_of((z * ext + x + 2) * K + kt * SUB, SUB)
                    to = pl.multiple_of((z * X + x) * K + kt * SUB, SUB)
                    both = []
                    for h in range(2):
                        s = out[h] + pt_ref[h, pl.ds(row, SUB), :]
                        s_ref[h, pl.ds(to, SUB), :] = s
                        both.append(s)
                    lines.append(jnp.concatenate(both, 1))
                his.append(jnp.concatenate(lines, 0).astype(BF16))
            coef = nt(jnp.concatenate(his, 0), factor)
            if coef.shape[1] < LANES:
                coef = jnp.concatenate([coef, jnp.zeros((NZ * K, LANES - coef.shape[1]), F32)], 1)
            for z in range(NZ):
                part = coef[z * K : (z + 1) * K]
                at = half * NZ * R + z * R
                here = (lane_k >= at) & (lane_k < at + R)
                for q in range(2):
                    for l in range(levels):
                        moved = pltpu.roll(part, (at - (q * levels + l) * R) % LANES, 1)
                        places[q][l] = jnp.where(here, moved, places[q][l])
        for l in range(levels):
            v_ref[l, i] = places[0][l].astype(BF16)
            u_ref[l, i] = places[1][l].astype(BF16)
        return carry

    lax.fori_loop(0, X // 2, stage_two, 0, unroll=UNROLL_TWO)


def gram_kernel(K, first, count, s_ref, block_ref, gx_ref):
    leaf_matrix = block_ref[...].astype(BF16)

    def chunk(i, carry):
        gram, mixed = carry
        his = []
        for n in range(NLINES):
            at = pl.multiple_of((first + i * NLINES + n) * K, SUB)
            hi, lo = halves(jnp.concatenate([s_ref[h, pl.ds(at, K), :] for h in range(2)], 1))
            gram = gram + nt(hi, jnp.concatenate([hi, lo], 0))
            his.append(hi)
        leaf = nt(jnp.concatenate(his, 0), leaf_matrix).astype(BF16)
        for n in range(NLINES):
            mixed = mixed + nt(his[n], leaf[n * K : (n + 1) * K])
        return gram, mixed

    init = (jnp.zeros((K, 2 * K), F32), jnp.zeros((K, K), F32))
    gram, mixed = lax.fori_loop(0, count // NLINES, chunk, init, unroll=UNROLL_GRAM)
    low = gram[:, K:]
    gx_ref[...] = jnp.zeros_like(gx_ref)
    gx_ref[:, :K] = gram[:, :K] + low + low.T
    gx_ref[:, LANES // 2 : LANES // 2 + K] = mixed


def couple_kernel(K, parts, u_ref, *refs):
    gx_refs, sib_refs, out_ref = refs[:parts], refs[parts:-1], refs[-1]
    total = jnp.zeros((K, K), F32)
    for l, ref in enumerate(sib_refs):
        for i in range(u_ref.shape[1]):
            total = total + nt(u_ref[l, i], ref[i])
    out_ref[...] = sum(ref[...] for ref in gx_refs)
    at = LANES // 2
    out_ref[:, at : at + K] = out_ref[:, at : at + K] + total


def finish_kernel(K, NZ, X, cells, gx_ref, s_ref, basis_ref, proj_ref, out, sem):
    lane = lanes_of((K, LANES))
    row = lax.broadcasted_iota(jnp.int32, (K, LANES), 0)
    half = LANES // 2
    gx = gx_ref[...] * (1.0 / cells)
    gram = gx[:, :K]
    mixed = gram + gx[:, half : half + K]
    aug = jnp.where(lane < K, gx, jnp.where(lane - half == row, 1.0, 0.0))
    for j in range(K - 1):
        pivot_row = aug[j : j + 1, :]
        factor = aug[:, j : j + 1] * (1.0 / aug[j : j + 1, j : j + 1])
        aug = aug - jnp.where(row > j, factor, 0.0) * pivot_row
    pivots = jnp.sum(jnp.where(lane == row, aug, 0.0), axis=1, keepdims=True)
    inverse = aug[:, half : half + K] * lax.rsqrt(pivots)
    left = jnp.dot(inverse, mixed, precision=HIGH, preferred_element_type=F32)
    proj_ref[...] = nt(left, inverse, precision=HIGH)
    i_hi, i_lo = halves(inverse)
    lhs = jnp.concatenate([i_hi, i_lo, i_hi], 1)
    W = 2 * LANES
    copies = []
    for z in range(NZ):

        def line(x, carry, z=z):
            at = pl.multiple_of((z * X + x) * K, SUB)
            s = jnp.concatenate([s_ref[h, pl.ds(at, K), :] for h in range(2)], 1)
            hi, lo = halves(s)
            b = jnp.dot(lhs, jnp.concatenate([hi, hi, lo], 0), preferred_element_type=F32)
            for h in range(2):
                out[h, z, pl.ds(x, K, stride=X), :] = b[:, h * LANES : (h + 1) * LANES]
            return carry

        lax.fori_loop(0, X, line, 0, unroll=True)
        for h in range(2):
            for part in range(1):
                copies.append(
                    pltpu.make_async_copy(
                        out.at[h, z].reshape(K, X, LANES), basis_ref.at[:, z, :, pl.ds(h * LANES, LANES)], sem.at[z, h]
                    )
                )
                copies[-1].start()
    for c in copies:
        c.wait()


def in_hbm(v):
    return pltpu.with_memory_space_constraint(v, pltpu.HBM)


def exchanged(v, axis, bits):
    return lax.ppermute(v, axis, [(i, i ^ bits) for i in range(lax.axis_size(axis))])


def paired(v, axis, first):
    n = lax.axis_size(axis)
    swaps = [(i, i + 1) for i in range(first, n - 1, 2)]
    return lax.ppermute(v, axis, swaps + [(j, i) for i, j in swaps])


def summed(v):
    for axis in AXES:
        bit = 1
        while bit < lax.axis_size(axis):
            v = v + exchanged(v, axis, bit)
            bit *= 2
    return v


def shards(probes, classes, class_table, weights, prior_block, prior_left, prior_right, block_ranks):
    K, NZ, X, W = probes.shape
    R = prior_left.shape[1]
    levels = lax.axis_size("gy").bit_length() - 1
    cells = float(NZ * X * W * lax.axis_size("gx") * lax.axis_size("gy"))
    rows, ext, wide = NZ * X, X + 4, X + 2
    shape = jax.ShapeDtypeStruct
    cls2, w2 = classes.reshape(rows, W), weights.reshape(rows, W)
    params = functools.partial(pltpu.CompilerParams, vmem_limit_bytes=32 << 20)
    y_rows, x_rows = 2 * K + AUX, 2 * NZ * K + NZ * SUB
    square = (LANES, LANES)
    pt, cg, wg, own, y0, y1, x0, x1 = pl.pallas_call(
        functools.partial(pack_kernel, K, NZ, X),
        out_shape=(
            shape((2, NZ * ext * K, LANES), F32),
            shape((2, *square), F32),
            shape((2, *square), F32),
            shape((2, K, LANES), F32),
            shape((y_rows, LANES), BF16),
            shape((y_rows, LANES), BF16),
            shape((x_rows, W), BF16),
            shape((x_rows, W), BF16),
        ),
        in_specs=[HBM] * 3,
        out_specs=(VMEM,) * 8,
        scratch_shapes=[
            pltpu.VMEM((K * rows, W), BF16),
            pltpu.VMEM((rows, W), jnp.int32),
            pltpu.VMEM((rows, W), F32),
            pltpu.VMEM((4, K, LANES), F32),
            pltpu.VMEM((NZ * SUB, W), F32),
            pltpu.VMEM((2, AUX, LANES), F32),
            pltpu.SemaphoreType.DMA((6,)),
        ],
        compiler_params=params(),
        name="pack",
    )(in_hbm(probes.reshape(K * rows, W)), in_hbm(cls2), in_hbm(w2))
    y0, y1 = paired(y0, "gy", 0), paired(y1, "gy", 1)
    x0, x1 = paired(x0, "gx", 0), paired(x1, "gx", 1)
    both = jnp.stack([y0, y1])
    q0, q1 = paired(both, "gx", 0), paired(both, "gx", 1)
    slab = (2, rows * K, LANES)
    side = (levels, X // 2, K, LANES)
    s, v, u, _ = pl.pallas_call(
        functools.partial(main_kernel, K, NZ, X, levels, R),
        out_shape=(shape(slab, F32), shape(side, BF16), shape(side, BF16), shape(pt.shape, F32)),
        in_specs=[HBM] * 2 + [VMEM] * 10 + [HBM] * 2,
        out_specs=(VMEM,) * 4,
        scratch_shapes=[
            pltpu.VMEM((2, NZ * wide * K, LANES), F32),
            pltpu.VMEM((4, *square), F32),
            pltpu.VMEM((4, *square), F32),
            pltpu.VMEM((4, *square), F32),
            pltpu.VMEM((14, 2, *square), F32),
            pltpu.VMEM((2, K, LANES), F32),
            pltpu.VMEM((2, K, LANES), F32),
            pltpu.VMEM((3, 2, y_rows, LANES), F32),
            pltpu.VMEM((2, levels, R, W), F32),
            pltpu.SMEM(class_table.shape, F32),
            pltpu.SMEM(block_ranks.shape, jnp.int32),
            pltpu.SemaphoreType.DMA((4,)),
        ],
        input_output_aliases={2: 3},
        compiler_params=params(),
        name="sketch",
    )(in_hbm(class_table), in_hbm(block_ranks), pt, x0, x1, y0, y1, q0, q1, own, cg, wg, in_hbm(prior_left), in_hbm(prior_right))
    share = rows // GRAM_PARTS
    parts = []
    for i in range(GRAM_PARTS):
        parts.append(
            pl.pallas_call(
                functools.partial(gram_kernel, K, i * share, share),
                out_shape=shape((K, LANES), F32),
                in_specs=[VMEM] * 2,
                out_specs=VMEM,
                cost_estimate=pl.CostEstimate(flops=2 * 300 * K * share * W, bytes_accessed=8 << 20, transcendentals=0),
                compiler_params=params(),
                name=f"gram_{i}",
            )(s, prior_block)
        )
    sibs = []
    pending = v
    for l in range(levels):
        got = exchanged(pending, "gy", 2**l)
        sibs.append(got[0])
        pending = (pending[1:].astype(F32) + got[1:].astype(F32)).astype(BF16)
    gx = pl.pallas_call(
        functools.partial(couple_kernel, K, GRAM_PARTS),
        out_shape=shape((K, LANES), F32),
        in_specs=[VMEM] * (1 + GRAM_PARTS + levels),
        out_specs=VMEM,
        compiler_params=params(),
        name="couple",
    )(u, *parts, *sibs)
    gx = summed(gx)
    basis, projected = pl.pallas_call(
        functools.partial(finish_kernel, K, NZ, X, cells),
        out_shape=(shape((K, NZ, X, W), F32), shape((K, K), F32)),
        in_specs=[VMEM] * 2,
        out_specs=(HBM, VMEM),
        scratch_shapes=[pltpu.VMEM((2, NZ, K * X, LANES), F32), pltpu.SemaphoreType.DMA((NZ, 2))],
        compiler_params=params(),
        name="finish",
    )(gx, s)
    return basis, projected


def solution(mesh):
    return jax.shard_map(
        shards,
        mesh=mesh,
        in_specs=(
            P(None, None, "gx", "gy"),
            P(None, "gx", "gy"),
            P(),
            P(None, "gx", "gy"),
            P("gy", None),
            P(None, None, "gy"),
            P(None, None, "gy"),
            P(),
        ),
        out_specs=(P(None, None, "gx", "gy"), P()),
        check_vma=False,
    )
```

time: 87.3 us -> 69.2 us (0.79)
  local copies, waits for them, and re-layouts: 5.36 us -> 0.01 us
  starting transfers between devices: 31.3 us -> 26.7 us
  Pallas kernels: 30.6 us -> 26.7 us
  other arithmetic: 2.58 us -> 0.06 us
  waiting for transfers between devices: 16.1 us -> 14.8 us
    pallas_call x1, Pallas kernels: 16 us -> 7.41 us  [shards(): pl.pallas_call(functools.partial(finish_kernel, K, NZ, X, cells), out_sha...]
    ppermute x6, starting transfers between devices: 15.7 us -> 10.7 us  [paired(): return lax.ppermute(v, axis, swaps + [(j, i) for i, j in swaps])]
    unnamed x10 -> x2, local copies, waits for them, and re-layouts: 4.57 us -> 0.01 us
    pallas_call x1 -> x3, Pallas kernels: 0.31 us -> 3.71 us  [the longest x2 3.42 us: shards(): pl.pallas_call(functools.partial(gram_kernel, K, i * share, share), out_s...]
    pallas_call x1, Pallas kernels: 1.74 us -> 4.27 us  [shards(): pl.pallas_call(functools.partial(pack_kernel, K, NZ, X), out_shape=(shape...]
    ppermute x8 -> x7, waiting for transfers between devices: 13.9 us -> 12.1 us  [exchanged(): lax.ppermute(v, axis, [(i, i ^ bits) for i in range(lax.axis_size(axis))])]
    pallas_call x1, Pallas kernels: 12.6 us -> 11.3 us  [shards(): pl.pallas_call(functools.partial(main_kernel, K, NZ, X, levels, R), out_s...]
    convert_element_type x1, other arithmetic: 0.96 us -> 0.03 us  [shards(): pending = (pending[1:].astype(F32) + got[1:].astype(F32)).astype(BF16)]
  transfers between devices with their start and end apart: 14 -> 13, of which waited for: 9 -> 8; matrix products, arithmetic and copies ran while one was open for 4% -> 0% of each run, Pallas kernels for 0% -> 5%
where the time goes in v1:
time: 69.2 us; the launch traced here: 69 us
  Pallas kernels  26.7 us (39%)
  starting transfers between devices  26.7 us (39%)
  waiting for transfers between devices  14.8 us (21%)
  between operations  0.74 us (1%)
    ppermute x7, starting transfers between devices, exchanged(): lax.ppermute(v, axis, [(i, i ^ bits) for i in range(lax.axis_size(axis))])  16 us
    ppermute x7, waiting for transfers between devices, exchanged(): lax.ppermute(v, axis, [(i, i ^ bits) for i in range(lax.axis_size(axis))])  12.1 us
    pallas_call x1, Pallas kernels, shards(): pl.pallas_call(functools.partial(main_kernel, K, NZ, X, levels, R), out_s...  11.3 us
    ppermute x6, starting transfers between devices, paired(): return lax.ppermute(v, axis, swaps + [(j, i) for i, j in swaps])  10.7 us
    pallas_call x1, Pallas kernels, shards(): pl.pallas_call(functools.partial(finish_kernel, K, NZ, X, cells), out_sha...  7.41 us
    pallas_call x1, Pallas kernels, shards(): pl.pallas_call(functools.partial(pack_kernel, K, NZ, X), out_shape=(shape...  4.27 us
    pallas_call x2, Pallas kernels, shards(): pl.pallas_call(functools.partial(gram_kernel, K, i * share, share), out_s...  3.42 us
    ppermute x6, waiting for transfers between devices, paired(): return lax.ppermute(v, axis, swaps + [(j, i) for i, j in swaps])  2.68 us
  transfers between devices with their start and end apart: 13, of which 8 were waited for; matrix products, arithmetic and copies ran while one was open for 0% of the time, Pallas kernels for 5%

profile of v1, /device:TPU:0, one launch (start us, length us, event | category | flops | bytes accessed | tf_op | source)
XLA Modules:
  0.0 69.0 jit_solution(386304820973624011)
XLA Ops:
  0.6 4.3 %pack.1 = (f32[2,3840,128]{2,1,0:T(8,128)S(1)}, f32[2,128,128]{2,1,0:T(8,128)S(1)}, f32[2,128,128]{2,1,0:T(8,128)S(1)}, f32[2,48,128]{2,1,0:T(8,128)S(1)}, bf16[...) custom-call(bf16[3072,256]{1,0:T(8,128)(2,1)} %bitcast.11, ...), custom_call_target="tpu_custom_call" | custom-call | tf_op jit(solution)/shard_map/pack/pallas_call | solution.py:447
  4.9 3.0 %collective-permute-start = (bf16[416,256]{1,0:T(8,128)(2,1)S(1)}, bf16[416,256]{1,0:T(8,128)(2,1)S(1)}, u32[]{:S(2)}, u32[]{:S(2)}) collective-permute-start(bf16[416,256]{1,0:T(8,128)(2,1)S(1)} %get-tuple-element.14), channel_id=1, source_target_pairs={{0,4},{8,12},{16,20},{24,28},{4,0},{12,8},{20,16},{28,24},{1,5},{9... | collective-permute-start | bytes 638984 | tf_op jit(solution)/shard_map/ppermute | solution.py:424
  8.0 0.7 collective-permute-start.1
  8.7 0.7 collective-permute-start.3
  9.4 0.5 collective-permute-done.2.y0_ref
  9.9 0.7 collective-permute-start.5
  10.6 5.6 %collective-permute-start.4 = (bf16[2,112,128]{2,1,0:T(8,128)(2,1)S(1)}, bf16[2,112,128]{2,1,0:T(8,128)(2,1)S(1)}, u32[]{:S(2)}, u32[]{:S(2)}) collective-permute-start(bf16[2,112,128]{2,1,0:T(8,128)(2,1)S(1)} %pad_maximum_fusion), channel_id=1, source_target_pairs={{0,4},{8,12},{16,20},{24,28},{4,0},{12,8},{20,16},{28,24},{1,5},{9... | collective-permute-start | bytes 172040 | tf_op jit(solution)/shard_map/ppermute | solution.py:424
  16.2 2.2 %collective-permute-done.4.q0_ref = bf16[2,112,128]{2,1,0:T(8,128)(2,1)S(1)} collective-permute-done((bf16[2,112,128]{2,1,0:T(8,128)(2,1)S(1)}, bf16[2,112,128]{2,1,0:T(8,128)(2,1)S(1)}, u32[]{:S(2)}, u32[]{:S(2)}) %collective-permute-start.4) | collective-permute-done | bytes 57376 | tf_op jit(solution)/shard_map/ppermute | solution.py:424
  18.3 11.3 %sketch.1 = (f32[2,3072,128]{2,1,0:T(8,128)S(1)}, bf16[2,8,48,128]{3,2,1,0:T(8,128)(2,1)S(1)}, bf16[2,8,48,128]{3,2,1,0:T(8,128)(2,1)S(1)}, f32[2,3840,128]{2,1,0:T(8,128)S(1)}) custom-call(f32[8]{0:T(128)} %table_hbm.1, s32[8]{0:T(128)} %ranks_hbm.1, f32[2,3840,128]{2,1,0:T(8,128)S(1)} %get-tuple-element.13.pt_in, ...), custom_call_target="tpu_custom_call", output_to_operand_aliasing={{3}: (2, {})} | custom-call | tf_op jit(solution)/shard_map/sketch/pallas_call | solution.py:479
  29.6 4.0 %collective-permute-start.6 = (bf16[2,8,48,128]{3,2,1,0:T(8,128)(2,1)S(1)}, bf16[2,8,48,128]{3,2,1,0:T(8,128)(2,1)S(1)}, u32[]{:S(2)}, u32[]{:S(2)}) collective-permute-start(bf16[2,8,48,128]{3,2,1,0:T(8,128)(2,1)S(1)} %get-tuple-element.23), channel_id=1, source_target_pairs={{0,1},{1,0},{2,3},{3,2},{4,5},{5,4},{6,7},{7,6},{8,9},{9,8},{10,11... | collective-permute-start | bytes 589832 | tf_op jit(solution)/shard_map/ppermute | solution.py:418
  33.6 1.7 %gram_1.1.refs_1_ = f32[48,128]{1,0:T(8,128)S(1)} custom-call(f32[2,3072,128]{2,1,0:T(8,128)S(1)} %get-tuple-element.22.s_ref, f32[256,256]{1,0:T(8,128)S(1)} %copy-done), custom_call_target="tpu_custom_call" | custom-call | flops 235929600 | bytes 8388608 | tf_op jit(solution)/shard_map/gram_1/pallas_call | solution.py:506
  35.3 1.7 %gram_0.1.refs_0_ = f32[48,128]{1,0:T(8,128)S(1)} custom-call(f32[2,3072,128]{2,1,0:T(8,128)S(1)} %get-tuple-element.22.s_ref, f32[256,256]{1,0:T(8,128)S(1)} %copy-done), custom_call_target="tpu_custom_call" | custom-call | flops 235929600 | bytes 8388608 | tf_op jit(solution)/shard_map/gram_0/pallas_call | solution.py:506
  37.1 2.1 %collective-permute-start.7 = (bf16[1,8,48,128]{3,2,1,0:T(8,128)(2,1)S(1)}, bf16[1,8,48,128]{3,2,1,0:T(8,128)(2,1)S(1)}, u32[]{:S(2)}, u32[]{:S(2)}) collective-permute-start(bf16[1,8,48,128]{3,2,1,0:T(8,128)(2,1)S(1)} %add_convert_fusion), channel_id=1, source_target_pairs={{0,2},{1,3},{2,0},{3,1},{4,6},{5,7},{6,4},{7,5},{8,10},{9,11},{10,... | collective-permute-start | bytes 294920 | tf_op jit(solution)/shard_map/ppermute | solution.py:418
  39.2 3.4 %collective-permute-done.7 = bf16[1,8,48,128]{3,2,1,0:T(8,128)(2,1)S(1)} collective-permute-done((bf16[1,8,48,128]{3,2,1,0:T(8,128)(2,1)S(1)}, bf16[1,8,48,128]{3,2,1,0:T(8,128)(2,1)S(1)}, u32[]{:S(2)}, u32[]{:S(2)}) %collective-permute-start.7) | collective-permute-done | bytes 98336 | tf_op jit(solution)/shard_map/ppermute | solution.py:418
  43.0 1.2 %collective-permute-done.8 = f32[48,128]{1,0:T(8,128)S(1)} collective-permute-done((f32[48,128]{1,0:T(8,128)S(1)}, f32[48,128]{1,0:T(8,128)S(1)}, u32[]{:S(2)}, u32[]{:S(2)}) %collective-permute-start.8) | collective-permute-done | bytes 24608 | tf_op jit(solution)/shard_map/ppermute | solution.py:418
  44.2 1.7 %collective-permute-start.9 = (f32[48,128]{1,0:T(8,128)S(1)}, f32[48,128]{1,0:T(8,128)S(1)}, u32[]{:S(2)}, u32[]{:S(2)}) collective-permute-start(f32[48,128]{1,0:T(8,128)S(1)} %add.19), channel_id=1, source_target_pairs={{0,2},{1,3},{2,0},{3,1},{4,6},{5,7},{6,4},{7,5},{8,10},{9,11},{10,... | collective-permute-start | bytes 73736 | tf_op jit(solution)/shard_map/ppermute | solution.py:418
  46.0 2.1 %collective-permute-done.9 = f32[48,128]{1,0:T(8,128)S(1)} collective-permute-done((f32[48,128]{1,0:T(8,128)S(1)}, f32[48,128]{1,0:T(8,128)S(1)}, u32[]{:S(2)}, u32[]{:S(2)}) %collective-permute-start.9) | collective-permute-done | bytes 24608 | tf_op jit(solution)/shard_map/ppermute | solution.py:418
  48.0 2.6 %collective-permute-start.10 = (f32[48,128]{1,0:T(8,128)S(1)}, f32[48,128]{1,0:T(8,128)S(1)}, u32[]{:S(2)}, u32[]{:S(2)}) collective-permute-start(f32[48,128]{1,0:T(8,128)S(1)} %add.20), channel_id=1, source_target_pairs={{0,4},{4,0},{8,12},{12,8},{16,20},{20,16},{24,28},{28,24},{1,5},{5... | collective-permute-start | bytes 73736 | tf_op jit(solution)/shard_map/ppermute | solution.py:418
  50.7 1.8 %collective-permute-done.10 = f32[48,128]{1,0:T(8,128)S(1)} collective-permute-done((f32[48,128]{1,0:T(8,128)S(1)}, f32[48,128]{1,0:T(8,128)S(1)}, u32[]{:S(2)}, u32[]{:S(2)}) %collective-permute-start.10) | collective-permute-done | bytes 24608 | tf_op jit(solution)/shard_map/ppermute | solution.py:418
  52.5 2.5 %collective-permute-start.11 = (f32[48,128]{1,0:T(8,128)S(1)}, f32[48,128]{1,0:T(8,128)S(1)}, u32[]{:S(2)}, u32[]{:S(2)}) collective-permute-start(f32[48,128]{1,0:T(8,128)S(1)} %add.21), channel_id=1, source_target_pairs={{0,8},{4,12},{8,0},{12,4},{16,24},{20,28},{24,16},{28,20},{1,9},{5... | collective-permute-start | bytes 73736 | tf_op jit(solution)/shard_map/ppermute | solution.py:418
  54.9 1.8 %collective-permute-done.11 = f32[48,128]{1,0:T(8,128)S(1)} collective-permute-done((f32[48,128]{1,0:T(8,128)S(1)}, f32[48,128]{1,0:T(8,128)S(1)}, u32[]{:S(2)}, u32[]{:S(2)}) %collective-permute-start.11) | collective-permute-done | bytes 24608 | tf_op jit(solution)/shard_map/ppermute | solution.py:418
  56.7 3.0 %collective-permute-start.12 = (f32[48,128]{1,0:T(8,128)S(1)}, f32[48,128]{1,0:T(8,128)S(1)}, u32[]{:S(2)}, u32[]{:S(2)}) collective-permute-start(f32[48,128]{1,0:T(8,128)S(1)} %add.22), channel_id=1, source_target_pairs={{0,16},{4,20},{8,24},{12,28},{16,0},{20,4},{24,8},{28,12},{1,17},{... | collective-permute-start | bytes 73736 | tf_op jit(solution)/shard_map/ppermute | solution.py:418
  59.8 1.8 %collective-permute-done.12 = f32[48,128]{1,0:T(8,128)S(1)} collective-permute-done((f32[48,128]{1,0:T(8,128)S(1)}, f32[48,128]{1,0:T(8,128)S(1)}, u32[]{:S(2)}, u32[]{:S(2)}) %collective-permute-start.12) | collective-permute-done | bytes 24608 | tf_op jit(solution)/shard_map/ppermute | solution.py:418
  61.6 7.4 %finish.1 = (f32[48,4,16,256]{3,2,1,0:T(8,128)}, f32[48,48]{1,0:T(8,128)}) custom-call(f32[48,128]{1,0:T(8,128)S(1)} %add.23.gx_ref, f32[2,3072,128]{2,1,0:T(8,128)S(1)} %get-tuple-element.22.s_ref), custom_call_target="tpu_custom_call" | custom-call | tf_op jit(solution)/shard_map/finish/pallas_call | solution.py:531
  (18 shorter events, 0.5 us)
Async XLA Ops:
  0.6 33.0 %copy-start = (f32[256,256]{1,0:T(8,128)S(1)}, f32[256,256]{1,0:T(8,128)}, u32[]{:S(2)}) copy-start(f32[256,256]{1,0:T(8,128)} %block_ref.3) | copy-start | bytes 786436
  4.9 13.4 %collective-permute-start = (bf16[416,256]{1,0:T(8,128)(2,1)S(1)}, bf16[416,256]{1,0:T(8,128)(2,1)S(1)}, u32[]{:S(2)}, u32[]{:S(2)}) collective-permute-start(bf16[416,256]{1,0:T(8,128)(2,1)S(1)} %get-tuple-element.14), channel_id=1, source_target_pairs={{0,4},{8,12},{16,20},{24,28},{4,0},{12,8},{20,16},{28,24},{1,5},{9... | collective-permute-start | bytes 638984 | tf_op jit(solution)/shard_map/ppermute | solution.py:424
  8.0 10.4 %collective-permute-start.1 = (bf16[416,256]{1,0:T(8,128)(2,1)S(1)}, bf16[416,256]{1,0:T(8,128)(2,1)S(1)}, u32[]{:S(2)}, u32[]{:S(2)}) collective-permute-start(bf16[416,256]{1,0:T(8,128)(2,1)S(1)} %get-tuple-element.15), channel_id=1, source_target_pairs={{4,8},{12,16},{20,24},{8,4},{16,12},{24,20},{5,9},{13,17},{21,25},... | collective-permute-start | bytes 638984 | tf_op jit(solution)/shard_map/ppermute | solution.py:424
  8.6 1.3 %collective-permute-start.2 = (bf16[112,128]{1,0:T(8,128)(2,1)S(1)}, bf16[112,128]{1,0:T(8,128)(2,1)S(1)}, u32[]{:S(2)}, u32[]{:S(2)}) collective-permute-start(bf16[112,128]{1,0:T(8,128)(2,1)S(1)} %get-tuple-element.16), channel_id=1, source_target_pairs={{0,1},{2,3},{1,0},{3,2},{4,5},{6,7},{5,4},{7,6},{8,9},{10,11},{9,8... | collective-permute-start | bytes 86024 | tf_op jit(solution)/shard_map/ppermute | solution.py:424
  8.7 1.2 %collective-permute-start.3 = (bf16[112,128]{1,0:T(8,128)(2,1)S(1)}, bf16[112,128]{1,0:T(8,128)(2,1)S(1)}, u32[]{:S(2)}, u32[]{:S(2)}) collective-permute-start(bf16[112,128]{1,0:T(8,128)(2,1)S(1)} %get-tuple-element.17), channel_id=1, source_target_pairs={{1,2},{2,1},{5,6},{6,5},{9,10},{10,9},{13,14},{14,13},{17,18},{18,... | collective-permute-start | bytes 86024 | tf_op jit(solution)/shard_map/ppermute | solution.py:424
  9.9 6.3 %collective-permute-start.5 = (bf16[2,112,128]{2,1,0:T(8,128)(2,1)S(1)}, bf16[2,112,128]{2,1,0:T(8,128)(2,1)S(1)}, u32[]{:S(2)}, u32[]{:S(2)}) collective-permute-start(bf16[2,112,128]{2,1,0:T(8,128)(2,1)S(1)} %pad_maximum_fusion), channel_id=1, source_target_pairs={{4,8},{12,16},{20,24},{8,4},{16,12},{24,20},{5,9},{13,17},{21,25},... | collective-permute-start | bytes 172040 | tf_op jit(solution)/shard_map/ppermute | solution.py:424
  10.6 7.8 %collective-permute-start.4 = (bf16[2,112,128]{2,1,0:T(8,128)(2,1)S(1)}, bf16[2,112,128]{2,1,0:T(8,128)(2,1)S(1)}, u32[]{:S(2)}, u32[]{:S(2)}) collective-permute-start(bf16[2,112,128]{2,1,0:T(8,128)(2,1)S(1)} %pad_maximum_fusion), channel_id=1, source_target_pairs={{0,4},{8,12},{16,20},{24,28},{4,0},{12,8},{20,16},{28,24},{1,5},{9... | collective-permute-start | bytes 172040 | tf_op jit(solution)/shard_map/ppermute | solution.py:424
  29.6 7.4 %collective-permute-start.6 = (bf16[2,8,48,128]{3,2,1,0:T(8,128)(2,1)S(1)}, bf16[2,8,48,128]{3,2,1,0:T(8,128)(2,1)S(1)}, u32[]{:S(2)}, u32[]{:S(2)}) collective-permute-start(bf16[2,8,48,128]{3,2,1,0:T(8,128)(2,1)S(1)} %get-tuple-element.23), channel_id=1, source_target_pairs={{0,1},{1,0},{2,3},{3,2},{4,5},{5,4},{6,7},{7,6},{8,9},{9,8},{10,11... | collective-permute-start | bytes 589832 | tf_op jit(solution)/shard_map/ppermute | solution.py:418
  37.1 5.6 %collective-permute-start.7 = (bf16[1,8,48,128]{3,2,1,0:T(8,128)(2,1)S(1)}, bf16[1,8,48,128]{3,2,1,0:T(8,128)(2,1)S(1)}, u32[]{:S(2)}, u32[]{:S(2)}) collective-permute-start(bf16[1,8,48,128]{3,2,1,0:T(8,128)(2,1)S(1)} %add_convert_fusion), channel_id=1, source_target_pairs={{0,2},{1,3},{2,0},{3,1},{4,6},{5,7},{6,4},{7,5},{8,10},{9,11},{10,... | collective-permute-start | bytes 294920 | tf_op jit(solution)/shard_map/ppermute | solution.py:418
  42.9 1.3 %collective-permute-start.8 = (f32[48,128]{1,0:T(8,128)S(1)}, f32[48,128]{1,0:T(8,128)S(1)}, u32[]{:S(2)}, u32[]{:S(2)}) collective-permute-start(f32[48,128]{1,0:T(8,128)S(1)} %couple.1), channel_id=1, source_target_pairs={{0,1},{1,0},{2,3},{3,2},{4,5},{5,4},{6,7},{7,6},{8,9},{9,8},{10,11... | collective-permute-start | bytes 73736 | tf_op jit(solution)/shard_map/ppermute | solution.py:418
  44.2 3.8 %collective-permute-start.9 = (f32[48,128]{1,0:T(8,128)S(1)}, f32[48,128]{1,0:T(8,128)S(1)}, u32[]{:S(2)}, u32[]{:S(2)}) collective-permute-start(f32[48,128]{1,0:T(8,128)S(1)} %add.19), channel_id=1, source_target_pairs={{0,2},{1,3},{2,0},{3,1},{4,6},{5,7},{6,4},{7,5},{8,10},{9,11},{10,... | collective-permute-start | bytes 73736 | tf_op jit(solution)/shard_map/ppermute | solution.py:418
  48.0 4.4 %collective-permute-start.10 = (f32[48,128]{1,0:T(8,128)S(1)}, f32[48,128]{1,0:T(8,128)S(1)}, u32[]{:S(2)}, u32[]{:S(2)}) collective-permute-start(f32[48,128]{1,0:T(8,128)S(1)} %add.20), channel_id=1, source_target_pairs={{0,4},{4,0},{8,12},{12,8},{16,20},{20,16},{24,28},{28,24},{1,5},{5... | collective-permute-start | bytes 73736 | tf_op jit(solution)/shard_map/ppermute | solution.py:418
  52.5 4.3 %collective-permute-start.11 = (f32[48,128]{1,0:T(8,128)S(1)}, f32[48,128]{1,0:T(8,128)S(1)}, u32[]{:S(2)}, u32[]{:S(2)}) collective-permute-start(f32[48,128]{1,0:T(8,128)S(1)} %add.21), channel_id=1, source_target_pairs={{0,8},{4,12},{8,0},{12,4},{16,24},{20,28},{24,16},{28,20},{1,9},{5... | collective-permute-start | bytes 73736 | tf_op jit(solution)/shard_map/ppermute | solution.py:418
  56.7 4.8 %collective-permute-start.12 = (f32[48,128]{1,0:T(8,128)S(1)}, f32[48,128]{1,0:T(8,128)S(1)}, u32[]{:S(2)}, u32[]{:S(2)}) collective-permute-start(f32[48,128]{1,0:T(8,128)S(1)} %add.22), channel_id=1, source_target_pairs={{0,16},{4,20},{8,24},{12,28},{16,0},{20,4},{24,8},{28,12},{1,17},{... | collective-permute-start | bytes 73736 | tf_op jit(solution)/shard_map/ppermute | solution.py:418

commit v2 on v1

--- a/solution.py
+++ b/solution.py
@@ -37,7 +37,7 @@
     return lax.dot_general(a, b, (((1,), (1,)), ((), ())), precision=precision, preferred_element_type=F32)
 
 
-def pack_kernel(K, NZ, X, p_hbm, cls_hbm, w_hbm, pt_ref, cg_ref, wg_ref, own_ref, y0_ref, y1_ref, x0_ref, x1_ref, p_ref, cls_ref, w_ref, edge, aux, yaux, sem):
+def pack_kernel(K, NZ, X, p_hbm, cls_hbm, w_hbm, pt_ref, cg_ref, wg_ref, own_ref, y0_ref, y1_ref, p_ref, cls_ref, w_ref, edge, yaux, sem):
     rows, ext = NZ * X, X + 4
     parts = 4
     step = K * rows // parts
@@ -48,7 +48,7 @@
         load.start()
     loads[0].wait()
     loads[1].wait()
-    odd = [lax.rem(lax.axis_index(axis), 2) for axis in ("gx", "gy")]
+    odd = lax.rem(lax.axis_index("gy"), 2)
     turned = []
     for source, grid in ((cls_ref, cg_ref), (w_ref, wg_ref)):
         for h in range(2):
@@ -92,25 +92,120 @@
         own_ref[0, kt * SUB : (kt + 1) * SUB, :] = out[0]
         own_ref[1, kt * SUB : (kt + 1) * SUB, :] = out[2]
     for m, ref in enumerate((y0_ref, y1_ref)):
-        side = 1 - odd[1] if m == 0 else odd[1]
+        side = side_of(m, odd)
         for d in range(2):
             ref[d * K : (d + 1) * K, :] = edge[2 * side + d].astype(BF16)
         ref[2 * K : 2 * K + AUX, :] = yaux[side].astype(BF16)
+
+
+def side_of(m, odd):
+    return 1 - odd if m == 0 else odd
+
+
+def send_kernel(K, NZ, X, pt_ref, cg_ref, wg_ref, y0_ref, y1_ref, q0_ref, q1_ref, x0_ref, x1_ref, aux):
+    ext = X + 4
+    odd = lax.rem(lax.axis_index("gx"), 2)
+    for m, ref in enumerate((q0_ref, q1_ref)):
+        side = side_of(m, odd)
+        for n, got in enumerate((y0_ref, y1_ref)):
+            at = n * (K + AUX)
+            ref[at : at + K, :] = got[:K, :]
+            ref[at + K : at + K + AUX, :] = got[2 * K : 2 * K + AUX, :]
+        aux[...] = jnp.zeros_like(aux)
+        for h in range(2):
+            for z in range(NZ):
+                to = (h * NZ + z) * SUB
+                for d in range(3):
+                    aux[to + d : to + d + 1, :] = cg_ref[h, pl.ds(z * GROUP + REACH + side * (X - 3) + d, 1), :]
+                w_hi, w_lo = halves(wg_ref[h, pl.ds(z * GROUP + REACH + side * (X - 1), 1), :])
+                aux[to + 3 : to + 4, :] = w_hi.astype(F32)
+                aux[to + 4 : to + 5, :] = w_lo.astype(F32)
+        ref[2 * (K + AUX) :, :] = aux[...].astype(BF16)
     for m, ref in enumerate((x0_ref, x1_ref)):
-        side = 1 - odd[0] if m == 0 else odd[0]
+        side = side_of(m, odd)
         for z in range(NZ):
             for i in range(2):
                 row = pl.multiple_of((z * ext + 2 + side * (X - 2) + i) * K, SUB)
                 for h in range(2):
                     ref[(z * 2 + i) * K : (z * 2 + i + 1) * K, h * LANES : (h + 1) * LANES] = pt_ref[h, pl.ds(row, K), :].astype(BF16)
-        aux[...] = jnp.zeros_like(aux)
-        for z in range(NZ):
-            for d in range(3):
-                aux[z * SUB + d : z * SUB + d + 1, :] = cls_ref[pl.ds(z * X + side * (X - 3) + d, 1), :].astype(F32) + 1.0
-            w_hi, w_lo = halves(w_ref[pl.ds(z * X + side * (X - 1), 1), :])
-            aux[z * SUB + 3 : z * SUB + 4, :] = w_hi.astype(F32)
-            aux[z * SUB + 4 : z * SUB + 5, :] = w_lo.astype(F32)
-        ref[2 * NZ * K : 2 * NZ * K + NZ * SUB, :] = aux[...].astype(BF16)
+
+
+def prep_kernel(levels, R, after_ref, ranks_ref, right_ref, left_ref, fr_ref, fl_ref):
+    del after_ref
+    rank = lax.broadcasted_iota(jnp.int32, (R, 1), 0)
+    per = fr_ref.shape[0]
+    fr_ref[...] = jnp.zeros_like(fr_ref)
+    fl_ref[...] = jnp.zeros_like(fl_ref)
+    for l in range(levels):
+        scale = float(2 * LANES * 2**l) ** -0.5
+        right = jnp.where(rank < ranks_ref[l], right_ref[l] * scale, 0.0).astype(BF16)
+        left = left_ref[l].astype(BF16)
+        for i in range(per):
+            at = l * LANES + i * R
+            fr_ref[i, at : at + R, :] = right
+            fl_ref[i, at : at + R, :] = left
+
+
+def mult(v):
+    return v if isinstance(v, int) else pl.multiple_of(v, SUB)
+
+
+def stencil(NZ, z, coef_row, cf, first_cf, src, centre_row, x_step, z_step, halo, kt):
+    lane = lanes_of((SUB, LANES))
+    is_first, is_last = lane == 0, lane == LANES - 1
+
+    def at(row):
+        return pl.ds(mult(row), SUB)
+
+    row = centre_row + kt * SUB
+    c = [src[h, at(row), :] for h in range(2)]
+    up = [src[h, at(row + x_step), :] for h in range(2)]
+    down = [src[h, at(row - x_step), :] for h in range(2)]
+    hl = pltpu.roll(halo[0, kt * SUB : (kt + 1) * SUB, :], LANES - coef_row, 1)
+    hr = pltpu.roll(halo[1, kt * SUB : (kt + 1) * SUB, :], LANES - 1 - coef_row, 1)
+    fwd = [pltpu.roll(v, LANES - 1, 1) for v in c]
+    bwd = [pltpu.roll(v, 1, 1) for v in c]
+    nxt = [jnp.where(is_last, fwd[1], fwd[0]), jnp.where(is_last, hr, fwd[1])]
+    prv = [jnp.where(is_first, hl, bwd[0]), jnp.where(is_first, bwd[0], bwd[1])]
+    out = []
+    for h in range(2):
+        co = [cf[first_cf + j, h, pl.ds(coef_row, 1), :] for j in range(7)]
+        acc = co[0] * c[h] + co[1] * up[h] + co[2] * down[h] + co[3] * nxt[h] + co[4] * prv[h]
+        if z < NZ - 1:
+            acc = acc + co[5] * src[h, at(row + z_step), :]
+        if z > 0:
+            acc = acc + co[6] * src[h, at(row - z_step), :]
+        out.append(acc)
+    return out
+
+
+def stage_one(K, NZ, X, x, cf, pt_ref, t_ref, hp):
+    ext, wide = X + 4, X + 2
+    for z in range(NZ):
+        for kt in range(K // SUB):
+            out = stencil(NZ, z, z * GROUP + x + REACH, cf, 0, pt_ref, (z * ext + x + 2) * K, K, ext * K, hp, kt)
+            to = mult((z * wide + x + 1) * K + kt * SUB)
+            for h in range(2):
+                t_ref[h, pl.ds(to, SUB), :] = out[h]
+
+
+def stage_two(K, NZ, X, x, cf, pt_ref, t_ref, s_ref, ht):
+    ext, wide = X + 4, X + 2
+    his = []
+    for z in range(NZ):
+        lines = []
+        for kt in range(K // SUB):
+            out = stencil(NZ, z, z * GROUP + x + REACH, cf, 7, t_ref, (z * wide + x + 1) * K, K, wide * K, ht, kt)
+            row = mult((z * ext + x + 2) * K + kt * SUB)
+            to = mult((z * X + x) * K + kt * SUB)
+            both = []
+            for h in range(2):
+                s = out[h] + pt_ref[h, pl.ds(row, SUB), :]
+                s_ref[h, pl.ds(to, SUB), :] = s
+                both.append(s)
+            lines.append(jnp.concatenate(both, 1))
+        his.append(jnp.concatenate(lines, 0).astype(BF16))
+    return jnp.concatenate(his, 0)
 
 
 def merged(own, from_left, from_right):
@@ -122,47 +217,47 @@
     return jnp.where(m < REACH, left, out)
 
 
-def main_kernel(
-    K, NZ, X, levels, R,
-    table_hbm, ranks_hbm, pt_in, x0_ref, x1_ref, y0_ref, y1_ref, q0_ref, q1_ref, own_ref, cin_ref, win_ref, left_hbm, right_hbm,
-    s_ref, v_ref, u_ref, pt_ref, t_ref, cg, wg, rg, cf, hp, ht, ys, fac, table_ref, ranks_ref, sem,
+def inner_kernel(
+    K, NZ, X, R,
+    table_hbm, pt_ref, y0_ref, y1_ref, q0_ref, q1_ref, own_ref, cin_ref, win_ref, fr_ref,
+    s_ref, t_ref, cf, hp, ht, acc_ref, cg, wg, rg, ys, xs, table_ref, sem,
 ):
-    ext, wide = X + 4, X + 2
-    KT = K // SUB
     sq = (LANES, LANES)
     lane_sq = lanes_of(sq)
-    loads = [pltpu.make_async_copy(ref.at[pl.ds(0, levels)], fac.at[i], sem.at[i]) for i, ref in enumerate((right_hbm, left_hbm))]
-    loads.append(pltpu.make_async_copy(table_hbm, table_ref, sem.at[2]))
-    loads.append(pltpu.make_async_copy(ranks_hbm, ranks_ref, sem.at[3]))
-    for load in loads:
-        load.start()
-    odd = [lax.rem(lax.axis_index(axis), 2) for axis in ("gx", "gy")]
-    for m, ref in enumerate((x0_ref, x1_ref)):
-        side = 1 - odd[0] if m == 0 else odd[0]
-        for z in range(NZ):
-            for i in range(2):
-                at = pl.multiple_of((z * ext + i + side * (X + 2)) * K, SUB)
-                for h in range(2):
-                    cut = (slice((z * 2 + i) * K, (z * 2 + i + 1) * K), slice(h * LANES, (h + 1) * LANES))
-                    pt_ref[h, pl.ds(at, K), :] = ref[cut].astype(F32)
+    load = pltpu.make_async_copy(table_hbm, table_ref, sem)
+    load.start()
+    place = [lax.axis_index(axis) for axis in ("gx", "gy")]
+    last = [lax.axis_size(axis) - 1 for axis in ("gx", "gy")]
+    odd = [lax.rem(v, 2) for v in place]
+
+    def there(axis, side):
+        edge = lax.select(side == 0, place[axis], last[axis] - place[axis])
+        return lax.select(edge > 0, jnp.float32(1.0), jnp.float32(0.0))
+
     for m, ref in enumerate((y0_ref, y1_ref)):
-        ys[0, 1 - odd[1] if m == 0 else odd[1]] = ref[...].astype(F32)
+        side = side_of(m, odd[1])
+        y_there = there(1, side)
+        ys[0, side] = ref[...].astype(F32) * y_there
         for n, relay in enumerate((q0_ref, q1_ref)):
-            ys[1 + (1 - odd[0] if n == 0 else odd[0]), 1 - odd[1] if m == 0 else odd[1]] = relay[m].astype(F32)
+            x_side = side_of(n, odd[0])
+            factor = y_there * there(0, x_side)
+            at = m * (K + AUX)
+            ys[1 + x_side, side, :K, :] = relay[at : at + K, :].astype(F32) * factor
+            ys[1 + x_side, side, 2 * K :, :] = relay[at + K : at + K + AUX, :].astype(F32) * factor
+    for n, relay in enumerate((q0_ref, q1_ref)):
+        x_side = side_of(n, odd[0])
+        xs[x_side] = relay[2 * (K + AUX) :, :].astype(F32) * there(0, x_side)
     for h in range(2):
         cg[1 + h] = cin_ref[h]
         wg[1 + h] = win_ref[h]
-    for m, ref in enumerate((x0_ref, x1_ref)):
-        side = 1 - odd[0] if m == 0 else odd[0]
-        x_aux = ref[2 * NZ * K : 2 * NZ * K + NZ * SUB, :].astype(F32)
+    for side in range(2):
         for z in range(NZ):
-            a = z * SUB
             for h in range(2):
-                lo = slice(h * LANES, (h + 1) * LANES)
-                for d in range(3):
-                    cg[1 + h, pl.ds(z * GROUP + side * (X + REACH) + d, 1), :] = x_aux[a + d : a + d + 1, lo]
+                a = (h * NZ + z) * SUB
+                start = z * GROUP + side * (X + REACH)
+                cg[1 + h, start : start + REACH, :] = xs[side, a : a + REACH, :]
                 beside = z * GROUP + REACH - 1 + side * (X + 1)
-                wg[1 + h, pl.ds(beside, 1), :] = x_aux[a + 3 : a + 4, lo] + x_aux[a + 4 : a + 5, lo]
+                wg[1 + h, beside : beside + 1, :] = xs[side, a + 3 : a + 4, :] + xs[side, a + 4 : a + 5, :]
     spread = jnp.zeros(sq, F32)
     row_sq = lax.broadcasted_iota(jnp.int32, sq, 0)
     spread_w = jnp.zeros(sq, F32)
@@ -177,8 +272,7 @@
     for side in range(2):
         cg[3 * side] = jnp.where(keep[side], y_class, 0.0)
         wg[3 * side] = jnp.where(keep[side], y_weight, 0.0)
-    loads[2].wait()
-    loads[3].wait()
+    load.wait()
     for t in range(4):
         ids = cg[t]
         cond = jnp.zeros(sq, F32)
@@ -247,91 +341,67 @@
         hp[side] = p1
         ht[side] = total
 
-    lane = lanes_of((SUB, LANES))
-    is_first, is_last = lane == 0, lane == LANES - 1
-
-    def stencil(z, coef_row, first_cf, src, centre_row, x_step, z_step, halo, kt):
-        row = pl.multiple_of(centre_row + kt * SUB, SUB)
-        c = [src[h, pl.ds(row, SUB), :] for h in range(2)]
-        up = [src[h, pl.ds(row + x_step, SUB), :] for h in range(2)]
-        down = [src[h, pl.ds(row - x_step, SUB), :] for h in range(2)]
-        hl = pltpu.roll(halo[0, kt * SUB : (kt + 1) * SUB, :], LANES - coef_row, 1)
-        hr = pltpu.roll(halo[1, kt * SUB : (kt + 1) * SUB, :], LANES - 1 - coef_row, 1)
-        fwd = [pltpu.roll(v, LANES - 1, 1) for v in c]
-        bwd = [pltpu.roll(v, 1, 1) for v in c]
-        nxt = [jnp.where(is_last, fwd[1], fwd[0]), jnp.where(is_last, hr, fwd[1])]
-        prv = [jnp.where(is_first, hl, bwd[0]), jnp.where(is_first, bwd[0], bwd[1])]
-        out = []
-        for h in range(2):
-            co = [cf[first_cf + j, h, pl.ds(coef_row, 1), :] for j in range(7)]
-            acc = co[0] * c[h] + co[1] * up[h] + co[2] * down[h] + co[3] * nxt[h] + co[4] * prv[h]
-            if z < NZ - 1:
-                acc = acc + co[5] * src[h, pl.ds(row + z_step, SUB), :]
-            if z > 0:
-                acc = acc + co[6] * src[h, pl.ds(row - z_step, SUB), :]
-            out.append(acc)
-        return row, out
-
-    def stage_one(i, carry):
+
+    def first_lines(i, carry):
+        stage_one(K, NZ, X, i, cf, pt_ref, t_ref, hp)
+        return carry
+
+    lax.fori_loop(1, X - 1, first_lines, 0, unroll=UNROLL_ONE)
+    acc_ref[...] = jnp.zeros_like(acc_ref)
+    per = LANES // R // 2
+
+    def second_lines(i, carry):
+        for half in range(2):
+            lines = stage_two(K, NZ, X, 2 * i + half, cf, pt_ref, t_ref, s_ref, ht)
+            group = lax.div(i, per)
+            acc_ref[group] = acc_ref[group] + nt(lines, fr_ref[2 * lax.rem(i, per) + half])
+        return carry
+
+    lax.fori_loop(1, X // 2 - 1, second_lines, 0, unroll=UNROLL_TWO)
+
+
+def edge_kernel(K, NZ, X, R, pt_in, t_in, s_in, x0_ref, x1_ref, cf, hp, ht, acc_ref, fr_ref, pt_ref, t_ref, s_ref, v_ref):
+    ext = X + 4
+    odd = lax.rem(lax.axis_index("gx"), 2)
+    for m, ref in enumerate((x0_ref, x1_ref)):
+        side = side_of(m, odd)
         for z in range(NZ):
-            for kt in range(KT):
-                _, out = stencil(z, z * GROUP + i + 2, 0, pt_ref, (z * ext + i + 1) * K, K, ext * K, hp, kt)
-                to = pl.multiple_of((z * wide + i) * K + kt * SUB, SUB)
+            for i in range(2):
+                at = pl.multiple_of((z * ext + i + side * (X + 2)) * K, SUB)
                 for h in range(2):
-                    t_ref[h, pl.ds(to, SUB), :] = out[h]
-        return carry
-
-    lax.fori_loop(0, wide, stage_one, 0, unroll=UNROLL_ONE)
-
-    lane_k = lanes_of((K, LANES))
-    loads[0].wait()
-    loads[1].wait()
-    rank = lax.broadcasted_iota(jnp.int32, (R, 1), 0)
-    terms = []
-    for l in range(levels):
-        scale = float(2 * LANES * 2**l) ** -0.5
-        terms.append(jnp.where(rank < ranks_ref[l], fac[0, l] * scale, 0.0))
-    terms += [fac[1, l] for l in range(levels)]
-    factor = jnp.concatenate(terms, 0).astype(BF16)
-
-    def stage_two(i, carry):
-        places = [[jnp.zeros((K, LANES), F32) for _ in range(levels)] for _ in range(2)]
-        for half in range(2):
-            x = 2 * i + half
-            his = []
+                    cut = (slice((z * 2 + i) * K, (z * 2 + i + 1) * K), slice(h * LANES, (h + 1) * LANES))
+                    pt_ref[h, pl.ds(at, K), :] = ref[cut].astype(F32)
+    for x in (-1, 0, X - 1, X):
+        stage_one(K, NZ, X, x, cf, pt_ref, t_ref, hp)
+    per = LANES // R
+    sums = [acc_ref[g] for g in range(X // per)]
+    for x in (0, 1, X - 2, X - 1):
+        lines = stage_two(K, NZ, X, x, cf, pt_ref, t_ref, s_ref, ht)
+        sums[x // per] = sums[x // per] + nt(lines, fr_ref[x % per])
+    for g, total in enumerate(sums):
+        for l in range(v_ref.shape[0]):
+            v_ref[l, g] = total[:, l * LANES : (l + 1) * LANES].astype(BF16)
+
+
+def left_kernel(K, NZ, X, R, after_ref, s_ref, fl_ref, u_ref):
+    del after_ref
+    per = LANES // R
+    for g in range(X // per):
+        total = None
+        for i in range(per):
+            x = g * per + i
+            lines = []
             for z in range(NZ):
-                lines = []
-                for kt in range(KT):
-                    _, out = stencil(z, z * GROUP + x + REACH, 7, t_ref, (z * wide + x + 1) * K, K, wide * K, ht, kt)
-                    row = pl.multiple_of((z * ext + x + 2) * K + kt * SUB, SUB)
-                    to = pl.multiple_of((z * X + x) * K + kt * SUB, SUB)
-                    both = []
-                    for h in range(2):
-                        s = out[h] + pt_ref[h, pl.ds(row, SUB), :]
-                        s_ref[h, pl.ds(to, SUB), :] = s
-                        both.append(s)
-                    lines.append(jnp.concatenate(both, 1))
-                his.append(jnp.concatenate(lines, 0).astype(BF16))
-            coef = nt(jnp.concatenate(his, 0), factor)
-            if coef.shape[1] < LANES:
-                coef = jnp.concatenate([coef, jnp.zeros((NZ * K, LANES - coef.shape[1]), F32)], 1)
-            for z in range(NZ):
-                part = coef[z * K : (z + 1) * K]
-                at = half * NZ * R + z * R
-                here = (lane_k >= at) & (lane_k < at + R)
-                for q in range(2):
-                    for l in range(levels):
-                        moved = pltpu.roll(part, (at - (q * levels + l) * R) % LANES, 1)
-                        places[q][l] = jnp.where(here, moved, places[q][l])
-        for l in range(levels):
-            v_ref[l, i] = places[0][l].astype(BF16)
-            u_ref[l, i] = places[1][l].astype(BF16)
-        return carry
-
-    lax.fori_loop(0, X // 2, stage_two, 0, unroll=UNROLL_TWO)
-
-
-def gram_kernel(K, first, count, s_ref, block_ref, gx_ref):
+                at = (z * X + x) * K
+                lines.append(jnp.concatenate([s_ref[h, at : at + K, :] for h in range(2)], 1).astype(BF16))
+            term = nt(jnp.concatenate(lines, 0), fl_ref[i])
+            total = term if total is None else total + term
+        for l in range(u_ref.shape[0]):
+            u_ref[l, g] = total[:, l * LANES : (l + 1) * LANES].astype(BF16)
+
+
+def gram_kernel(K, first, count, s_ref, block_ref, *refs):
+    gx_ref = refs[-1]
     leaf_matrix = block_ref[...].astype(BF16)
 
     def chunk(i, carry):
@@ -359,8 +429,9 @@
     gx_refs, sib_refs, out_ref = refs[:parts], refs[parts:-1], refs[-1]
     total = jnp.zeros((K, K), F32)
     for l, ref in enumerate(sib_refs):
-        for i in range(u_ref.shape[1]):
-            total = total + nt(u_ref[l, i], ref[i])
+        for g in range(u_ref.shape[1]):
+            for at in range(0, u_ref.shape[2], K):
+                total = total + nt(u_ref[l, g, at : at + K, :], ref[g, at : at + K, :])
     out_ref[...] = sum(ref[...] for ref in gx_refs)
     at = LANES // 2
     out_ref[:, at : at + K] = out_ref[:, at : at + K] + total
@@ -384,7 +455,6 @@
     proj_ref[...] = nt(left, inverse, precision=HIGH)
     i_hi, i_lo = halves(inverse)
     lhs = jnp.concatenate([i_hi, i_lo, i_hi], 1)
-    W = 2 * LANES
     copies = []
     for z in range(NZ):
 
@@ -399,7 +469,7 @@
 
         lax.fori_loop(0, X, line, 0, unroll=True)
         for h in range(2):
-            for part in range(1):
+            for _ in range(1):
                 copies.append(
                     pltpu.make_async_copy(
                         out.at[h, z].reshape(K, X, LANES), basis_ref.at[:, z, :, pl.ds(h * LANES, LANES)], sem.at[z, h]
@@ -418,9 +488,11 @@
     return lax.ppermute(v, axis, [(i, i ^ bits) for i in range(lax.axis_size(axis))])
 
 
-def paired(v, axis, first):
+def paired(v, axis, first, ring=True):
     n = lax.axis_size(axis)
     swaps = [(i, i + 1) for i in range(first, n - 1, 2)]
+    if first and ring:
+        swaps = swaps + [(0, n - 1)]
     return lax.ppermute(v, axis, swaps + [(j, i) for i, j in swaps])
 
 
@@ -442,9 +514,16 @@
     shape = jax.ShapeDtypeStruct
     cls2, w2 = classes.reshape(rows, W), weights.reshape(rows, W)
     params = functools.partial(pltpu.CompilerParams, vmem_limit_bytes=32 << 20)
-    y_rows, x_rows = 2 * K + AUX, 2 * NZ * K + NZ * SUB
+    y_rows, x_rows = 2 * K + AUX, 2 * NZ * K
+    q_rows = 2 * (K + AUX) + 2 * NZ * SUB
     square = (LANES, LANES)
-    pt, cg, wg, own, y0, y1, x0, x1 = pl.pallas_call(
+    per = LANES // R
+    groups = X // per
+
+    def cost(flops, nbytes=4 << 20):
+        return pl.CostEstimate(flops=flops, bytes_accessed=nbytes, transcendentals=0)
+
+    pt, cg, wg, own, y0, y1 = pl.pallas_call(
         functools.partial(pack_kernel, K, NZ, X),
         out_shape=(
             shape((2, NZ * ext * K, LANES), F32),
@@ -453,17 +532,14 @@
             shape((2, K, LANES), F32),
             shape((y_rows, LANES), BF16),
             shape((y_rows, LANES), BF16),
-            shape((x_rows, W), BF16),
-            shape((x_rows, W), BF16),
         ),
         in_specs=[HBM] * 3,
-        out_specs=(VMEM,) * 8,
+        out_specs=(VMEM,) * 6,
         scratch_shapes=[
             pltpu.VMEM((K * rows, W), BF16),
             pltpu.VMEM((rows, W), jnp.int32),
             pltpu.VMEM((rows, W), F32),
             pltpu.VMEM((4, K, LANES), F32),
-            pltpu.VMEM((NZ * SUB, W), F32),
             pltpu.VMEM((2, AUX, LANES), F32),
             pltpu.SemaphoreType.DMA((6,)),
         ],
@@ -471,54 +547,91 @@
         name="pack",
     )(in_hbm(probes.reshape(K * rows, W)), in_hbm(cls2), in_hbm(w2))
     y0, y1 = paired(y0, "gy", 0), paired(y1, "gy", 1)
-    x0, x1 = paired(x0, "gx", 0), paired(x1, "gx", 1)
-    both = jnp.stack([y0, y1])
-    q0, q1 = paired(both, "gx", 0), paired(both, "gx", 1)
-    slab = (2, rows * K, LANES)
-    side = (levels, X // 2, K, LANES)
-    s, v, u, _ = pl.pallas_call(
-        functools.partial(main_kernel, K, NZ, X, levels, R),
-        out_shape=(shape(slab, F32), shape(side, BF16), shape(side, BF16), shape(pt.shape, F32)),
-        in_specs=[HBM] * 2 + [VMEM] * 10 + [HBM] * 2,
+    q0, q1, x0, x1 = pl.pallas_call(
+        functools.partial(send_kernel, K, NZ, X),
+        out_shape=(shape((q_rows, LANES), BF16),) * 2 + (shape((x_rows, W), BF16),) * 2,
+        in_specs=[VMEM] * 5,
         out_specs=(VMEM,) * 4,
-        scratch_shapes=[
-            pltpu.VMEM((2, NZ * wide * K, LANES), F32),
-            pltpu.VMEM((4, *square), F32),
-            pltpu.VMEM((4, *square), F32),
-            pltpu.VMEM((4, *square), F32),
-            pltpu.VMEM((14, 2, *square), F32),
-            pltpu.VMEM((2, K, LANES), F32),
-            pltpu.VMEM((2, K, LANES), F32),
+        scratch_shapes=[pltpu.VMEM((2 * NZ * SUB, LANES), F32)],
+        compiler_params=params(),
+        name="send",
+    )(pt, cg, wg, y0, y1)
+    q0 = paired(q0, "gx", 0)
+    q1 = paired(q1, "gx", 1)
+    x0 = paired(x0, "gx", 0)
+    x1 = paired(x1, "gx", 1, False)
+    factors = shape((per, levels * LANES, W), BF16)
+    fr, fl = pl.pallas_call(
+        functools.partial(prep_kernel, levels, R),
+        out_shape=(factors, factors),
+        in_specs=[VMEM, pl.BlockSpec(memory_space=pltpu.SMEM), VMEM, VMEM],
+        out_specs=(VMEM, VMEM),
+        cost_estimate=cost(1 << 20, 2 << 20),
+        compiler_params=params(),
+        name="prep",
+    )(y0, block_ranks, prior_right, prior_left)
+    slab = shape((2, rows * K, LANES), F32)
+    firsts = shape((2, NZ * wide * K, LANES), F32)
+    pair = shape((2, K, LANES), F32)
+    coefs = shape((14, 2, *square), F32)
+    s, t, cf, hp, ht, acc = pl.pallas_call(
+        functools.partial(inner_kernel, K, NZ, X, R),
+        out_shape=(slab, firsts, coefs, pair, pair, shape((groups, NZ * K, levels * LANES), F32)),
+        in_specs=[HBM] + [VMEM] * 9,
+        out_specs=(VMEM,) * 6,
+        scratch_shapes=[pltpu.VMEM((4, *square), F32)] * 3
+        + [
             pltpu.VMEM((3, 2, y_rows, LANES), F32),
-            pltpu.VMEM((2, levels, R, W), F32),
+            pltpu.VMEM((2, 2 * NZ * SUB, LANES), F32),
             pltpu.SMEM(class_table.shape, F32),
-            pltpu.SMEM(block_ranks.shape, jnp.int32),
-            pltpu.SemaphoreType.DMA((4,)),
+            pltpu.SemaphoreType.DMA,
         ],
-        input_output_aliases={2: 3},
-        compiler_params=params(),
-        name="sketch",
-    )(in_hbm(class_table), in_hbm(block_ranks), pt, x0, x1, y0, y1, q0, q1, own, cg, wg, in_hbm(prior_left), in_hbm(prior_right))
+        cost_estimate=cost(1 << 30, 20 << 20),
+        compiler_params=params(),
+        name="inner",
+    )(in_hbm(class_table), pt, y0, y1, q0, q1, own, cg, wg, fr)
+    side = shape((levels, groups, NZ * K, LANES), BF16)
+    _, _, s, v = pl.pallas_call(
+        functools.partial(edge_kernel, K, NZ, X, R),
+        out_shape=(shape(pt.shape, F32), firsts, slab, side),
+        in_specs=[VMEM] * 10,
+        out_specs=(VMEM,) * 4,
+        input_output_aliases={0: 0, 1: 1, 2: 2},
+        compiler_params=params(),
+        name="edge",
+    )(pt, t, s, x0, x1, cf, hp, ht, acc, fr)
     share = rows // GRAM_PARTS
     parts = []
-    for i in range(GRAM_PARTS):
-        parts.append(
-            pl.pallas_call(
-                functools.partial(gram_kernel, K, i * share, share),
-                out_shape=shape((K, LANES), F32),
-                in_specs=[VMEM] * 2,
-                out_specs=VMEM,
-                cost_estimate=pl.CostEstimate(flops=2 * 300 * K * share * W, bytes_accessed=8 << 20, transcendentals=0),
-                compiler_params=params(),
-                name=f"gram_{i}",
-            )(s, prior_block)
-        )
+
+    def gram_part(i, *after):
+        return pl.pallas_call(
+            functools.partial(gram_kernel, K, i * share, share),
+            out_shape=shape((K, LANES), F32),
+            in_specs=[VMEM] * (2 + len(after)),
+            out_specs=VMEM,
+            cost_estimate=cost(2 * 300 * K * share * W, 8 << 20),
+            compiler_params=params(),
+        )(s, prior_block, *after)
+
+    parts.append(gram_part(0))
     sibs = []
     pending = v
     for l in range(levels):
         got = exchanged(pending, "gy", 2**l)
+        if l == 0:
+            first_got = got
         sibs.append(got[0])
         pending = (pending[1:].astype(F32) + got[1:].astype(F32)).astype(BF16)
+    parts += [gram_part(i, first_got) for i in range(1, GRAM_PARTS)]
+    u = pl.pallas_call(
+        functools.partial(left_kernel, K, NZ, X, R),
+        out_shape=side,
+        in_specs=[VMEM] * 3,
+        out_specs=VMEM,
+        cost_estimate=cost(1 << 28, 8 << 20),
+        compiler_params=params(),
+        name="left",
+    )(first_got, s, fl)
     gx = pl.pallas_call(
         functools.partial(couple_kernel, K, GRAM_PARTS),
         out_shape=shape((K, LANES), F32),

time: 69.2 us -> 65 us (0.939)
  starting transfers between devices: 26.7 us -> 21.7 us
  waiting for transfers between devices: 14.8 us -> 16.3 us
  Pallas kernels: 26.7 us -> 25.8 us
    ppermute x7, starting transfers between devices: 16 us -> 9.16 us  [exchanged(): lax.ppermute(v, axis, [(i, i ^ bits) for i in range(lax.axis_size(axis))])]
    ppermute x6, waiting for transfers between devices: 2.68 us -> 5.25 us  [paired(): return lax.ppermute(v, axis, swaps + [(j, i) for i, j in swaps])]
    ppermute x6, starting transfers between devices: 10.7 us -> 12.5 us  [paired(): return lax.ppermute(v, axis, swaps + [(j, i) for i, j in swaps])]
    ppermute x7, waiting for transfers between devices: 12.1 us -> 11 us  [exchanged(): lax.ppermute(v, axis, [(i, i ^ bits) for i in range(lax.axis_size(axis))])]
    pallas_call x3 -> x7, Pallas kernels: 14.7 us -> 13.9 us  [the longest x1 7.3 us: shards(): pl.pallas_call(functools.partial(inner_kernel, K, NZ, X, R), out_shape=(s...]
  transfers between devices with their start and end apart: 13 -> 13, of which waited for: 8 -> 9; matrix products, arithmetic and copies ran while one was open for 0% -> 0% of each run, Pallas kernels for 5% -> 19%
where the time goes in v2:
time: 65 us; the launch traced here: 64.8 us
  Pallas kernels  25.8 us (40%)
  starting transfers between devices  21.7 us (33%)
  waiting for transfers between devices  16.3 us (25%)
  between operations  0.95 us (1%)
    ppermute x6, starting transfers between devices, paired(): return lax.ppermute(v, axis, swaps + [(j, i) for i, j in swaps])  12.5 us
    ppermute x7, waiting for transfers between devices, exchanged(): lax.ppermute(v, axis, [(i, i ^ bits) for i in range(lax.axis_size(axis))])  11 us
    ppermute x7, starting transfers between devices, exchanged(): lax.ppermute(v, axis, [(i, i ^ bits) for i in range(lax.axis_size(axis))])  9.16 us
    pallas_call x1, Pallas kernels, shards(): pl.pallas_call(functools.partial(finish_kernel, K, NZ, X, cells), out_sha...  7.42 us
    pallas_call x1, Pallas kernels, shards(): pl.pallas_call(functools.partial(inner_kernel, K, NZ, X, R), out_shape=(s...  7.3 us
    ppermute x6, waiting for transfers between devices, paired(): return lax.ppermute(v, axis, swaps + [(j, i) for i, j in swaps])  5.25 us
    pallas_call x1, Pallas kernels, shards(): pl.pallas_call(functools.partial(pack_kernel, K, NZ, X), out_shape=(shape...  4.2 us
    pallas_call x2, Pallas kernels, gram_part(): pl.pallas_call(functools.partial(gram_kernel, K, i * share, share), out_s...  3.41 us
  transfers between devices with their start and end apart: 13, of which 9 were waited for; matrix products, arithmetic and copies ran while one was open for 0% of the time, Pallas kernels for 19%

profile of v2, /device:TPU:0, one launch (start us, length us, event | category | flops | bytes accessed | tf_op | source)
XLA Modules:
  0.0 64.8 jit_solution(3266081567581620819)
XLA Ops:
  0.7 4.2 %pack.1 = (f32[2,3840,128]{2,1,0:T(8,128)S(1)}, f32[2,128,128]{2,1,0:T(8,128)S(1)}, f32[2,128,128]{2,1,0:T(8,128)S(1)}, f32[2,48,128]{2,1,0:T(8,128)S(1)}, bf16[...) custom-call(bf16[3072,256]{1,0:T(8,128)(2,1)} %bitcast.7, s32[64,256]{1,0:T(8,128)} %bitcast.8, f32[64,256]{1,0:T(8,128)} %bitcast.9), custom_call_target="tpu_custom_call" | custom-call | tf_op jit(solution)/shard_map/pack/pallas_call | solution.py:526
  5.4 2.6 %collective-permute-start.1 = (bf16[112,128]{1,0:T(8,128)(2,1)S(1)}, bf16[112,128]{1,0:T(8,128)(2,1)S(1)}, u32[]{:S(2)}, u32[]{:S(2)}) collective-permute-start(bf16[112,128]{1,0:T(8,128)(2,1)S(1)} %get-tuple-element.24), channel_id=1, source_target_pairs={{1,2},{0,3},{2,1},{3,0},{5,6},{4,7},{6,5},{7,4},{9,10},{8,11},{10,... | collective-permute-start | bytes 86024 | tf_op jit(solution)/shard_map/ppermute | solution.py:496
  8.1 1.6 %collective-permute-done.1.y1_ref = bf16[112,128]{1,0:T(8,128)(2,1)S(1)} collective-permute-done((bf16[112,128]{1,0:T(8,128)(2,1)S(1)}, bf16[112,128]{1,0:T(8,128)(2,1)S(1)}, u32[]{:S(2)}, u32[]{:S(2)}) %collective-permute-start.1) | collective-permute-done | bytes 28704 | tf_op jit(solution)/shard_map/ppermute | solution.py:496
  9.7 1.7 %collective-permute-start.4 = (bf16[384,256]{1,0:T(8,128)(2,1)S(1)}, bf16[384,256]{1,0:T(8,128)(2,1)S(1)}, u32[]{:S(2)}, u32[]{:S(2)}) collective-permute-start(bf16[384,256]{1,0:T(8,128)(2,1)S(1)} %get-tuple-element.33), channel_id=1, source_target_pairs={{0,4},{8,12},{16,20},{24,28},{4,0},{12,8},{20,16},{28,24},{1,5},{9... | collective-permute-start | bytes 589832 | tf_op jit(solution)/shard_map/ppermute | solution.py:496
  12.3 4.3 %collective-permute-start.2 = (bf16[192,128]{1,0:T(8,128)(2,1)S(1)}, bf16[192,128]{1,0:T(8,128)(2,1)S(1)}, u32[]{:S(2)}, u32[]{:S(2)}) collective-permute-start(bf16[192,128]{1,0:T(8,128)(2,1)S(1)} %get-tuple-element.27), channel_id=1, source_target_pairs={{0,4},{8,12},{16,20},{24,28},{4,0},{12,8},{20,16},{28,24},{1,5},{9... | collective-permute-start | bytes 147464 | tf_op jit(solution)/shard_map/ppermute | solution.py:496
  16.6 2.4 %collective-permute-start.3 = (bf16[192,128]{1,0:T(8,128)(2,1)S(1)}, bf16[192,128]{1,0:T(8,128)(2,1)S(1)}, u32[]{:S(2)}, u32[]{:S(2)}) collective-permute-start(bf16[192,128]{1,0:T(8,128)(2,1)S(1)} %get-tuple-element.28), channel_id=1, source_target_pairs={{4,8},{12,16},{20,24},{0,28},{8,4},{16,12},{24,20},{28,0},{5,9},{1... | collective-permute-start | bytes 147464 | tf_op jit(solution)/shard_map/ppermute | solution.py:496
  19.8 2.7 %collective-permute-done.2.q0_ref = bf16[192,128]{1,0:T(8,128)(2,1)S(1)} collective-permute-done((bf16[192,128]{1,0:T(8,128)(2,1)S(1)}, bf16[192,128]{1,0:T(8,128)(2,1)S(1)}, u32[]{:S(2)}, u32[]{:S(2)}) %collective-permute-start.2) | collective-permute-done | bytes 49184 | tf_op jit(solution)/shard_map/ppermute | solution.py:496
  22.5 0.9 %collective-permute-done.3.q1_ref = bf16[192,128]{1,0:T(8,128)(2,1)S(1)} collective-permute-done((bf16[192,128]{1,0:T(8,128)(2,1)S(1)}, bf16[192,128]{1,0:T(8,128)(2,1)S(1)}, u32[]{:S(2)}, u32[]{:S(2)}) %collective-permute-start.3) | collective-permute-done | bytes 49184 | tf_op jit(solution)/shard_map/ppermute | solution.py:496
  23.4 7.3 %inner.1 = (f32[2,3072,128]{2,1,0:T(8,128)S(1)}, f32[2,3456,128]{2,1,0:T(8,128)S(1)}, f32[14,2,128,128]{3,2,1,0:T(8,128)S(1)}, f32[2,48,128]{2,1,0:T(8,128)S(1)}...) custom-call(f32[8]{0:T(128)} %table_hbm.1, f32[2,3840,128]{2,1,0:T(8,128)S(1)} %get-tuple-element.22.pt_ref.pt_in, ...), custom_call_target="tpu_custom_call" | custom-call | flops 1073741824 | bytes 20971520 | tf_op jit(solution)/shard_map/inner/pallas_call | solution.py:577
  30.8 1.6 %edge.1 = (f32[2,3840,128]{2,1,0:T(8,128)S(1)}, f32[2,3456,128]{2,1,0:T(8,128)S(1)}, f32[2,3072,128]{2,1,0:T(8,128)S(1)}, bf16[2,2,192,128]{3,2,1,0:T(8,128)(2,1)S(1)}) custom-call(f32[2,3840,128]{2,1,0:T(8,128)S(1)} %get-tuple-element.22.pt_ref.pt_in, ...), custom_call_target="tpu_custom_call", output_to_operand_aliasing={{0}: (0, {}), {1}: (1, {}), {2}: (2, {})} | custom-call | tf_op jit(solution)/shard_map/edge/pallas_call | solution.py:594
  32.4 1.7 %shard_map.95.refs_0_ = f32[48,128]{1,0:T(8,128)S(1)} custom-call(f32[2,3072,128]{2,1,0:T(8,128)S(1)} %get-tuple-element.40.s_ref, f32[256,256]{1,0:T(8,128)S(1)} %copy-done), custom_call_target="tpu_custom_call" | custom-call | flops 235929600 | bytes 8388608 | tf_op jit(solution)/shard_map/pallas_call | solution.py:607
  34.2 1.6 %collective-permute-start.7 = (bf16[1,2,192,128]{3,2,1,0:T(8,128)(2,1)S(1)}, bf16[1,2,192,128]{3,2,1,0:T(8,128)(2,1)S(1)}, u32[]{:S(2)}, u32[]{:S(2)}) collective-permute-start(bf16[1,2,192,128]{3,2,1,0:T(8,128)(2,1)S(1)} %add_convert_fusion), channel_id=1, source_target_pairs={{0,2},{1,3},{2,0},{3,1},{4,6},{5,7},{6,4},{7,5},{8,10},{9,11},{10,... | collective-permute-start | bytes 294920 | tf_op jit(solution)/shard_map/ppermute | solution.py:488
  35.8 1.7 %shard_map.96.refs_1_ = f32[48,128]{1,0:T(8,128)S(1)} custom-call(f32[2,3072,128]{2,1,0:T(8,128)S(1)} %get-tuple-element.40.s_ref, f32[256,256]{1,0:T(8,128)S(1)} %copy-done, bf16[2,2,192,128]{3,2,1,0:T(8,128)(2,1)S(1)} %collective-permute-done.6.after_ref.refs_0_), custom_call_target="tpu_custom_call" | custom-call | flops 235929600 | bytes 8388608 | tf_op jit(solution)/shard_map/pallas_call | solution.py:607
  38.3 1.1 %collective-permute-done.7 = bf16[1,2,192,128]{3,2,1,0:T(8,128)(2,1)S(1)} collective-permute-done((bf16[1,2,192,128]{3,2,1,0:T(8,128)(2,1)S(1)}, bf16[1,2,192,128]{3,2,1,0:T(8,128)(2,1)S(1)}, u32[]{:S(2)}, u32[]{:S(2)}) %collective-permute-start.7) | collective-permute-done | bytes 98336 | tf_op jit(solution)/shard_map/ppermute | solution.py:488
  39.8 1.2 %collective-permute-done.8 = f32[48,128]{1,0:T(8,128)S(1)} collective-permute-done((f32[48,128]{1,0:T(8,128)S(1)}, f32[48,128]{1,0:T(8,128)S(1)}, u32[]{:S(2)}, u32[]{:S(2)}) %collective-permute-start.8) | collective-permute-done | bytes 24608 | tf_op jit(solution)/shard_map/ppermute | solution.py:488
  41.0 1.5 %collective-permute-start.9 = (f32[48,128]{1,0:T(8,128)S(1)}, f32[48,128]{1,0:T(8,128)S(1)}, u32[]{:S(2)}, u32[]{:S(2)}) collective-permute-start(f32[48,128]{1,0:T(8,128)S(1)} %add.19), channel_id=1, source_target_pairs={{0,2},{1,3},{2,0},{3,1},{4,6},{5,7},{6,4},{7,5},{8,10},{9,11},{10,... | collective-permute-start | bytes 73736 | tf_op jit(solution)/shard_map/ppermute | solution.py:488
  42.5 2.3 %collective-permute-done.9 = f32[48,128]{1,0:T(8,128)S(1)} collective-permute-done((f32[48,128]{1,0:T(8,128)S(1)}, f32[48,128]{1,0:T(8,128)S(1)}, u32[]{:S(2)}, u32[]{:S(2)}) %collective-permute-start.9) | collective-permute-done | bytes 24608 | tf_op jit(solution)/shard_map/ppermute | solution.py:488
  44.9 1.6 %collective-permute-start.10 = (f32[48,128]{1,0:T(8,128)S(1)}, f32[48,128]{1,0:T(8,128)S(1)}, u32[]{:S(2)}, u32[]{:S(2)}) collective-permute-start(f32[48,128]{1,0:T(8,128)S(1)} %add.20), channel_id=1, source_target_pairs={{0,4},{4,0},{8,12},{12,8},{16,20},{20,16},{24,28},{28,24},{1,5},{5... | collective-permute-start | bytes 73736 | tf_op jit(solution)/shard_map/ppermute | solution.py:488
  46.4 2.2 %collective-permute-done.10 = f32[48,128]{1,0:T(8,128)S(1)} collective-permute-done((f32[48,128]{1,0:T(8,128)S(1)}, f32[48,128]{1,0:T(8,128)S(1)}, u32[]{:S(2)}, u32[]{:S(2)}) %collective-permute-start.10) | collective-permute-done | bytes 24608 | tf_op jit(solution)/shard_map/ppermute | solution.py:488
  48.7 1.7 %collective-permute-start.11 = (f32[48,128]{1,0:T(8,128)S(1)}, f32[48,128]{1,0:T(8,128)S(1)}, u32[]{:S(2)}, u32[]{:S(2)}) collective-permute-start(f32[48,128]{1,0:T(8,128)S(1)} %add.21), channel_id=1, source_target_pairs={{0,8},{4,12},{8,0},{12,4},{16,24},{20,28},{24,16},{28,20},{1,9},{5... | collective-permute-start | bytes 73736 | tf_op jit(solution)/shard_map/ppermute | solution.py:488
  50.4 2.2 %collective-permute-done.11 = f32[48,128]{1,0:T(8,128)S(1)} collective-permute-done((f32[48,128]{1,0:T(8,128)S(1)}, f32[48,128]{1,0:T(8,128)S(1)}, u32[]{:S(2)}, u32[]{:S(2)}) %collective-permute-start.11) | collective-permute-done | bytes 24608 | tf_op jit(solution)/shard_map/ppermute | solution.py:488
  52.5 2.7 %collective-permute-start.12 = (f32[48,128]{1,0:T(8,128)S(1)}, f32[48,128]{1,0:T(8,128)S(1)}, u32[]{:S(2)}, u32[]{:S(2)}) collective-permute-start(f32[48,128]{1,0:T(8,128)S(1)} %add.22), channel_id=1, source_target_pairs={{0,16},{4,20},{8,24},{12,28},{16,0},{20,4},{24,8},{28,12},{1,17},{... | collective-permute-start | bytes 73736 | tf_op jit(solution)/shard_map/ppermute | solution.py:488
  55.2 2.0 %collective-permute-done.12 = f32[48,128]{1,0:T(8,128)S(1)} collective-permute-done((f32[48,128]{1,0:T(8,128)S(1)}, f32[48,128]{1,0:T(8,128)S(1)}, u32[]{:S(2)}, u32[]{:S(2)}) %collective-permute-start.12) | collective-permute-done | bytes 24608 | tf_op jit(solution)/shard_map/ppermute | solution.py:488
  57.2 7.4 %finish.1 = (f32[48,4,16,256]{3,2,1,0:T(8,128)}, f32[48,48]{1,0:T(8,128)}) custom-call(f32[48,128]{1,0:T(8,128)S(1)} %add.23.gx_ref, f32[2,3072,128]{2,1,0:T(8,128)S(1)} %get-tuple-element.40.s_ref), custom_call_target="tpu_custom_call" | custom-call | tf_op jit(solution)/shard_map/finish/pallas_call | solution.py:644
  (27 shorter events, 3.5 us)
Async XLA Ops:
  0.6 18.5 %copy-start.3 = (s32[8]{0:T(128)S(1)}, s32[8]{0:T(128)}, u32[]{:S(2)}) copy-start(s32[8]{0:T(128)} %ranks_ref.1) | copy-start | bytes 100
  0.6 18.4 %copy-start.1 = (f32[8,16,256]{2,1,0:T(8,128)S(1)}, f32[8,16,256]{2,1,0:T(8,128)}, u32[]{:S(2)}) copy-start(f32[8,16,256]{2,1,0:T(8,128)} %right_ref.1) | copy-start | bytes 393220
  0.7 18.4 %copy-start.2 = (f32[8,16,256]{2,1,0:T(8,128)S(1)}, f32[8,16,256]{2,1,0:T(8,128)}, u32[]{:S(2)}) copy-start(f32[8,16,256]{2,1,0:T(8,128)} %left_ref.1) | copy-start | bytes 393220
  4.9 3.2 %collective-permute-start = (bf16[112,128]{1,0:T(8,128)(2,1)S(1)}, bf16[112,128]{1,0:T(8,128)(2,1)S(1)}, u32[]{:S(2)}, u32[]{:S(2)}) collective-permute-start(bf16[112,128]{1,0:T(8,128)(2,1)S(1)} %get-tuple-element.23), channel_id=1, source_target_pairs={{0,1},{2,3},{1,0},{3,2},{4,5},{6,7},{5,4},{7,6},{8,9},{10,11},{9,8... | collective-permute-start | bytes 86024 | tf_op jit(solution)/shard_map/ppermute | solution.py:496
  5.4 4.2 %collective-permute-start.1 = (bf16[112,128]{1,0:T(8,128)(2,1)S(1)}, bf16[112,128]{1,0:T(8,128)(2,1)S(1)}, u32[]{:S(2)}, u32[]{:S(2)}) collective-permute-start(bf16[112,128]{1,0:T(8,128)(2,1)S(1)} %get-tuple-element.24), channel_id=1, source_target_pairs={{1,2},{0,3},{2,1},{3,0},{5,6},{4,7},{6,5},{7,4},{9,10},{8,11},{10,... | collective-permute-start | bytes 86024 | tf_op jit(solution)/shard_map/ppermute | solution.py:496
  9.7 21.0 %collective-permute-start.4 = (bf16[384,256]{1,0:T(8,128)(2,1)S(1)}, bf16[384,256]{1,0:T(8,128)(2,1)S(1)}, u32[]{:S(2)}, u32[]{:S(2)}) collective-permute-start(bf16[384,256]{1,0:T(8,128)(2,1)S(1)} %get-tuple-element.33), channel_id=1, source_target_pairs={{0,4},{8,12},{16,20},{24,28},{4,0},{12,8},{20,16},{28,24},{1,5},{9... | collective-permute-start | bytes 589832 | tf_op jit(solution)/shard_map/ppermute | solution.py:496
  11.4 19.3 %collective-permute-start.5 = (bf16[384,256]{1,0:T(8,128)(2,1)S(1)}, bf16[384,256]{1,0:T(8,128)(2,1)S(1)}, u32[]{:S(2)}, u32[]{:S(2)}) collective-permute-start(bf16[384,256]{1,0:T(8,128)(2,1)S(1)} %get-tuple-element.34), channel_id=1, source_target_pairs={{4,8},{12,16},{20,24},{8,4},{16,12},{24,20},{5,9},{13,17},{21,25},... | collective-permute-start | bytes 589832 | tf_op jit(solution)/shard_map/ppermute | solution.py:496
  12.3 10.2 %collective-permute-start.2 = (bf16[192,128]{1,0:T(8,128)(2,1)S(1)}, bf16[192,128]{1,0:T(8,128)(2,1)S(1)}, u32[]{:S(2)}, u32[]{:S(2)}) collective-permute-start(bf16[192,128]{1,0:T(8,128)(2,1)S(1)} %get-tuple-element.27), channel_id=1, source_target_pairs={{0,4},{8,12},{16,20},{24,28},{4,0},{12,8},{20,16},{28,24},{1,5},{9... | collective-permute-start | bytes 147464 | tf_op jit(solution)/shard_map/ppermute | solution.py:496
  16.6 6.8 %collective-permute-start.3 = (bf16[192,128]{1,0:T(8,128)(2,1)S(1)}, bf16[192,128]{1,0:T(8,128)(2,1)S(1)}, u32[]{:S(2)}, u32[]{:S(2)}) collective-permute-start(bf16[192,128]{1,0:T(8,128)(2,1)S(1)} %get-tuple-element.28), channel_id=1, source_target_pairs={{4,8},{12,16},{20,24},{0,28},{8,4},{16,12},{24,20},{28,0},{5,9},{1... | collective-permute-start | bytes 147464 | tf_op jit(solution)/shard_map/ppermute | solution.py:496
  30.8 1.7 %copy-start = (f32[256,256]{1,0:T(8,128)S(1)}, f32[256,256]{1,0:T(8,128)}, u32[]{:S(2)}) copy-start(f32[256,256]{1,0:T(8,128)} %block_ref.3) | copy-start | bytes 786436
  32.4 1.8 %collective-permute-start.6 = (bf16[2,2,192,128]{3,2,1,0:T(8,128)(2,1)S(1)}, bf16[2,2,192,128]{3,2,1,0:T(8,128)(2,1)S(1)}, u32[]{:S(2)}, u32[]{:S(2)}) collective-permute-start(bf16[2,2,192,128]{3,2,1,0:T(8,128)(2,1)S(1)} %get-tuple-element.39), channel_id=1, source_target_pairs={{0,1},{1,0},{2,3},{3,2},{4,5},{5,4},{6,7},{7,6},{8,9},{9,8},{10,11... | collective-permute-start | bytes 589832 | tf_op jit(solution)/shard_map/ppermute | solution.py:488
  34.2 5.3 %collective-permute-start.7 = (bf16[1,2,192,128]{3,2,1,0:T(8,128)(2,1)S(1)}, bf16[1,2,192,128]{3,2,1,0:T(8,128)(2,1)S(1)}, u32[]{:S(2)}, u32[]{:S(2)}) collective-permute-start(bf16[1,2,192,128]{3,2,1,0:T(8,128)(2,1)S(1)} %add_convert_fusion), channel_id=1, source_target_pairs={{0,2},{1,3},{2,0},{3,1},{4,6},{5,7},{6,4},{7,5},{8,10},{9,11},{10,... | collective-permute-start | bytes 294920 | tf_op jit(solution)/shard_map/ppermute | solution.py:488
  39.8 1.3 %collective-permute-start.8 = (f32[48,128]{1,0:T(8,128)S(1)}, f32[48,128]{1,0:T(8,128)S(1)}, u32[]{:S(2)}, u32[]{:S(2)}) collective-permute-start(f32[48,128]{1,0:T(8,128)S(1)} %couple.1), channel_id=1, source_target_pairs={{0,1},{1,0},{2,3},{3,2},{4,5},{5,4},{6,7},{7,6},{8,9},{9,8},{10,11... | collective-permute-start | bytes 73736 | tf_op jit(solution)/shard_map/ppermute | solution.py:488
  41.0 3.8 %collective-permute-start.9 = (f32[48,128]{1,0:T(8,128)S(1)}, f32[48,128]{1,0:T(8,128)S(1)}, u32[]{:S(2)}, u32[]{:S(2)}) collective-permute-start(f32[48,128]{1,0:T(8,128)S(1)} %add.19), channel_id=1, source_target_pairs={{0,2},{1,3},{2,0},{3,1},{4,6},{5,7},{6,4},{7,5},{8,10},{9,11},{10,... | collective-permute-start | bytes 73736 | tf_op jit(solution)/shard_map/ppermute | solution.py:488
  44.9 3.8 %collective-permute-start.10 = (f32[48,128]{1,0:T(8,128)S(1)}, f32[48,128]{1,0:T(8,128)S(1)}, u32[]{:S(2)}, u32[]{:S(2)}) collective-permute-start(f32[48,128]{1,0:T(8,128)S(1)} %add.20), channel_id=1, source_target_pairs={{0,4},{4,0},{8,12},{12,8},{16,20},{20,16},{24,28},{28,24},{1,5},{5... | collective-permute-start | bytes 73736 | tf_op jit(solution)/shard_map/ppermute | solution.py:488
  48.7 3.8 %collective-permute-start.11 = (f32[48,128]{1,0:T(8,128)S(1)}, f32[48,128]{1,0:T(8,128)S(1)}, u32[]{:S(2)}, u32[]{:S(2)}) collective-permute-start(f32[48,128]{1,0:T(8,128)S(1)} %add.21), channel_id=1, source_target_pairs={{0,8},{4,12},{8,0},{12,4},{16,24},{20,28},{24,16},{28,20},{1,9},{5... | collective-permute-start | bytes 73736 | tf_op jit(solution)/shard_map/ppermute | solution.py:488
  52.5 4.7 %collective-permute-start.12 = (f32[48,128]{1,0:T(8,128)S(1)}, f32[48,128]{1,0:T(8,128)S(1)}, u32[]{:S(2)}, u32[]{:S(2)}) collective-permute-start(f32[48,128]{1,0:T(8,128)S(1)} %add.22), channel_id=1, source_target_pairs={{0,16},{4,20},{8,24},{12,28},{16,0},{20,4},{24,8},{28,12},{1,17},{... | collective-permute-start | bytes 73736 | tf_op jit(solution)/shard_map/ppermute | solution.py:488

commit v3 on v2

--- a/solution.py
+++ b/solution.py
@@ -14,8 +14,8 @@
 GROUP = 32
 REACH = 3
 AXES = ("gy", "gx")
-UNROLL_ONE = 3
-UNROLL_TWO = 2
+UNROLL_ONE = 7
+UNROLL_TWO = 3
 UNROLL_GRAM = 8
 NLINES = 4
 GRAM_PARTS = 2
@@ -39,8 +39,8 @@
 
 def pack_kernel(K, NZ, X, p_hbm, cls_hbm, w_hbm, pt_ref, cg_ref, wg_ref, own_ref, y0_ref, y1_ref, p_ref, cls_ref, w_ref, edge, yaux, sem):
     rows, ext = NZ * X, X + 4
-    parts = 4
-    step = K * rows // parts
+    parts = K // SUB
+    step = SUB * rows
     loads = [pltpu.make_async_copy(cls_hbm, cls_ref, sem.at[parts]), pltpu.make_async_copy(w_hbm, w_ref, sem.at[parts + 1])]
     for i in range(parts):
         loads.append(pltpu.make_async_copy(p_hbm.at[pl.ds(i * step, step)], p_ref.at[pl.ds(i * step, step)], sem.at[i]))
@@ -69,15 +69,14 @@
         w_hi, w_lo = halves(turned[1][at[0] : at[0] + 1, :])
         yaux[side, 3:4, :] = w_hi.astype(F32)
         yaux[side, 4:5, :] = w_lo.astype(F32)
-    for i in range(parts):
-        loads[2 + i].wait()
-        for k in range(i * K // parts, (i + 1) * K // parts):
+    lane = lanes_of((SUB, LANES))
+    for kt in range(parts):
+        loads[2 + kt].wait()
+        for k in range(kt * SUB, (kt + 1) * SUB):
             v = p_ref[k * rows : (k + 1) * rows, :].astype(F32)
             for z in range(NZ):
                 for h in range(2):
                     pt_ref[h, pl.ds((z * ext + 2) * K + k, X, stride=K), :] = v[z * X : (z + 1) * X, h * LANES : (h + 1) * LANES]
-    lane = lanes_of((SUB, LANES))
-    for kt in range(K // SUB):
         out = [jnp.zeros((SUB, LANES), F32) for _ in range(4)]
         for z in range(NZ):
             for x in range(X):
@@ -150,7 +149,7 @@
     return v if isinstance(v, int) else pl.multiple_of(v, SUB)
 
 
-def stencil(NZ, z, coef_row, cf, first_cf, src, centre_row, x_step, z_step, halo, kt):
+def stencil(NZ, z, coef_row, coefs, src, centre_row, x_step, z_step, halo, kt):
     lane = lanes_of((SUB, LANES))
     is_first, is_last = lane == 0, lane == LANES - 1
 
@@ -169,7 +168,7 @@
     prv = [jnp.where(is_first, hl, bwd[0]), jnp.where(is_first, bwd[0], bwd[1])]
     out = []
     for h in range(2):
-        co = [cf[first_cf + j, h, pl.ds(coef_row, 1), :] for j in range(7)]
+        co = coefs[h]
         acc = co[0] * c[h] + co[1] * up[h] + co[2] * down[h] + co[3] * nxt[h] + co[4] * prv[h]
         if z < NZ - 1:
             acc = acc + co[5] * src[h, at(row + z_step), :]
@@ -179,11 +178,16 @@
     return out
 
 
+def line_coefs(cf, first, row):
+    return [[jnp.broadcast_to(cf[first + j, h, pl.ds(row, 1), :], (SUB, LANES)) for j in range(7)] for h in range(2)]
+
+
 def stage_one(K, NZ, X, x, cf, pt_ref, t_ref, hp):
     ext, wide = X + 4, X + 2
     for z in range(NZ):
+        coefs = line_coefs(cf, 0, z * GROUP + x + REACH)
         for kt in range(K // SUB):
-            out = stencil(NZ, z, z * GROUP + x + REACH, cf, 0, pt_ref, (z * ext + x + 2) * K, K, ext * K, hp, kt)
+            out = stencil(NZ, z, z * GROUP + x + REACH, coefs, pt_ref, (z * ext + x + 2) * K, K, ext * K, hp, kt)
             to = mult((z * wide + x + 1) * K + kt * SUB)
             for h in range(2):
                 t_ref[h, pl.ds(to, SUB), :] = out[h]
@@ -194,8 +198,9 @@
     his = []
     for z in range(NZ):
         lines = []
+        coefs = line_coefs(cf, 7, z * GROUP + x + REACH)
         for kt in range(K // SUB):
-            out = stencil(NZ, z, z * GROUP + x + REACH, cf, 7, t_ref, (z * wide + x + 1) * K, K, wide * K, ht, kt)
+            out = stencil(NZ, z, z * GROUP + x + REACH, coefs, t_ref, (z * wide + x + 1) * K, K, wide * K, ht, kt)
             row = mult((z * ext + x + 2) * K + kt * SUB)
             to = mult((z * X + x) * K + kt * SUB)
             both = []
@@ -437,6 +442,37 @@
     out_ref[:, at : at + K] = out_ref[:, at : at + K] + total
 
 
+def eliminated(K, aug):
+    tile = (SUB, LANES)
+    tiles = [aug[i : i + SUB] for i in range(0, K, SUB)]
+    sub = lax.broadcasted_iota(jnp.int32, tile, 0)
+    for first in range(K // SUB):
+        rest = range(first, K // SUB)
+        j = first * SUB
+        columns = [[jnp.broadcast_to(tiles[i][:, j + q : j + q + 1], tile) for i in rest] for q in range(SUB)]
+        rows = [jnp.broadcast_to(tiles[first][q : q + 1, :], tile) for q in range(SUB)]
+        block = [[jnp.broadcast_to(columns[t][0][q : q + 1, :], tile) for t in range(SUB)] for q in range(SUB)]
+        for q in range(SUB):
+            inverse = 1.0 / block[q][q]
+            multiples = [c * inverse for c in columns[q]]
+            for t in range(q + 1, SUB):
+                factor = block[q][t] * inverse
+                for u in range(t, SUB):
+                    block[t][u] = block[t][u] - factor * block[q][u]
+                rows[t] = rows[t] - factor * rows[q]
+                columns[t] = [c - m * block[q][t] for c, m in zip(columns[t], multiples)]
+            columns[q] = multiples
+        for n, i in enumerate(rest):
+            for q in range(SUB):
+                m = columns[q][n]
+                if n == 0:
+                    if q == SUB - 1:
+                        continue
+                    m = jnp.where(sub > q, m, 0.0)
+                tiles[i] = tiles[i] - m * rows[q]
+    return jnp.concatenate(tiles, 0)
+
+
 def finish_kernel(K, NZ, X, cells, gx_ref, s_ref, basis_ref, proj_ref, out, sem):
     lane = lanes_of((K, LANES))
     row = lax.broadcasted_iota(jnp.int32, (K, LANES), 0)
@@ -445,10 +481,7 @@
     gram = gx[:, :K]
     mixed = gram + gx[:, half : half + K]
     aug = jnp.where(lane < K, gx, jnp.where(lane - half == row, 1.0, 0.0))
-    for j in range(K - 1):
-        pivot_row = aug[j : j + 1, :]
-        factor = aug[:, j : j + 1] * (1.0 / aug[j : j + 1, j : j + 1])
-        aug = aug - jnp.where(row > j, factor, 0.0) * pivot_row
+    aug = eliminated(K, aug)
     pivots = jnp.sum(jnp.where(lane == row, aug, 0.0), axis=1, keepdims=True)
     inverse = aug[:, half : half + K] * lax.rsqrt(pivots)
     left = jnp.dot(inverse, mixed, precision=HIGH, preferred_element_type=F32)
@@ -541,7 +574,7 @@
             pltpu.VMEM((rows, W), F32),
             pltpu.VMEM((4, K, LANES), F32),
             pltpu.VMEM((2, AUX, LANES), F32),
-            pltpu.SemaphoreType.DMA((6,)),
+            pltpu.SemaphoreType.DMA((K // SUB + 2,)),
         ],
         compiler_params=params(),
         name="pack",

time: 65 us -> 61.3 us (0.943)
  Pallas kernels: 25.8 us -> 22.1 us
    pallas_call x1, Pallas kernels: 7.42 us -> 4.87 us  [shards(): pl.pallas_call(functools.partial(finish_kernel, K, NZ, X, cells), out_sha...]
    pallas_call x1, Pallas kernels: 4.2 us -> 3.52 us  [shards(): pl.pallas_call(functools.partial(pack_kernel, K, NZ, X), out_shape=(shape...]
where the time goes in v3:
time: 61.3 us; the launch traced here: 61.1 us
  Pallas kernels  22.1 us (36%)
  starting transfers between devices  21.7 us (35%)
  waiting for transfers between devices  16.3 us (27%)
  between operations  0.95 us (2%)
    ppermute x6, starting transfers between devices, paired(): return lax.ppermute(v, axis, swaps + [(j, i) for i, j in swaps])  12.5 us
    ppermute x7, waiting for transfers between devices, exchanged(): lax.ppermute(v, axis, [(i, i ^ bits) for i in range(lax.axis_size(axis))])  11 us
    ppermute x7, starting transfers between devices, exchanged(): lax.ppermute(v, axis, [(i, i ^ bits) for i in range(lax.axis_size(axis))])  9.17 us
    pallas_call x1, Pallas kernels, shards(): pl.pallas_call(functools.partial(inner_kernel, K, NZ, X, R), out_shape=(s...  6.83 us
    ppermute x6, waiting for transfers between devices, paired(): return lax.ppermute(v, axis, swaps + [(j, i) for i, j in swaps])  5.25 us
    pallas_call x1, Pallas kernels, shards(): pl.pallas_call(functools.partial(finish_kernel, K, NZ, X, cells), out_sha...  4.87 us
    pallas_call x1, Pallas kernels, shards(): pl.pallas_call(functools.partial(pack_kernel, K, NZ, X), out_shape=(shape...  3.52 us
    pallas_call x2, Pallas kernels, gram_part(): pl.pallas_call(functools.partial(gram_kernel, K, i * share, share), out_s...  3.41 us
  transfers between devices with their start and end apart: 13, of which 9 were waited for; matrix products, arithmetic and copies ran while one was open for 0% of the time, Pallas kernels for 19%

profile of v3, /device:TPU:0, one launch (start us, length us, event | category | flops | bytes accessed | tf_op | source)
XLA Modules:
  0.0 61.1 jit_solution(2728577955316392439)
XLA Ops:
  0.7 3.5 %pack.1 = (f32[2,3840,128]{2,1,0:T(8,128)S(1)}, f32[2,128,128]{2,1,0:T(8,128)S(1)}, f32[2,128,128]{2,1,0:T(8,128)S(1)}, f32[2,48,128]{2,1,0:T(8,128)S(1)}, bf16[...) custom-call(bf16[3072,256]{1,0:T(8,128)(2,1)} %bitcast.7, s32[64,256]{1,0:T(8,128)} %bitcast.8, f32[64,256]{1,0:T(8,128)} %bitcast.9), custom_call_target="tpu_custom_call" | custom-call | tf_op jit(solution)/shard_map/pack/pallas_call | solution.py:559
  4.8 2.6 %collective-permute-start.1 = (bf16[112,128]{1,0:T(8,128)(2,1)S(1)}, bf16[112,128]{1,0:T(8,128)(2,1)S(1)}, u32[]{:S(2)}, u32[]{:S(2)}) collective-permute-start(bf16[112,128]{1,0:T(8,128)(2,1)S(1)} %get-tuple-element.24), channel_id=1, source_target_pairs={{1,2},{0,3},{2,1},{3,0},{5,6},{4,7},{6,5},{7,4},{9,10},{8,11},{10,... | collective-permute-start | bytes 86024 | tf_op jit(solution)/shard_map/ppermute | solution.py:529
  7.4 1.6 %collective-permute-done.1.y1_ref = bf16[112,128]{1,0:T(8,128)(2,1)S(1)} collective-permute-done((bf16[112,128]{1,0:T(8,128)(2,1)S(1)}, bf16[112,128]{1,0:T(8,128)(2,1)S(1)}, u32[]{:S(2)}, u32[]{:S(2)}) %collective-permute-start.1) | collective-permute-done | bytes 28704 | tf_op jit(solution)/shard_map/ppermute | solution.py:529
  9.1 1.7 %collective-permute-start.4 = (bf16[384,256]{1,0:T(8,128)(2,1)S(1)}, bf16[384,256]{1,0:T(8,128)(2,1)S(1)}, u32[]{:S(2)}, u32[]{:S(2)}) collective-permute-start(bf16[384,256]{1,0:T(8,128)(2,1)S(1)} %get-tuple-element.33), channel_id=1, source_target_pairs={{0,4},{8,12},{16,20},{24,28},{4,0},{12,8},{20,16},{28,24},{1,5},{9... | collective-permute-start | bytes 589832 | tf_op jit(solution)/shard_map/ppermute | solution.py:529
  11.6 4.3 %collective-permute-start.2 = (bf16[192,128]{1,0:T(8,128)(2,1)S(1)}, bf16[192,128]{1,0:T(8,128)(2,1)S(1)}, u32[]{:S(2)}, u32[]{:S(2)}) collective-permute-start(bf16[192,128]{1,0:T(8,128)(2,1)S(1)} %get-tuple-element.27), channel_id=1, source_target_pairs={{0,4},{8,12},{16,20},{24,28},{4,0},{12,8},{20,16},{28,24},{1,5},{9... | collective-permute-start | bytes 147464 | tf_op jit(solution)/shard_map/ppermute | solution.py:529
  16.0 2.4 %collective-permute-start.3 = (bf16[192,128]{1,0:T(8,128)(2,1)S(1)}, bf16[192,128]{1,0:T(8,128)(2,1)S(1)}, u32[]{:S(2)}, u32[]{:S(2)}) collective-permute-start(bf16[192,128]{1,0:T(8,128)(2,1)S(1)} %get-tuple-element.28), channel_id=1, source_target_pairs={{4,8},{12,16},{20,24},{0,28},{8,4},{16,12},{24,20},{28,0},{5,9},{1... | collective-permute-start | bytes 147464 | tf_op jit(solution)/shard_map/ppermute | solution.py:529
  19.1 2.7 %collective-permute-done.2.q0_ref = bf16[192,128]{1,0:T(8,128)(2,1)S(1)} collective-permute-done((bf16[192,128]{1,0:T(8,128)(2,1)S(1)}, bf16[192,128]{1,0:T(8,128)(2,1)S(1)}, u32[]{:S(2)}, u32[]{:S(2)}) %collective-permute-start.2) | collective-permute-done | bytes 49184 | tf_op jit(solution)/shard_map/ppermute | solution.py:529
  21.8 0.9 %collective-permute-done.3.q1_ref = bf16[192,128]{1,0:T(8,128)(2,1)S(1)} collective-permute-done((bf16[192,128]{1,0:T(8,128)(2,1)S(1)}, bf16[192,128]{1,0:T(8,128)(2,1)S(1)}, u32[]{:S(2)}, u32[]{:S(2)}) %collective-permute-start.3) | collective-permute-done | bytes 49184 | tf_op jit(solution)/shard_map/ppermute | solution.py:529
  22.7 6.8 %inner.1 = (f32[2,3072,128]{2,1,0:T(8,128)S(1)}, f32[2,3456,128]{2,1,0:T(8,128)S(1)}, f32[14,2,128,128]{3,2,1,0:T(8,128)S(1)}, f32[2,48,128]{2,1,0:T(8,128)S(1)}...) custom-call(f32[8]{0:T(128)} %table_hbm.1, f32[2,3840,128]{2,1,0:T(8,128)S(1)} %get-tuple-element.22.pt_ref.pt_in, ...), custom_call_target="tpu_custom_call" | custom-call | flops 1073741824 | bytes 20971520 | tf_op jit(solution)/shard_map/inner/pallas_call | solution.py:610
  29.6 1.6 %edge.1 = (f32[2,3840,128]{2,1,0:T(8,128)S(1)}, f32[2,3456,128]{2,1,0:T(8,128)S(1)}, f32[2,3072,128]{2,1,0:T(8,128)S(1)}, bf16[2,2,192,128]{3,2,1,0:T(8,128)(2,1)S(1)}) custom-call(f32[2,3840,128]{2,1,0:T(8,128)S(1)} %get-tuple-element.22.pt_ref.pt_in, ...), custom_call_target="tpu_custom_call", output_to_operand_aliasing={{0}: (0, {}), {1}: (1, {}), {2}: (2, {})} | custom-call | tf_op jit(solution)/shard_map/edge/pallas_call | solution.py:627
  31.3 1.7 %shard_map.95.refs_0_ = f32[48,128]{1,0:T(8,128)S(1)} custom-call(f32[2,3072,128]{2,1,0:T(8,128)S(1)} %get-tuple-element.40.s_ref, f32[256,256]{1,0:T(8,128)S(1)} %copy-done), custom_call_target="tpu_custom_call" | custom-call | flops 235929600 | bytes 8388608 | tf_op jit(solution)/shard_map/pallas_call | solution.py:640
  33.0 1.6 %collective-permute-start.7 = (bf16[1,2,192,128]{3,2,1,0:T(8,128)(2,1)S(1)}, bf16[1,2,192,128]{3,2,1,0:T(8,128)(2,1)S(1)}, u32[]{:S(2)}, u32[]{:S(2)}) collective-permute-start(bf16[1,2,192,128]{3,2,1,0:T(8,128)(2,1)S(1)} %add_convert_fusion), channel_id=1, source_target_pairs={{0,2},{1,3},{2,0},{3,1},{4,6},{5,7},{6,4},{7,5},{8,10},{9,11},{10,... | collective-permute-start | bytes 294920 | tf_op jit(solution)/shard_map/ppermute | solution.py:521
  34.6 1.7 %shard_map.96.refs_1_ = f32[48,128]{1,0:T(8,128)S(1)} custom-call(f32[2,3072,128]{2,1,0:T(8,128)S(1)} %get-tuple-element.40.s_ref, f32[256,256]{1,0:T(8,128)S(1)} %copy-done, bf16[2,2,192,128]{3,2,1,0:T(8,128)(2,1)S(1)} %collective-permute-done.6.after_ref.refs_0_), custom_call_target="tpu_custom_call" | custom-call | flops 235929600 | bytes 8388608 | tf_op jit(solution)/shard_map/pallas_call | solution.py:640
  37.2 1.1 %collective-permute-done.7 = bf16[1,2,192,128]{3,2,1,0:T(8,128)(2,1)S(1)} collective-permute-done((bf16[1,2,192,128]{3,2,1,0:T(8,128)(2,1)S(1)}, bf16[1,2,192,128]{3,2,1,0:T(8,128)(2,1)S(1)}, u32[]{:S(2)}, u32[]{:S(2)}) %collective-permute-start.7) | collective-permute-done | bytes 98336 | tf_op jit(solution)/shard_map/ppermute | solution.py:521
  38.7 1.2 %collective-permute-done.8 = f32[48,128]{1,0:T(8,128)S(1)} collective-permute-done((f32[48,128]{1,0:T(8,128)S(1)}, f32[48,128]{1,0:T(8,128)S(1)}, u32[]{:S(2)}, u32[]{:S(2)}) %collective-permute-start.8) | collective-permute-done | bytes 24608 | tf_op jit(solution)/shard_map/ppermute | solution.py:521
  39.9 1.5 %collective-permute-start.9 = (f32[48,128]{1,0:T(8,128)S(1)}, f32[48,128]{1,0:T(8,128)S(1)}, u32[]{:S(2)}, u32[]{:S(2)}) collective-permute-start(f32[48,128]{1,0:T(8,128)S(1)} %add.19), channel_id=1, source_target_pairs={{0,2},{1,3},{2,0},{3,1},{4,6},{5,7},{6,4},{7,5},{8,10},{9,11},{10,... | collective-permute-start | bytes 73736 | tf_op jit(solution)/shard_map/ppermute | solution.py:521
  41.4 2.3 %collective-permute-done.9 = f32[48,128]{1,0:T(8,128)S(1)} collective-permute-done((f32[48,128]{1,0:T(8,128)S(1)}, f32[48,128]{1,0:T(8,128)S(1)}, u32[]{:S(2)}, u32[]{:S(2)}) %collective-permute-start.9) | collective-permute-done | bytes 24608 | tf_op jit(solution)/shard_map/ppermute | solution.py:521
  43.7 1.6 %collective-permute-start.10 = (f32[48,128]{1,0:T(8,128)S(1)}, f32[48,128]{1,0:T(8,128)S(1)}, u32[]{:S(2)}, u32[]{:S(2)}) collective-permute-start(f32[48,128]{1,0:T(8,128)S(1)} %add.20), channel_id=1, source_target_pairs={{0,4},{4,0},{8,12},{12,8},{16,20},{20,16},{24,28},{28,24},{1,5},{5... | collective-permute-start | bytes 73736 | tf_op jit(solution)/shard_map/ppermute | solution.py:521
  45.3 2.2 %collective-permute-done.10 = f32[48,128]{1,0:T(8,128)S(1)} collective-permute-done((f32[48,128]{1,0:T(8,128)S(1)}, f32[48,128]{1,0:T(8,128)S(1)}, u32[]{:S(2)}, u32[]{:S(2)}) %collective-permute-start.10) | collective-permute-done | bytes 24608 | tf_op jit(solution)/shard_map/ppermute | solution.py:521
  47.5 1.7 %collective-permute-start.11 = (f32[48,128]{1,0:T(8,128)S(1)}, f32[48,128]{1,0:T(8,128)S(1)}, u32[]{:S(2)}, u32[]{:S(2)}) collective-permute-start(f32[48,128]{1,0:T(8,128)S(1)} %add.21), channel_id=1, source_target_pairs={{0,8},{4,12},{8,0},{12,4},{16,24},{20,28},{24,16},{28,20},{1,9},{5... | collective-permute-start | bytes 73736 | tf_op jit(solution)/shard_map/ppermute | solution.py:521
  49.2 2.2 %collective-permute-done.11 = f32[48,128]{1,0:T(8,128)S(1)} collective-permute-done((f32[48,128]{1,0:T(8,128)S(1)}, f32[48,128]{1,0:T(8,128)S(1)}, u32[]{:S(2)}, u32[]{:S(2)}) %collective-permute-start.11) | collective-permute-done | bytes 24608 | tf_op jit(solution)/shard_map/ppermute | solution.py:521
  51.4 2.7 %collective-permute-start.12 = (f32[48,128]{1,0:T(8,128)S(1)}, f32[48,128]{1,0:T(8,128)S(1)}, u32[]{:S(2)}, u32[]{:S(2)}) collective-permute-start(f32[48,128]{1,0:T(8,128)S(1)} %add.22), channel_id=1, source_target_pairs={{0,16},{4,20},{8,24},{12,28},{16,0},{20,4},{24,8},{28,12},{1,17},{... | collective-permute-start | bytes 73736 | tf_op jit(solution)/shard_map/ppermute | solution.py:521
  54.0 2.0 %collective-permute-done.12 = f32[48,128]{1,0:T(8,128)S(1)} collective-permute-done((f32[48,128]{1,0:T(8,128)S(1)}, f32[48,128]{1,0:T(8,128)S(1)}, u32[]{:S(2)}, u32[]{:S(2)}) %collective-permute-start.12) | collective-permute-done | bytes 24608 | tf_op jit(solution)/shard_map/ppermute | solution.py:521
  56.1 4.9 %finish.1 = (f32[48,4,16,256]{3,2,1,0:T(8,128)}, f32[48,48]{1,0:T(8,128)}) custom-call(f32[48,128]{1,0:T(8,128)S(1)} %add.23.gx_ref, f32[2,3072,128]{2,1,0:T(8,128)S(1)} %get-tuple-element.40.s_ref), custom_call_target="tpu_custom_call" | custom-call | tf_op jit(solution)/shard_map/finish/pallas_call | solution.py:677
  (27 shorter events, 3.5 us)
Async XLA Ops:
  0.6 17.8 %copy-start.3 = (s32[8]{0:T(128)S(1)}, s32[8]{0:T(128)}, u32[]{:S(2)}) copy-start(s32[8]{0:T(128)} %ranks_ref.1) | copy-start | bytes 100
  0.6 17.8 %copy-start.1 = (f32[8,16,256]{2,1,0:T(8,128)S(1)}, f32[8,16,256]{2,1,0:T(8,128)}, u32[]{:S(2)}) copy-start(f32[8,16,256]{2,1,0:T(8,128)} %right_ref.1) | copy-start | bytes 393220
  0.7 17.8 %copy-start.2 = (f32[8,16,256]{2,1,0:T(8,128)S(1)}, f32[8,16,256]{2,1,0:T(8,128)}, u32[]{:S(2)}) copy-start(f32[8,16,256]{2,1,0:T(8,128)} %left_ref.1) | copy-start | bytes 393220
  4.2 3.2 %collective-permute-start = (bf16[112,128]{1,0:T(8,128)(2,1)S(1)}, bf16[112,128]{1,0:T(8,128)(2,1)S(1)}, u32[]{:S(2)}, u32[]{:S(2)}) collective-permute-start(bf16[112,128]{1,0:T(8,128)(2,1)S(1)} %get-tuple-element.23), channel_id=1, source_target_pairs={{0,1},{2,3},{1,0},{3,2},{4,5},{6,7},{5,4},{7,6},{8,9},{10,11},{9,8... | collective-permute-start | bytes 86024 | tf_op jit(solution)/shard_map/ppermute | solution.py:529
  4.8 4.2 %collective-permute-start.1 = (bf16[112,128]{1,0:T(8,128)(2,1)S(1)}, bf16[112,128]{1,0:T(8,128)(2,1)S(1)}, u32[]{:S(2)}, u32[]{:S(2)}) collective-permute-start(bf16[112,128]{1,0:T(8,128)(2,1)S(1)} %get-tuple-element.24), channel_id=1, source_target_pairs={{1,2},{0,3},{2,1},{3,0},{5,6},{4,7},{6,5},{7,4},{9,10},{8,11},{10,... | collective-permute-start | bytes 86024 | tf_op jit(solution)/shard_map/ppermute | solution.py:529
  9.1 20.5 %collective-permute-start.4 = (bf16[384,256]{1,0:T(8,128)(2,1)S(1)}, bf16[384,256]{1,0:T(8,128)(2,1)S(1)}, u32[]{:S(2)}, u32[]{:S(2)}) collective-permute-start(bf16[384,256]{1,0:T(8,128)(2,1)S(1)} %get-tuple-element.33), channel_id=1, source_target_pairs={{0,4},{8,12},{16,20},{24,28},{4,0},{12,8},{20,16},{28,24},{1,5},{9... | collective-permute-start | bytes 589832 | tf_op jit(solution)/shard_map/ppermute | solution.py:529
  10.8 18.8 %collective-permute-start.5 = (bf16[384,256]{1,0:T(8,128)(2,1)S(1)}, bf16[384,256]{1,0:T(8,128)(2,1)S(1)}, u32[]{:S(2)}, u32[]{:S(2)}) collective-permute-start(bf16[384,256]{1,0:T(8,128)(2,1)S(1)} %get-tuple-element.34), channel_id=1, source_target_pairs={{4,8},{12,16},{20,24},{8,4},{16,12},{24,20},{5,9},{13,17},{21,25},... | collective-permute-start | bytes 589832 | tf_op jit(solution)/shard_map/ppermute | solution.py:529
  11.6 10.2 %collective-permute-start.2 = (bf16[192,128]{1,0:T(8,128)(2,1)S(1)}, bf16[192,128]{1,0:T(8,128)(2,1)S(1)}, u32[]{:S(2)}, u32[]{:S(2)}) collective-permute-start(bf16[192,128]{1,0:T(8,128)(2,1)S(1)} %get-tuple-element.27), channel_id=1, source_target_pairs={{0,4},{8,12},{16,20},{24,28},{4,0},{12,8},{20,16},{28,24},{1,5},{9... | collective-permute-start | bytes 147464 | tf_op jit(solution)/shard_map/ppermute | solution.py:529
  16.0 6.8 %collective-permute-start.3 = (bf16[192,128]{1,0:T(8,128)(2,1)S(1)}, bf16[192,128]{1,0:T(8,128)(2,1)S(1)}, u32[]{:S(2)}, u32[]{:S(2)}) collective-permute-start(bf16[192,128]{1,0:T(8,128)(2,1)S(1)} %get-tuple-element.28), channel_id=1, source_target_pairs={{4,8},{12,16},{20,24},{0,28},{8,4},{16,12},{24,20},{28,0},{5,9},{1... | collective-permute-start | bytes 147464 | tf_op jit(solution)/shard_map/ppermute | solution.py:529
  29.6 1.7 %copy-start = (f32[256,256]{1,0:T(8,128)S(1)}, f32[256,256]{1,0:T(8,128)}, u32[]{:S(2)}) copy-start(f32[256,256]{1,0:T(8,128)} %block_ref.3) | copy-start | bytes 786436
  31.2 1.8 %collective-permute-start.6 = (bf16[2,2,192,128]{3,2,1,0:T(8,128)(2,1)S(1)}, bf16[2,2,192,128]{3,2,1,0:T(8,128)(2,1)S(1)}, u32[]{:S(2)}, u32[]{:S(2)}) collective-permute-start(bf16[2,2,192,128]{3,2,1,0:T(8,128)(2,1)S(1)} %get-tuple-element.39), channel_id=1, source_target_pairs={{0,1},{1,0},{2,3},{3,2},{4,5},{5,4},{6,7},{7,6},{8,9},{9,8},{10,11... | collective-permute-start | bytes 589832 | tf_op jit(solution)/shard_map/ppermute | solution.py:521
  33.0 5.3 %collective-permute-start.7 = (bf16[1,2,192,128]{3,2,1,0:T(8,128)(2,1)S(1)}, bf16[1,2,192,128]{3,2,1,0:T(8,128)(2,1)S(1)}, u32[]{:S(2)}, u32[]{:S(2)}) collective-permute-start(bf16[1,2,192,128]{3,2,1,0:T(8,128)(2,1)S(1)} %add_convert_fusion), channel_id=1, source_target_pairs={{0,2},{1,3},{2,0},{3,1},{4,6},{5,7},{6,4},{7,5},{8,10},{9,11},{10,... | collective-permute-start | bytes 294920 | tf_op jit(solution)/shard_map/ppermute | solution.py:521
  38.6 1.3 %collective-permute-start.8 = (f32[48,128]{1,0:T(8,128)S(1)}, f32[48,128]{1,0:T(8,128)S(1)}, u32[]{:S(2)}, u32[]{:S(2)}) collective-permute-start(f32[48,128]{1,0:T(8,128)S(1)} %couple.1), channel_id=1, source_target_pairs={{0,1},{1,0},{2,3},{3,2},{4,5},{5,4},{6,7},{7,6},{8,9},{9,8},{10,11... | collective-permute-start | bytes 73736 | tf_op jit(solution)/shard_map/ppermute | solution.py:521
  39.9 3.8 %collective-permute-start.9 = (f32[48,128]{1,0:T(8,128)S(1)}, f32[48,128]{1,0:T(8,128)S(1)}, u32[]{:S(2)}, u32[]{:S(2)}) collective-permute-start(f32[48,128]{1,0:T(8,128)S(1)} %add.19), channel_id=1, source_target_pairs={{0,2},{1,3},{2,0},{3,1},{4,6},{5,7},{6,4},{7,5},{8,10},{9,11},{10,... | collective-permute-start | bytes 73736 | tf_op jit(solution)/shard_map/ppermute | solution.py:521
  43.7 3.8 %collective-permute-start.10 = (f32[48,128]{1,0:T(8,128)S(1)}, f32[48,128]{1,0:T(8,128)S(1)}, u32[]{:S(2)}, u32[]{:S(2)}) collective-permute-start(f32[48,128]{1,0:T(8,128)S(1)} %add.20), channel_id=1, source_target_pairs={{0,4},{4,0},{8,12},{12,8},{16,20},{20,16},{24,28},{28,24},{1,5},{5... | collective-permute-start | bytes 73736 | tf_op jit(solution)/shard_map/ppermute | solution.py:521
  47.5 3.8 %collective-permute-start.11 = (f32[48,128]{1,0:T(8,128)S(1)}, f32[48,128]{1,0:T(8,128)S(1)}, u32[]{:S(2)}, u32[]{:S(2)}) collective-permute-start(f32[48,128]{1,0:T(8,128)S(1)} %add.21), channel_id=1, source_target_pairs={{0,8},{4,12},{8,0},{12,4},{16,24},{20,28},{24,16},{28,20},{1,9},{5... | collective-permute-start | bytes 73736 | tf_op jit(solution)/shard_map/ppermute | solution.py:521
  51.4 4.7 %collective-permute-start.12 = (f32[48,128]{1,0:T(8,128)S(1)}, f32[48,128]{1,0:T(8,128)S(1)}, u32[]{:S(2)}, u32[]{:S(2)}) collective-permute-start(f32[48,128]{1,0:T(8,128)S(1)} %add.22), channel_id=1, source_target_pairs={{0,16},{4,20},{8,24},{12,28},{16,0},{20,4},{24,8},{28,12},{1,17},{... | collective-permute-start | bytes 73736 | tf_op jit(solution)/shard_map/ppermute | solution.py:521

commit v4 on v3

--- a/solution.py
+++ b/solution.py
@@ -13,8 +13,7 @@
 SUB = 8
 GROUP = 32
 REACH = 3
-AXES = ("gy", "gx")
-UNROLL_ONE = 7
+UNROLL_ONE = 14
 UNROLL_TWO = 3
 UNROLL_GRAM = 8
 NLINES = 4
@@ -530,11 +529,12 @@
 
 
 def summed(v):
-    for axis in AXES:
-        bit = 1
-        while bit < lax.axis_size(axis):
-            v = v + exchanged(v, axis, bit)
-            bit *= 2
+    n, m = lax.axis_size("gx"), lax.axis_size("gy")
+    v = v + exchanged(v, "gy", 1)
+    steps = [(0, 2**i) for i in range(1, m.bit_length() - 1)] + [(2**i, 0) for i in range(n.bit_length() - 1)]
+    for dx, dy in steps:
+        swaps = [(i * m + j, (i ^ dx) * m + (j ^ dy ^ 1)) for i in range(n) for j in range(m)]
+        v = v + lax.ppermute(v, ("gx", "gy"), swaps)
     return v
 
 
@@ -650,7 +650,7 @@
     sibs = []
     pending = v
     for l in range(levels):
-        got = exchanged(pending, "gy", 2**l)
+        got = exchanged(pending, "gy", 2**l + (l > 0))
         if l == 0:
             first_got = got
         sibs.append(got[0])

time: 61.3 us -> 58.3 us (0.951)
  waiting for transfers between devices: 16.3 us -> 12.7 us
    ppermute x7 -> x3, waiting for transfers between devices: 11 us -> 1.1 us  [exchanged(): lax.ppermute(v, axis, [(i, i ^ bits) for i in range(lax.axis_size(axis))])]
    ppermute x0 -> x4, starting transfers between devices: none -> 7.72 us  [summed(): v = v + lax.ppermute(v, ('gx', 'gy'), swaps)]
    ppermute x7 -> x3, starting transfers between devices: 9.17 us -> 2.29 us  [exchanged(): lax.ppermute(v, axis, [(i, i ^ bits) for i in range(lax.axis_size(axis))])]
    ppermute x0 -> x4, waiting for transfers between devices: none -> 6.37 us  [summed(): v = v + lax.ppermute(v, ('gx', 'gy'), swaps)]
  transfers between devices with their start and end apart: 13 -> 13, of which waited for: 9 -> 9; matrix products, arithmetic and copies ran while one was open for 0% -> 0% of each run, Pallas kernels for 19% -> 20%
where the time goes in v4:
time: 58.3 us; the launch traced here: 58.2 us
  starting transfers between devices  22.3 us (38%)
  Pallas kernels  22.1 us (38%)
  waiting for transfers between devices  12.7 us (22%)
  between operations  0.95 us (2%)
    ppermute x6, starting transfers between devices, paired(): return lax.ppermute(v, axis, swaps + [(j, i) for i, j in swaps])  12.3 us
    ppermute x4, starting transfers between devices, summed(): v = v + lax.ppermute(v, ('gx', 'gy'), swaps)  7.72 us
    pallas_call x1, Pallas kernels, shards(): pl.pallas_call(functools.partial(inner_kernel, K, NZ, X, R), out_shape=(s...  6.8 us
    ppermute x4, waiting for transfers between devices, summed(): v = v + lax.ppermute(v, ('gx', 'gy'), swaps)  6.37 us
    ppermute x6, waiting for transfers between devices, paired(): return lax.ppermute(v, axis, swaps + [(j, i) for i, j in swaps])  5.25 us
    pallas_call x1, Pallas kernels, shards(): pl.pallas_call(functools.partial(finish_kernel, K, NZ, X, cells), out_sha...  4.88 us
    pallas_call x1, Pallas kernels, shards(): pl.pallas_call(functools.partial(pack_kernel, K, NZ, X), out_shape=(shape...  3.52 us
    pallas_call x2, Pallas kernels, gram_part(): pl.pallas_call(functools.partial(gram_kernel, K, i * share, share), out_s...  3.41 us
  transfers between devices with their start and end apart: 13, of which 9 were waited for; matrix products, arithmetic and copies ran while one was open for 0% of the time, Pallas kernels for 20%

profile of v4, /device:TPU:0, one launch (start us, length us, event | category | flops | bytes accessed | tf_op | source)
XLA Modules:
  0.0 58.2 jit_solution(5372813473636829675)
XLA Ops:
  0.7 3.5 %pack.1 = (f32[2,3840,128]{2,1,0:T(8,128)S(1)}, f32[2,128,128]{2,1,0:T(8,128)S(1)}, f32[2,128,128]{2,1,0:T(8,128)S(1)}, f32[2,48,128]{2,1,0:T(8,128)S(1)}, bf16[...) custom-call(bf16[3072,256]{1,0:T(8,128)(2,1)} %bitcast.7, s32[64,256]{1,0:T(8,128)} %bitcast.8, f32[64,256]{1,0:T(8,128)} %bitcast.9), custom_call_target="tpu_custom_call" | custom-call | tf_op jit(solution)/shard_map/pack/pallas_call | solution.py:559
  4.8 2.6 %collective-permute-start.1 = (bf16[112,128]{1,0:T(8,128)(2,1)S(1)}, bf16[112,128]{1,0:T(8,128)(2,1)S(1)}, u32[]{:S(2)}, u32[]{:S(2)}) collective-permute-start(bf16[112,128]{1,0:T(8,128)(2,1)S(1)} %get-tuple-element.24), channel_id=1, source_target_pairs={{1,2},{0,3},{2,1},{3,0},{5,6},{4,7},{6,5},{7,4},{9,10},{8,11},{10,... | collective-permute-start | bytes 86024 | tf_op jit(solution)/shard_map/ppermute | solution.py:528
  7.4 1.6 %collective-permute-done.1.y1_ref = bf16[112,128]{1,0:T(8,128)(2,1)S(1)} collective-permute-done((bf16[112,128]{1,0:T(8,128)(2,1)S(1)}, bf16[112,128]{1,0:T(8,128)(2,1)S(1)}, u32[]{:S(2)}, u32[]{:S(2)}) %collective-permute-start.1) | collective-permute-done | bytes 28704 | tf_op jit(solution)/shard_map/ppermute | solution.py:528
  9.1 1.7 %collective-permute-start.4 = (bf16[384,256]{1,0:T(8,128)(2,1)S(1)}, bf16[384,256]{1,0:T(8,128)(2,1)S(1)}, u32[]{:S(2)}, u32[]{:S(2)}) collective-permute-start(bf16[384,256]{1,0:T(8,128)(2,1)S(1)} %get-tuple-element.33), channel_id=1, source_target_pairs={{0,4},{8,12},{16,20},{24,28},{4,0},{12,8},{20,16},{28,24},{1,5},{9... | collective-permute-start | bytes 589832 | tf_op jit(solution)/shard_map/ppermute | solution.py:528
  11.4 4.3 %collective-permute-start.2 = (bf16[192,128]{1,0:T(8,128)(2,1)S(1)}, bf16[192,128]{1,0:T(8,128)(2,1)S(1)}, u32[]{:S(2)}, u32[]{:S(2)}) collective-permute-start(bf16[192,128]{1,0:T(8,128)(2,1)S(1)} %get-tuple-element.27), channel_id=1, source_target_pairs={{0,4},{8,12},{16,20},{24,28},{4,0},{12,8},{20,16},{28,24},{1,5},{9... | collective-permute-start | bytes 147464 | tf_op jit(solution)/shard_map/ppermute | solution.py:528
  15.8 2.4 %collective-permute-start.3 = (bf16[192,128]{1,0:T(8,128)(2,1)S(1)}, bf16[192,128]{1,0:T(8,128)(2,1)S(1)}, u32[]{:S(2)}, u32[]{:S(2)}) collective-permute-start(bf16[192,128]{1,0:T(8,128)(2,1)S(1)} %get-tuple-element.28), channel_id=1, source_target_pairs={{4,8},{12,16},{20,24},{0,28},{8,4},{16,12},{24,20},{28,0},{5,9},{1... | collective-permute-start | bytes 147464 | tf_op jit(solution)/shard_map/ppermute | solution.py:528
  18.9 2.9 %collective-permute-done.2.q0_ref = bf16[192,128]{1,0:T(8,128)(2,1)S(1)} collective-permute-done((bf16[192,128]{1,0:T(8,128)(2,1)S(1)}, bf16[192,128]{1,0:T(8,128)(2,1)S(1)}, u32[]{:S(2)}, u32[]{:S(2)}) %collective-permute-start.2) | collective-permute-done | bytes 49184 | tf_op jit(solution)/shard_map/ppermute | solution.py:528
  21.8 0.7 %collective-permute-done.3.q1_ref = bf16[192,128]{1,0:T(8,128)(2,1)S(1)} collective-permute-done((bf16[192,128]{1,0:T(8,128)(2,1)S(1)}, bf16[192,128]{1,0:T(8,128)(2,1)S(1)}, u32[]{:S(2)}, u32[]{:S(2)}) %collective-permute-start.3) | collective-permute-done | bytes 49184 | tf_op jit(solution)/shard_map/ppermute | solution.py:528
  22.6 6.8 %inner.1 = (f32[2,3072,128]{2,1,0:T(8,128)S(1)}, f32[2,3456,128]{2,1,0:T(8,128)S(1)}, f32[14,2,128,128]{3,2,1,0:T(8,128)S(1)}, f32[2,48,128]{2,1,0:T(8,128)S(1)}...) custom-call(f32[8]{0:T(128)} %table_hbm.1, f32[2,3840,128]{2,1,0:T(8,128)S(1)} %get-tuple-element.22.pt_ref.pt_in, ...), custom_call_target="tpu_custom_call" | custom-call | flops 1073741824 | bytes 20971520 | tf_op jit(solution)/shard_map/inner/pallas_call | solution.py:610
  29.4 1.6 %edge.1 = (f32[2,3840,128]{2,1,0:T(8,128)S(1)}, f32[2,3456,128]{2,1,0:T(8,128)S(1)}, f32[2,3072,128]{2,1,0:T(8,128)S(1)}, bf16[2,2,192,128]{3,2,1,0:T(8,128)(2,1)S(1)}) custom-call(f32[2,3840,128]{2,1,0:T(8,128)S(1)} %get-tuple-element.22.pt_ref.pt_in, ...), custom_call_target="tpu_custom_call", output_to_operand_aliasing={{0}: (0, {}), {1}: (1, {}), {2}: (2, {})} | custom-call | tf_op jit(solution)/shard_map/edge/pallas_call | solution.py:627
  31.1 1.7 %shard_map.95.refs_0_ = f32[48,128]{1,0:T(8,128)S(1)} custom-call(f32[2,3072,128]{2,1,0:T(8,128)S(1)} %get-tuple-element.40.s_ref, f32[256,256]{1,0:T(8,128)S(1)} %copy-done), custom_call_target="tpu_custom_call" | custom-call | flops 235929600 | bytes 8388608 | tf_op jit(solution)/shard_map/pallas_call | solution.py:640
  32.8 1.7 %collective-permute-start.7 = (bf16[1,2,192,128]{3,2,1,0:T(8,128)(2,1)S(1)}, bf16[1,2,192,128]{3,2,1,0:T(8,128)(2,1)S(1)}, u32[]{:S(2)}, u32[]{:S(2)}) collective-permute-start(bf16[1,2,192,128]{3,2,1,0:T(8,128)(2,1)S(1)} %add_convert_fusion), channel_id=1, source_target_pairs={{0,3},{1,2},{2,1},{3,0},{4,7},{5,6},{6,5},{7,4},{8,11},{9,10},{10,... | collective-permute-start | bytes 294920 | tf_op jit(solution)/shard_map/ppermute | solution.py:520
  34.5 1.7 %shard_map.96.refs_1_ = f32[48,128]{1,0:T(8,128)S(1)} custom-call(f32[2,3072,128]{2,1,0:T(8,128)S(1)} %get-tuple-element.40.s_ref, f32[256,256]{1,0:T(8,128)S(1)} %copy-done, bf16[2,2,192,128]{3,2,1,0:T(8,128)(2,1)S(1)} %collective-permute-done.6.after_ref.refs_0_), custom_call_target="tpu_custom_call" | custom-call | flops 235929600 | bytes 8388608 | tf_op jit(solution)/shard_map/pallas_call | solution.py:640
  36.2 0.8 %left.1.u_ref = bf16[2,2,192,128]{3,2,1,0:T(8,128)(2,1)S(1)} custom-call(bf16[2,2,192,128]{3,2,1,0:T(8,128)(2,1)S(1)} %collective-permute-done.6.after_ref.refs_0_, f32[2,3072,128]{2,1,0:T(8,128)S(1)} %get-tuple-element.40.s_ref, bf16[8,256,256]{2,1,0:T(8,128)(2,1)S(1)} %get-tuple-element.41.fl_ref), custom_call_target="tpu_custom_call" | custom-call | flops 268435456 | bytes 8388608 | tf_op jit(solution)/shard_map/left/pallas_call | solution.py:659
  38.2 0.8 %collective-permute-done.8 = f32[48,128]{1,0:T(8,128)S(1)} collective-permute-done((f32[48,128]{1,0:T(8,128)S(1)}, f32[48,128]{1,0:T(8,128)S(1)}, u32[]{:S(2)}, u32[]{:S(2)}) %collective-permute-start.8) | collective-permute-done | bytes 24608 | tf_op jit(solution)/shard_map/ppermute | solution.py:520
  39.0 1.5 %collective-permute-start.9 = (f32[48,128]{1,0:T(8,128)S(1)}, f32[48,128]{1,0:T(8,128)S(1)}, u32[]{:S(2)}, u32[]{:S(2)}) collective-permute-start(f32[48,128]{1,0:T(8,128)S(1)} %add.19), channel_id=1, source_target_pairs={{0,3},{1,2},{2,1},{3,0},{4,7},{5,6},{6,5},{7,4},{8,11},{9,10},{10,... | collective-permute-start | bytes 73736 | tf_op jit(solution)/shard_map/ppermute | solution.py:537
  40.5 1.8 %collective-permute-done.9 = f32[48,128]{1,0:T(8,128)S(1)} collective-permute-done((f32[48,128]{1,0:T(8,128)S(1)}, f32[48,128]{1,0:T(8,128)S(1)}, u32[]{:S(2)}, u32[]{:S(2)}) %collective-permute-start.9) | collective-permute-done | bytes 24608 | tf_op jit(solution)/shard_map/ppermute | solution.py:537
  42.3 1.7 %collective-permute-start.10 = (f32[48,128]{1,0:T(8,128)S(1)}, f32[48,128]{1,0:T(8,128)S(1)}, u32[]{:S(2)}, u32[]{:S(2)}) collective-permute-start(f32[48,128]{1,0:T(8,128)S(1)} %add.20), channel_id=1, source_target_pairs={{0,5},{1,4},{2,7},{3,6},{4,1},{5,0},{6,3},{7,2},{8,13},{9,12},{10,... | collective-permute-start | bytes 73736 | tf_op jit(solution)/shard_map/ppermute | solution.py:537
  44.0 1.5 %collective-permute-done.10 = f32[48,128]{1,0:T(8,128)S(1)} collective-permute-done((f32[48,128]{1,0:T(8,128)S(1)}, f32[48,128]{1,0:T(8,128)S(1)}, u32[]{:S(2)}, u32[]{:S(2)}) %collective-permute-start.10) | collective-permute-done | bytes 24608 | tf_op jit(solution)/shard_map/ppermute | solution.py:537
  45.6 1.8 %collective-permute-start.11 = (f32[48,128]{1,0:T(8,128)S(1)}, f32[48,128]{1,0:T(8,128)S(1)}, u32[]{:S(2)}, u32[]{:S(2)}) collective-permute-start(f32[48,128]{1,0:T(8,128)S(1)} %add.21), channel_id=1, source_target_pairs={{0,9},{1,8},{2,11},{3,10},{4,13},{5,12},{6,15},{7,14},{8,1},{9,0},... | collective-permute-start | bytes 73736 | tf_op jit(solution)/shard_map/ppermute | solution.py:537
  47.4 1.5 %collective-permute-done.11 = f32[48,128]{1,0:T(8,128)S(1)} collective-permute-done((f32[48,128]{1,0:T(8,128)S(1)}, f32[48,128]{1,0:T(8,128)S(1)}, u32[]{:S(2)}, u32[]{:S(2)}) %collective-permute-start.11) | collective-permute-done | bytes 24608 | tf_op jit(solution)/shard_map/ppermute | solution.py:537
  48.9 2.7 %collective-permute-start.12 = (f32[48,128]{1,0:T(8,128)S(1)}, f32[48,128]{1,0:T(8,128)S(1)}, u32[]{:S(2)}, u32[]{:S(2)}) collective-permute-start(f32[48,128]{1,0:T(8,128)S(1)} %add.22), channel_id=1, source_target_pairs={{0,17},{1,16},{2,19},{3,18},{4,21},{5,20},{6,23},{7,22},{8,25},{9,... | collective-permute-start | bytes 73736 | tf_op jit(solution)/shard_map/ppermute | solution.py:537
  51.6 1.5 %collective-permute-done.12 = f32[48,128]{1,0:T(8,128)S(1)} collective-permute-done((f32[48,128]{1,0:T(8,128)S(1)}, f32[48,128]{1,0:T(8,128)S(1)}, u32[]{:S(2)}, u32[]{:S(2)}) %collective-permute-start.12) | collective-permute-done | bytes 24608 | tf_op jit(solution)/shard_map/ppermute | solution.py:537
  53.1 4.9 %finish.1 = (f32[48,4,16,256]{3,2,1,0:T(8,128)}, f32[48,48]{1,0:T(8,128)}) custom-call(f32[48,128]{1,0:T(8,128)S(1)} %add.23.gx_ref, f32[2,3072,128]{2,1,0:T(8,128)S(1)} %get-tuple-element.40.s_ref), custom_call_target="tpu_custom_call" | custom-call | tf_op jit(solution)/shard_map/finish/pallas_call | solution.py:677
  (27 shorter events, 3.2 us)
Async XLA Ops:
  0.6 17.6 %copy-start.3 = (s32[8]{0:T(128)S(1)}, s32[8]{0:T(128)}, u32[]{:S(2)}) copy-start(s32[8]{0:T(128)} %ranks_ref.1) | copy-start | bytes 100
  0.6 17.6 %copy-start.1 = (f32[8,16,256]{2,1,0:T(8,128)S(1)}, f32[8,16,256]{2,1,0:T(8,128)}, u32[]{:S(2)}) copy-start(f32[8,16,256]{2,1,0:T(8,128)} %right_ref.1) | copy-start | bytes 393220
  0.7 17.6 %copy-start.2 = (f32[8,16,256]{2,1,0:T(8,128)S(1)}, f32[8,16,256]{2,1,0:T(8,128)}, u32[]{:S(2)}) copy-start(f32[8,16,256]{2,1,0:T(8,128)} %left_ref.1) | copy-start | bytes 393220
  4.2 3.2 %collective-permute-start = (bf16[112,128]{1,0:T(8,128)(2,1)S(1)}, bf16[112,128]{1,0:T(8,128)(2,1)S(1)}, u32[]{:S(2)}, u32[]{:S(2)}) collective-permute-start(bf16[112,128]{1,0:T(8,128)(2,1)S(1)} %get-tuple-element.23), channel_id=1, source_target_pairs={{0,1},{2,3},{1,0},{3,2},{4,5},{6,7},{5,4},{7,6},{8,9},{10,11},{9,8... | collective-permute-start | bytes 86024 | tf_op jit(solution)/shard_map/ppermute | solution.py:528
  4.8 4.2 %collective-permute-start.1 = (bf16[112,128]{1,0:T(8,128)(2,1)S(1)}, bf16[112,128]{1,0:T(8,128)(2,1)S(1)}, u32[]{:S(2)}, u32[]{:S(2)}) collective-permute-start(bf16[112,128]{1,0:T(8,128)(2,1)S(1)} %get-tuple-element.24), channel_id=1, source_target_pairs={{1,2},{0,3},{2,1},{3,0},{5,6},{4,7},{6,5},{7,4},{9,10},{8,11},{10,... | collective-permute-start | bytes 86024 | tf_op jit(solution)/shard_map/ppermute | solution.py:528
  9.1 20.3 %collective-permute-start.4 = (bf16[384,256]{1,0:T(8,128)(2,1)S(1)}, bf16[384,256]{1,0:T(8,128)(2,1)S(1)}, u32[]{:S(2)}, u32[]{:S(2)}) collective-permute-start(bf16[384,256]{1,0:T(8,128)(2,1)S(1)} %get-tuple-element.33), channel_id=1, source_target_pairs={{0,4},{8,12},{16,20},{24,28},{4,0},{12,8},{20,16},{28,24},{1,5},{9... | collective-permute-start | bytes 589832 | tf_op jit(solution)/shard_map/ppermute | solution.py:528
  10.8 18.6 %collective-permute-start.5 = (bf16[384,256]{1,0:T(8,128)(2,1)S(1)}, bf16[384,256]{1,0:T(8,128)(2,1)S(1)}, u32[]{:S(2)}, u32[]{:S(2)}) collective-permute-start(bf16[384,256]{1,0:T(8,128)(2,1)S(1)} %get-tuple-element.34), channel_id=1, source_target_pairs={{4,8},{12,16},{20,24},{8,4},{16,12},{24,20},{5,9},{13,17},{21,25},... | collective-permute-start | bytes 589832 | tf_op jit(solution)/shard_map/ppermute | solution.py:528
  11.4 10.4 %collective-permute-start.2 = (bf16[192,128]{1,0:T(8,128)(2,1)S(1)}, bf16[192,128]{1,0:T(8,128)(2,1)S(1)}, u32[]{:S(2)}, u32[]{:S(2)}) collective-permute-start(bf16[192,128]{1,0:T(8,128)(2,1)S(1)} %get-tuple-element.27), channel_id=1, source_target_pairs={{0,4},{8,12},{16,20},{24,28},{4,0},{12,8},{20,16},{28,24},{1,5},{9... | collective-permute-start | bytes 147464 | tf_op jit(solution)/shard_map/ppermute | solution.py:528
  15.8 6.8 %collective-permute-start.3 = (bf16[192,128]{1,0:T(8,128)(2,1)S(1)}, bf16[192,128]{1,0:T(8,128)(2,1)S(1)}, u32[]{:S(2)}, u32[]{:S(2)}) collective-permute-start(bf16[192,128]{1,0:T(8,128)(2,1)S(1)} %get-tuple-element.28), channel_id=1, source_target_pairs={{4,8},{12,16},{20,24},{0,28},{8,4},{16,12},{24,20},{28,0},{5,9},{1... | collective-permute-start | bytes 147464 | tf_op jit(solution)/shard_map/ppermute | solution.py:528
  29.4 1.7 %copy-start = (f32[256,256]{1,0:T(8,128)S(1)}, f32[256,256]{1,0:T(8,128)}, u32[]{:S(2)}) copy-start(f32[256,256]{1,0:T(8,128)} %block_ref.3) | copy-start | bytes 786436
  31.0 1.8 %collective-permute-start.6 = (bf16[2,2,192,128]{3,2,1,0:T(8,128)(2,1)S(1)}, bf16[2,2,192,128]{3,2,1,0:T(8,128)(2,1)S(1)}, u32[]{:S(2)}, u32[]{:S(2)}) collective-permute-start(bf16[2,2,192,128]{3,2,1,0:T(8,128)(2,1)S(1)} %get-tuple-element.39), channel_id=1, source_target_pairs={{0,1},{1,0},{2,3},{3,2},{4,5},{5,4},{6,7},{7,6},{8,9},{9,8},{10,11... | collective-permute-start | bytes 589832 | tf_op jit(solution)/shard_map/ppermute | solution.py:520
  32.8 4.5 %collective-permute-start.7 = (bf16[1,2,192,128]{3,2,1,0:T(8,128)(2,1)S(1)}, bf16[1,2,192,128]{3,2,1,0:T(8,128)(2,1)S(1)}, u32[]{:S(2)}, u32[]{:S(2)}) collective-permute-start(bf16[1,2,192,128]{3,2,1,0:T(8,128)(2,1)S(1)} %add_convert_fusion), channel_id=1, source_target_pairs={{0,3},{1,2},{2,1},{3,0},{4,7},{5,6},{6,5},{7,4},{8,11},{9,10},{10,... | collective-permute-start | bytes 294920 | tf_op jit(solution)/shard_map/ppermute | solution.py:520
  37.6 1.4 %collective-permute-start.8 = (f32[48,128]{1,0:T(8,128)S(1)}, f32[48,128]{1,0:T(8,128)S(1)}, u32[]{:S(2)}, u32[]{:S(2)}) collective-permute-start(f32[48,128]{1,0:T(8,128)S(1)} %couple.1), channel_id=1, source_target_pairs={{0,1},{1,0},{2,3},{3,2},{4,5},{5,4},{6,7},{7,6},{8,9},{9,8},{10,11... | collective-permute-start | bytes 73736 | tf_op jit(solution)/shard_map/ppermute | solution.py:520
  39.0 3.3 %collective-permute-start.9 = (f32[48,128]{1,0:T(8,128)S(1)}, f32[48,128]{1,0:T(8,128)S(1)}, u32[]{:S(2)}, u32[]{:S(2)}) collective-permute-start(f32[48,128]{1,0:T(8,128)S(1)} %add.19), channel_id=1, source_target_pairs={{0,3},{1,2},{2,1},{3,0},{4,7},{5,6},{6,5},{7,4},{8,11},{9,10},{10,... | collective-permute-start | bytes 73736 | tf_op jit(solution)/shard_map/ppermute | solution.py:537
  42.3 3.3 %collective-permute-start.10 = (f32[48,128]{1,0:T(8,128)S(1)}, f32[48,128]{1,0:T(8,128)S(1)}, u32[]{:S(2)}, u32[]{:S(2)}) collective-permute-start(f32[48,128]{1,0:T(8,128)S(1)} %add.20), channel_id=1, source_target_pairs={{0,5},{1,4},{2,7},{3,6},{4,1},{5,0},{6,3},{7,2},{8,13},{9,12},{10,... | collective-permute-start | bytes 73736 | tf_op jit(solution)/shard_map/ppermute | solution.py:537
  45.6 3.3 %collective-permute-start.11 = (f32[48,128]{1,0:T(8,128)S(1)}, f32[48,128]{1,0:T(8,128)S(1)}, u32[]{:S(2)}, u32[]{:S(2)}) collective-permute-start(f32[48,128]{1,0:T(8,128)S(1)} %add.21), channel_id=1, source_target_pairs={{0,9},{1,8},{2,11},{3,10},{4,13},{5,12},{6,15},{7,14},{8,1},{9,0},... | collective-permute-start | bytes 73736 | tf_op jit(solution)/shard_map/ppermute | solution.py:537
  48.9 4.3 %collective-permute-start.12 = (f32[48,128]{1,0:T(8,128)S(1)}, f32[48,128]{1,0:T(8,128)S(1)}, u32[]{:S(2)}, u32[]{:S(2)}) collective-permute-start(f32[48,128]{1,0:T(8,128)S(1)} %add.22), channel_id=1, source_target_pairs={{0,17},{1,16},{2,19},{3,18},{4,21},{5,20},{6,23},{7,22},{8,25},{9,... | collective-permute-start | bytes 73736 | tf_op jit(solution)/shard_map/ppermute | solution.py:537
